TPU v7x, 256 devices: a whole 4x4x8 slice. The times are simulated.
256 devices in a mesh: ctx: 64 (over z, y, core), head: 4 (over x).
Axes of the slice: x: 4, y: 4, z: 8, core: 2. Of those that a mesh axis runs over, the one named last changes fastest.
Arguments:
- query: bfloat16 [32768, 8192], P('ctx', 'head'), may hold values from -6 to 6
- key: bfloat16 [32768, 1024], P('ctx', 'head'), may hold values from -6 to 6
- value: bfloat16 [32768, 1024], P('ctx', 'head'), may hold values from -6 to 6
- attn_out: bfloat16 [32768, 8192], P('ctx', 'head'), may hold values from -6 to 6
- grad_out: bfloat16 [32768, 8192], P('ctx', 'head'), may hold values from -48 to 48
- log_norm: float32 [64, 32768], P('head', 'ctx')
- doc_bounds: int32 [40], replicated, may hold values from 0 to 32768, as said below
- local_pairs: int32 [2816, 2], P('ctx'), may hold values from -1 to 15, as said below
- ship_table: int32 [64, 2, 9], replicated, may hold values from -1 to 15, as said below
Outputs:
- grad_query: bfloat16 [32768, 8192], P('ctx', 'head')
- grad_key: bfloat16 [32768, 1024], P('ctx', 'head')
- grad_value: bfloat16 [32768, 1024], P('ctx', 'head')
Inputs may be any that keep to these rules, and one draw needn't show every extreme that they name: `doc_bounds`: entry 0 is 0, entry 39 is 32768, entries rise strictly. No document is longer than 1280 tokens, and one is exactly that long. `local_pairs`: rows (q, w) of ctx index c: q is one of its 4 query blocks, w a block of its key window of 16 blocks, which begins 3 * 4 blocks before its first block. Live rows come first; the others are -1 in both columns. Together with ship_table every block pair whose blocks hold a query token and a key token of one document, the key not after the query, is named exactly once, and no other pair is named. `ship_table`: row (c, r): column 0 is a query block of ctx index c; the other 8 columns are blocks of c's key window, live first (at least one), -1 after. The pairs of a row are computed by the index of ctx that differs from c in bit number log2(64) - 1 - r.
All inputs are finite; a program needn't handle non-finite values.
Results may differ from a plain program's by a relative error of at most 0.006.
Values may be sent and summed in bfloat16 or wider, within the bound.
A program may use at most 192 MiB of HBM per device.

v0:
```python
import jax
import jax.numpy as jnp
from jax import lax
from jax.sharding import PartitionSpec as P

HEAD_DIM = 128
BLOCK = 128
SHIP_SLOTS = 8
ROUNDS = 2
REACH = 3
WIN_BLOCKS = 16


GROUP_PAIRS = 4


def shifted(shard, axis, by):
    length = lax.axis_size(axis)
    pairs = [(i, i + by) for i in range(length) if 0 <= i + by < length]
    return lax.ppermute(shard, axis, pairs)


def swapped(shard, axis, apart):
    return lax.ppermute(shard, axis, [(i, i ^ 1 << apart) for i in range(lax.axis_size(axis))])


def doc_index(positions, doc_bounds):
    flat = positions.reshape(-1)
    edges = doc_bounds[1:]
    counts = jnp.sum((edges[None, :] <= flat[:, None]).astype(jnp.int32), axis=1)
    return counts.reshape(positions.shape)


def pad_front(rows_in, total_rows):
    missing = total_rows - rows_in.shape[0]
    return rows_in


def run_pairs(pair_rows, live_count, sources, query_starts, key_starts, doc_bounds, totals):
    queries, outgrads, norm_blocks, delta_blocks, keyval_blocks = sources
    features = queries.shape[2]
    kv_features = keyval_blocks.shape[2] // 2
    kv_heads = kv_features // HEAD_DIM
    heads = norm_blocks.shape[1]
    group = heads // kv_heads
    scale = HEAD_DIM ** (-0.5)
    offsets = jnp.arange(BLOCK, dtype=jnp.int32)

    def one_turn(turn, state):
        query_grads, keyval_grads = state
        rows = lax.dynamic_slice_in_dim(pair_rows, turn * GROUP_PAIRS, GROUP_PAIRS, 0)
        live = rows[:, 0] >= 0
        query_index = jnp.maximum(rows[:, 0], 0)
        key_index = jnp.maximum(rows[:, 1], 0)
        query_pos = query_starts[query_index][:, None] + offsets[None, :]
        key_pos = key_starts[key_index][:, None] + offsets[None, :]
        same_doc = (
            doc_index(query_pos, doc_bounds)[:, :, None]
            == doc_index(key_pos, doc_bounds)[:, None, :]
        )
        allowed = same_doc & (key_pos[:, None, :] <= query_pos[:, :, None]) & live[:, None, None]
        query_rows = queries[query_index].reshape(GROUP_PAIRS, BLOCK, kv_heads, group, HEAD_DIM)
        outgrad_rows = outgrads[query_index].reshape(GROUP_PAIRS, BLOCK, kv_heads, group, HEAD_DIM)
        both_rows = keyval_blocks[key_index]
        key_rows = both_rows[:, :, :kv_features].reshape(GROUP_PAIRS, BLOCK, kv_heads, HEAD_DIM)
        value_rows = both_rows[:, :, kv_features:].reshape(GROUP_PAIRS, BLOCK, kv_heads, HEAD_DIM)
        norms = norm_blocks[query_index].reshape(GROUP_PAIRS, kv_heads, group, BLOCK)
        dots = delta_blocks[query_index].reshape(GROUP_PAIRS, kv_heads, group, BLOCK)
        scores = (
            jnp.einsum(
                "pqhgd,pkhd->phgqk", query_rows, key_rows, preferred_element_type=jnp.float32
            )
            * scale
        )
        weights = jnp.where(allowed[:, None, None], jnp.exp(scores - norms[..., None]), 0.0)
        weight_grads = jnp.einsum(
            "pqhgd,pkhd->phgqk", outgrad_rows, value_rows, preferred_element_type=jnp.float32
        )
        score_grads = (weights * (weight_grads - dots[..., None])).astype(jnp.bfloat16)
        weights_low = weights.astype(jnp.bfloat16)
        part_query = (
            jnp.einsum(
                "phgqk,pkhd->pqhgd", score_grads, key_rows, preferred_element_type=jnp.float32
            )
            * scale
        )
        part_key = (
            jnp.einsum(
                "phgqk,pqhgd->pkhd", score_grads, query_rows, preferred_element_type=jnp.float32
            )
            * scale
        )
        part_value = jnp.einsum(
            "phgqk,pqhgd->pkhd", weights_low, outgrad_rows, preferred_element_type=jnp.float32
        )
        query_grads = query_grads.at[query_index].add(
            part_query.reshape(GROUP_PAIRS, BLOCK, features)
        )
        part_both = jnp.concatenate(
            [
                part_key.reshape(GROUP_PAIRS, BLOCK, kv_features),
                part_value.reshape(GROUP_PAIRS, BLOCK, kv_features),
            ],
            axis=2,
        )
        keyval_grads = keyval_grads.at[key_index].add(part_both)
        return (query_grads, keyval_grads)

    turns = (live_count + GROUP_PAIRS - 1) // GROUP_PAIRS
    return lax.fori_loop(0, turns, one_turn, totals)


def help_partner(far_row, far_rows, far_keys, partner, own_blocks, received, doc_bounds):
    got_query, got_grad, got_norms, got_delta, got_keyval = received
    far_query_start = ((partner * own_blocks + jnp.maximum(far_row[0], 0)) * BLOCK)[None]
    sources = (got_query[None], got_grad[None], got_norms[None], got_delta[None], got_keyval)
    totals = (
        jnp.zeros((1,) + got_query.shape, jnp.float32),
        jnp.zeros(got_keyval.shape, jnp.float32),
    )
    count = jnp.sum((far_row[1:] >= 0).astype(jnp.int32))
    return run_pairs(far_rows, count, sources, far_query_start, far_keys, doc_bounds, totals)


def local(query, key, value, attn_out, grad_out, log_norm, doc_bounds, local_pairs, ship_table):
    position = lax.axis_index("ctx")
    tokens, features = query.shape
    kv_features = key.shape[1]
    heads = log_norm.shape[0]
    own_blocks = tokens // BLOCK
    delta = jnp.einsum(
        "thd,thd->ht",
        grad_out.reshape(tokens, heads, HEAD_DIM),
        attn_out.reshape(tokens, heads, HEAD_DIM),
        preferred_element_type=jnp.float32,
    )
    queries = query.reshape(own_blocks, BLOCK, features)
    outgrads = grad_out.reshape(own_blocks, BLOCK, features)
    norm_blocks = log_norm.reshape(heads, own_blocks, BLOCK).transpose(1, 0, 2)
    delta_blocks = delta.reshape(heads, own_blocks, BLOCK).transpose(1, 0, 2)
    own_keyval = jnp.concatenate([key, value], axis=1)
    pieces = []
    for hop in range(REACH, 0, -1):
        outgoing = own_keyval
        pieces.append(pad_front(shifted(outgoing, "ctx", hop), tokens))
    keyval_window = jnp.concatenate(pieces + [own_keyval], axis=0).reshape(
        WIN_BLOCKS, BLOCK, 2 * kv_features
    )
    first_block = position * own_blocks
    query_starts = (first_block + jnp.arange(own_blocks, dtype=jnp.int32)) * BLOCK
    window_first = first_block - REACH * own_blocks
    key_starts = (window_first + jnp.arange(WIN_BLOCKS, dtype=jnp.int32)) * BLOCK
    sources = (queries, outgrads, norm_blocks, delta_blocks, keyval_window)
    totals = (
        jnp.zeros((own_blocks, BLOCK, features), jnp.float32),
        jnp.zeros((WIN_BLOCKS, BLOCK, 2 * kv_features), jnp.float32),
    )
    local_count = jnp.sum((local_pairs[:, 0] >= 0).astype(jnp.int32))
    totals = run_pairs(
        local_pairs, local_count, sources, query_starts, key_starts, doc_bounds, totals
    )
    head_bits = lax.axis_size("head").bit_length() - 1
    all_bits = lax.axis_size(("ctx", "head")).bit_length() - 1
    for section in range(ROUNDS):
        my_row = ship_table[position, section]
        bit = all_bits - 1 - section
        partner = jnp.bitwise_xor(position, 1 << bit - head_bits)
        far_row = ship_table[partner, section]
        sent = jnp.maximum(my_row[0], 0)
        my_slots = jnp.maximum(my_row[1:], 0)
        got_norms, got_delta = swapped(
            (norm_blocks[sent], delta_blocks[sent]), ("ctx", "head"), bit
        )
        got_query, got_grad, got_keyval = swapped(
            (queries[sent], outgrads[sent], keyval_window[my_slots]), ("ctx", "head"), bit
        )
        far_live = far_row[1:] >= 0
        slot_range = jnp.arange(SHIP_SLOTS, dtype=jnp.int32)
        far_pairs = jnp.stack(
            [jnp.where(far_live, 0, -1), jnp.where(far_live, slot_range, -1)], axis=1
        )
        far_first = (partner - REACH) * own_blocks
        far_keys = (far_first + jnp.maximum(far_row[1:], 0)) * BLOCK
        back_query, back_keyval = help_partner(
            far_row,
            far_pairs,
            far_keys,
            partner,
            own_blocks,
            (got_query, got_grad, got_norms, got_delta, got_keyval),
            doc_bounds,
        )
        returned = swapped((back_query, back_keyval), ("ctx", "head"), bit)
        totals = (totals[0].at[sent].add(returned[0][0]), totals[1].at[my_slots].add(returned[1]))
    segments = totals[1].reshape(REACH + 1, own_blocks * BLOCK, 2 * kv_features)
    own_grads = segments[REACH]
    for hop in range(1, REACH + 1):
        outgoing = segments[REACH - hop]
        own_grads = own_grads + pad_front(shifted(outgoing, "ctx", -hop), tokens)
    grad_query = totals[0].reshape(tokens, features).astype(jnp.bfloat16)
    grad_key = own_grads[:, :kv_features].astype(jnp.bfloat16)
    grad_value = own_grads[:, kv_features:].astype(jnp.bfloat16)
    return (grad_query, grad_key, grad_value)


def solution(mesh):
    in_specs = (
        P("ctx", "head"),
        P("ctx", "head"),
        P("ctx", "head"),
        P("ctx", "head"),
        P("ctx", "head"),
        P("head", "ctx"),
        P(),
        P("ctx", None),
        P(),
    )
    out_specs = (P("ctx", "head"), P("ctx", "head"), P("ctx", "head"))
    return jax.shard_map(local, mesh=mesh, in_specs=in_specs, out_specs=out_specs, check_vma=False)
```

profile of v0, /device:TPU:23, one launch (start us, length us, event | category | flops | bytes accessed | tf_op | source)
XLA Modules:
  0.0 900.2 jit_solution(39356328843095453)
XLA Ops:
  21.9 5.1 collective-permute-done.1
  33.8 12.5 %collective-permute-start.3 = (bf16[8,128,512]{2,1,0:T(8,128)(2,1)}, bf16[8,128,512]{2,1,0:T(8,128)(2,1)}, u32[]{:S(2)}, u32[]{:S(2)}) collective-permute-start(bf16[8,128,512]{2,1,0:T(8,128)(2,1)} %gather_fusion.11), channel_id=1, source_target_pairs={{0,128},{1,129},{2,130},{3,131},{4,132},{5,133},{6,134},{7,135},{8... | collective-permute-start | bytes 3145736 | tf_op jit(solution)/shard_map/ppermute | solution.py:24
  46.5 5.4 collective-permute-start.7
  56.3 5.3 collective-permute-start.6
  75.1 41.7 %collective-permute-start.11 = (f32[16,128]{1,0:T(8,128)S(1)}, f32[16,128]{1,0:T(8,128)S(1)}, u32[]{:S(2)}, u32[]{:S(2)}) collective-permute-start(f32[16,128]{1,0:T(8,128)S(1)} %bitcast.558), channel_id=1, source_target_pairs={{0,64},{1,65},{2,66},{3,67},{4,68},{5,69},{6,70},{7,71},{8,72},{9,... | collective-permute-start | bytes 24584 | tf_op jit(solution)/shard_map/ppermute | solution.py:24
  117.0 11.2 %collective-permute-start.10 = (bf16[128,2048]{0,1:T(8,128)(2,1)}, bf16[128,2048]{0,1:T(8,128)(2,1)}, u32[]{:S(2)}, u32[]{:S(2)}) collective-permute-start(bf16[128,2048]{0,1:T(8,128)(2,1)} %bitcast.538), channel_id=1, source_target_pairs={{0,64},{1,65},{2,66},{3,67},{4,68},{5,69},{6,70},{7,71},{8,72},{9,... | collective-permute-start | bytes 1572872 | tf_op jit(solution)/shard_map/ppermute | solution.py:24
  128.2 11.2 %collective-permute-start.12 = (bf16[128,2048]{0,1:T(8,128)(2,1)}, bf16[128,2048]{0,1:T(8,128)(2,1)}, u32[]{:S(2)}, u32[]{:S(2)}) collective-permute-start(bf16[128,2048]{0,1:T(8,128)(2,1)} %bitcast.537), channel_id=1, source_target_pairs={{0,64},{1,65},{2,66},{3,67},{4,68},{5,69},{6,70},{7,71},{8,72},{9,... | collective-permute-start | bytes 1572872 | tf_op jit(solution)/shard_map/ppermute | solution.py:24
  142.2 37.9 %while.45 = (s32[]{:T(128)}, f32[1,128,2048]{2,1,0:T(8,128)}, f32[8,128,512]{2,1,0:T(8,128)}, s32[]{:T(128)}, s32[8,2]{0,1:T(2,128)S(1)}, /*index=5*/bf16[8,128,...) while((s32[]{:T(128)}, f32[1,128,2048]{2,1,0:T(8,128)}, ...), condition=%wide.region_14.15_spmd.clone.clone, body=%wide.region_9.0_spmd.clone.clone.sunk | while | flops 1355798144 | bytes 103950968 | solution.py:110
  166.4 5.4 copy.274
  171.8 8.2 scatter_fusion.2
  184.8 57.3 %collective-permute-done.10 = bf16[128,2048]{0,1:T(8,128)(2,1)} collective-permute-done((bf16[128,2048]{0,1:T(8,128)(2,1)}, bf16[128,2048]{0,1:T(8,128)(2,1)}, u32[]{:S(2)}, u32[]{:S(2)}) %collective-permute-start.10) | collective-permute-done | bytes 524320 | tf_op jit(solution)/shard_map/ppermute | solution.py:24
  242.1 11.5 %collective-permute-done.12 = bf16[128,2048]{0,1:T(8,128)(2,1)} collective-permute-done((bf16[128,2048]{0,1:T(8,128)(2,1)}, bf16[128,2048]{0,1:T(8,128)(2,1)}, u32[]{:S(2)}, u32[]{:S(2)}) %collective-permute-start.12) | collective-permute-done | bytes 524320 | tf_op jit(solution)/shard_map/ppermute | solution.py:24
  253.5 22.9 %collective-permute-done.9 = bf16[8,128,512]{2,1,0:T(8,128)(2,1)} collective-permute-done((bf16[8,128,512]{2,1,0:T(8,128)(2,1)}, bf16[8,128,512]{2,1,0:T(8,128)(2,1)}, u32[]{:S(2)}, u32[]{:S(2)}) %collective-permute-start.9) | collective-permute-done | bytes 1048608 | tf_op jit(solution)/shard_map/ppermute | solution.py:24
  279.1 38.7 %while.46 = (s32[]{:T(128)}, f32[1,128,2048]{2,1,0:T(8,128)}, f32[8,128,512]{2,1,0:T(8,128)}, s32[]{:T(128)}, s32[8,2]{0,1:T(2,128)S(1)}, /*index=5*/bf16[8,128,...) while((s32[]{:T(128)}, f32[1,128,2048]{2,1,0:T(8,128)}, ...), condition=%wide.region_22.23_spmd.clone.clone, body=%wide.region_17.22_spmd.clone.clone.sunk | while | flops 1355798144 | bytes 95562248 | solution.py:110
  303.9 5.4 copy.279
  309.3 8.5 scatter_fusion.4
  327.9 299.4 %while.44 = (s32[]{:T(128)}, f32[4,128,2048]{2,1,0:T(8,128)}, f32[16,128,512]{2,1,0:T(8,128)}, s32[]{:T(128)}, s32[44,2]{0,1:T(2,128)S(1)}, /*index=5*/bf16[16,1...) while((s32[]{:T(128)}, f32[4,128,2048]{2,1,0:T(8,128)}, ...), condition=%wide.region_6.7_spmd.clone.clone, body=%wide.region_1.6_spmd.clone.clone.sunk | while | flops 1355799552 | bytes 98896416 | solution.py:110
  347.5 4.5 fusion.166
  374.0 5.4 copy.267
  379.4 8.3 scatter_fusion
  433.5 5.4 copy.267
  438.9 8.7 scatter_fusion
  493.5 5.4 copy.267
  499.0 8.7 scatter_fusion
  553.4 5.4 copy.267
  558.8 8.6 scatter_fusion
  613.2 5.4 copy.267
  618.6 8.6 scatter_fusion
  627.3 4.9 scatter_fusion.6
  632.2 4.7 scatter_fusion.7
  644.6 97.5 %collective-permute-start.19 = (f32[512,512]{1,0:T(8,128)S(1)}, f32[512,512]{1,0:T(8,128)S(1)}, u32[]{:S(2)}, u32[]{:S(2)}) collective-permute-start(f32[512,512]{1,0:T(8,128)S(1)} %bitcast.533), channel_id=1, source_target_pairs={{12,0},{16,4},{20,8},{24,12},{28,16},{32,20},{36,24},{40,28},{44,3... | collective-permute-start | bytes 3145736 | tf_op jit(solution)/shard_map/ppermute | solution.py:20
  748.6 150.0 %collective-permute-done.19 = f32[512,512]{1,0:T(8,128)S(1)} collective-permute-done((f32[512,512]{1,0:T(8,128)S(1)}, f32[512,512]{1,0:T(8,128)S(1)}, u32[]{:S(2)}, u32[]{:S(2)}) %collective-permute-start.19) | collective-permute-done | bytes 1048608 | tf_op jit(solution)/shard_map/ppermute | solution.py:20
  (381 shorter events, 349.7 us)
Async XLA Ops:
  2.6 19.3 %collective-permute-start = (bf16[512,512]{1,0:T(8,128)(2,1)S(1)}, bf16[512,512]{1,0:T(8,128)(2,1)S(1)}, u32[]{:S(2)}, u32[]{:S(2)}) collective-permute-start(bf16[512,512]{1,0:T(8,128)(2,1)S(1)} %constant_dynamic-update-slice_fusion), channel_id=1, source_target_pairs={{0,12},{4,16},{8,20},{12,24},{16,28},{20,32},{24,36},{28,40},{32,4... | collective-permute-start | bytes 1572872 | tf_op jit(solution)/shard_map/ppermute | solution.py:20
  6.5 20.5 %collective-permute-start.1 = (bf16[512,512]{1,0:T(8,128)(2,1)S(1)}, bf16[512,512]{1,0:T(8,128)(2,1)S(1)}, u32[]{:S(2)}, u32[]{:S(2)}) collective-permute-start(bf16[512,512]{1,0:T(8,128)(2,1)S(1)} %constant_dynamic-update-slice_fusion), channel_id=1, source_target_pairs={{0,8},{4,12},{8,16},{12,20},{16,24},{20,28},{24,32},{28,36},{32,40... | collective-permute-start | bytes 1572872 | tf_op jit(solution)/shard_map/ppermute | solution.py:20
  10.3 18.7 %collective-permute-start.2 = (bf16[512,512]{1,0:T(8,128)(2,1)S(1)}, bf16[512,512]{1,0:T(8,128)(2,1)S(1)}, u32[]{:S(2)}, u32[]{:S(2)}) collective-permute-start(bf16[512,512]{1,0:T(8,128)(2,1)S(1)} %constant_dynamic-update-slice_fusion), channel_id=1, source_target_pairs={{0,4},{4,8},{8,12},{12,16},{16,20},{20,24},{24,28},{28,32},{32,36}... | collective-permute-start | bytes 1572872 | tf_op jit(solution)/shard_map/ppermute | solution.py:20
  20.9 41.8 %copy-start.22 = (s32[8]{0:T(128)}, s32[8]{0:T(128)S(1)}, u32[]{:S(2)}) copy-start(s32[8]{0:T(128)S(1)} %get-tuple-element.504) | copy-start | bytes 100
  30.5 21.4 %copy-start.6 = (bf16[512,2048]{1,0:T(8,128)(2,1)S(1)}, bf16[512,2048]{1,0:T(8,128)(2,1)}, u32[]{:S(2)}) copy-start(bf16[512,2048]{1,0:T(8,128)(2,1)} %param.23) | copy-start | bytes 6291460
  33.8 105.6 %collective-permute-start.3 = (bf16[8,128,512]{2,1,0:T(8,128)(2,1)}, bf16[8,128,512]{2,1,0:T(8,128)(2,1)}, u32[]{:S(2)}, u32[]{:S(2)}) collective-permute-start(bf16[8,128,512]{2,1,0:T(8,128)(2,1)} %gather_fusion.11), channel_id=1, source_target_pairs={{0,128},{1,129},{2,130},{3,131},{4,132},{5,133},{6,134},{7,135},{8... | collective-permute-start | bytes 3145736 | tf_op jit(solution)/shard_map/ppermute | solution.py:24
  46.4 28.7 %collective-permute-start.5 = (f32[16,128]{1,0:T(8,128)S(1)}, f32[16,128]{1,0:T(8,128)S(1)}, u32[]{:S(2)}, u32[]{:S(2)}) collective-permute-start(f32[16,128]{1,0:T(8,128)S(1)} %bitcast.560), channel_id=1, source_target_pairs={{0,128},{1,129},{2,130},{3,131},{4,132},{5,133},{6,134},{7,135},{8... | collective-permute-start | bytes 24584 | tf_op jit(solution)/shard_map/ppermute | solution.py:24
  46.5 70.3 %collective-permute-start.7 = (f32[16,128]{1,0:T(8,128)S(1)}, f32[16,128]{1,0:T(8,128)S(1)}, u32[]{:S(2)}, u32[]{:S(2)}) collective-permute-start(f32[16,128]{1,0:T(8,128)S(1)} %bitcast.559), channel_id=1, source_target_pairs={{0,128},{1,129},{2,130},{3,131},{4,132},{5,133},{6,134},{7,135},{8... | collective-permute-start | bytes 24584 | tf_op jit(solution)/shard_map/ppermute | solution.py:24
  54.2 17.0 %copy-start.9 = (bf16[2048,512]{1,0:T(8,128)(2,1)S(1)}, bf16[2048,512]{1,0:T(8,128)(2,1)}, u32[]{:S(2)}) copy-start(bf16[2048,512]{1,0:T(8,128)(2,1)} %pad_maximum_fusion.3) | copy-start | bytes 6291460
  55.2 61.8 %collective-permute-start.4 = (bf16[128,2048]{0,1:T(8,128)(2,1)}, bf16[128,2048]{0,1:T(8,128)(2,1)S(1)}, u32[]{:S(2)}, u32[]{:S(2)}) collective-permute-start(bf16[128,2048]{0,1:T(8,128)(2,1)} %bitcast.540), channel_id=1, source_target_pairs={{0,128},{1,129},{2,130},{3,131},{4,132},{5,133},{6,134},{7,135},{8... | collective-permute-start | bytes 1572872 | tf_op jit(solution)/shard_map/ppermute | solution.py:24
  56.3 71.9 %collective-permute-start.6 = (bf16[128,2048]{0,1:T(8,128)(2,1)}, bf16[128,2048]{0,1:T(8,128)(2,1)S(1)}, u32[]{:S(2)}, u32[]{:S(2)}) collective-permute-start(bf16[128,2048]{0,1:T(8,128)(2,1)} %bitcast.539), channel_id=1, source_target_pairs={{0,128},{1,129},{2,130},{3,131},{4,132},{5,133},{6,134},{7,135},{8... | collective-permute-start | bytes 1572872 | tf_op jit(solution)/shard_map/ppermute | solution.py:24
  72.8 69.4 %copy-start.26 = (s32[40]{0:T(128)S(1)}, s32[40]{0:T(128)}, u32[]{:S(2)}) copy-start(s32[40]{0:T(128)} %param.25) | copy-start | bytes 484
  75.1 105.0 %collective-permute-start.11 = (f32[16,128]{1,0:T(8,128)S(1)}, f32[16,128]{1,0:T(8,128)S(1)}, u32[]{:S(2)}, u32[]{:S(2)}) collective-permute-start(f32[16,128]{1,0:T(8,128)S(1)} %bitcast.558), channel_id=1, source_target_pairs={{0,64},{1,65},{2,66},{3,67},{4,68},{5,69},{6,70},{7,71},{8,72},{9,... | collective-permute-start | bytes 24584 | tf_op jit(solution)/shard_map/ppermute | solution.py:24
  116.8 68.0 %collective-permute-start.13 = (f32[16,128]{1,0:T(8,128)S(1)}, f32[16,128]{1,0:T(8,128)S(1)}, u32[]{:S(2)}, u32[]{:S(2)}) collective-permute-start(f32[16,128]{1,0:T(8,128)S(1)} %bitcast.557), channel_id=1, source_target_pairs={{0,64},{1,65},{2,66},{3,67},{4,68},{5,69},{6,70},{7,71},{8,72},{9,... | collective-permute-start | bytes 24584 | tf_op jit(solution)/shard_map/ppermute | solution.py:24
  117.0 125.1 %collective-permute-start.10 = (bf16[128,2048]{0,1:T(8,128)(2,1)}, bf16[128,2048]{0,1:T(8,128)(2,1)}, u32[]{:S(2)}, u32[]{:S(2)}) collective-permute-start(bf16[128,2048]{0,1:T(8,128)(2,1)} %bitcast.538), channel_id=1, source_target_pairs={{0,64},{1,65},{2,66},{3,67},{4,68},{5,69},{6,70},{7,71},{8,72},{9,... | collective-permute-start | bytes 1572872 | tf_op jit(solution)/shard_map/ppermute | solution.py:24
  128.2 125.3 %collective-permute-start.12 = (bf16[128,2048]{0,1:T(8,128)(2,1)}, bf16[128,2048]{0,1:T(8,128)(2,1)}, u32[]{:S(2)}, u32[]{:S(2)}) collective-permute-start(bf16[128,2048]{0,1:T(8,128)(2,1)} %bitcast.537), channel_id=1, source_target_pairs={{0,64},{1,65},{2,66},{3,67},{4,68},{5,69},{6,70},{7,71},{8,72},{9,... | collective-permute-start | bytes 1572872 | tf_op jit(solution)/shard_map/ppermute | solution.py:24
  139.4 136.9 %collective-permute-start.9 = (bf16[8,128,512]{2,1,0:T(8,128)(2,1)}, bf16[8,128,512]{2,1,0:T(8,128)(2,1)}, u32[]{:S(2)}, u32[]{:S(2)}) collective-permute-start(bf16[8,128,512]{2,1,0:T(8,128)(2,1)} %gather_fusion.12), channel_id=1, source_target_pairs={{0,64},{1,65},{2,66},{3,67},{4,68},{5,69},{6,70},{7,71},{8,72},{9,... | collective-permute-start | bytes 3145736 | tf_op jit(solution)/shard_map/ppermute | solution.py:24
  180.1 447.2 %collective-permute-start.15 = (f32[8,128,512]{2,1,0:T(8,128)}, f32[8,128,512]{2,1,0:T(8,128)}, u32[]{:S(2)}, u32[]{:S(2)}) collective-permute-start(f32[8,128,512]{2,1,0:T(8,128)} %get-tuple-element.262), channel_id=1, source_target_pairs={{0,128},{1,129},{2,130},{3,131},{4,132},{5,133},{6,134},{7,135},{8... | collective-permute-start | bytes 6291464 | tf_op jit(solution)/shard_map/ppermute | solution.py:24
  317.8 314.4 %collective-permute-start.16 = (f32[8,128,512]{2,1,0:T(8,128)}, f32[8,128,512]{2,1,0:T(8,128)}, u32[]{:S(2)}, u32[]{:S(2)}) collective-permute-start(f32[8,128,512]{2,1,0:T(8,128)} %get-tuple-element.263), channel_id=1, source_target_pairs={{0,64},{1,65},{2,66},{3,67},{4,68},{5,69},{6,70},{7,71},{8,72},{9,... | collective-permute-start | bytes 6291464 | tf_op jit(solution)/shard_map/ppermute | solution.py:24
  317.8 425.0 %collective-permute-start.8 = (f32[1,128,2048]{2,1,0:T(8,128)}, f32[1,128,2048]{2,1,0:T(8,128)}, u32[]{:S(2)}, u32[]{:S(2)}) collective-permute-start(f32[1,128,2048]{2,1,0:T(8,128)} %get-tuple-element.259), channel_id=1, source_target_pairs={{0,128},{1,129},{2,130},{3,131},{4,132},{5,133},{6,134},{7,135},{8... | collective-permute-start | bytes 3145736 | tf_op jit(solution)/shard_map/ppermute | solution.py:24
  320.5 424.3 %collective-permute-start.14 = (f32[1,128,2048]{2,1,0:T(8,128)}, f32[1,128,2048]{2,1,0:T(8,128)}, u32[]{:S(2)}, u32[]{:S(2)}) collective-permute-start(f32[1,128,2048]{2,1,0:T(8,128)} %get-tuple-element.260), channel_id=1, source_target_pairs={{0,64},{1,65},{2,66},{3,67},{4,68},{5,69},{6,70},{7,71},{8,72},{9,... | collective-permute-start | bytes 3145736 | tf_op jit(solution)/shard_map/ppermute | solution.py:24
  438.9 8.7 copy-start.17
  438.9 8.7 copy-start.28
  499.0 8.7 copy-start.17
  499.0 8.7 copy-start.28
  558.8 8.6 copy-start.17
  558.8 8.6 copy-start.28
  636.9 105.2 %copy-start.25 = (s32[3]{0:T(128)S(1)}, s32[3]{0:T(128)}, u32[]{:S(2)}) copy-start(s32[3]{0:T(128)} %constant.176.clone.1) | copy-start | bytes 40
  636.9 105.9 %copy-start = (f32[4,128,2048]{2,1,0:T(8,128)S(1)}, f32[4,128,2048]{2,1,0:T(8,128)}, u32[]{:S(2)}) copy-start(f32[4,128,2048]{2,1,0:T(8,128)} %get-tuple-element.1109) | copy-start | bytes 12582916
  640.0 108.6 %collective-permute-start.17 = (f32[512,512]{1,0:T(8,128)S(1)}, f32[512,512]{1,0:T(8,128)S(1)}, u32[]{:S(2)}, u32[]{:S(2)}) collective-permute-start(f32[512,512]{1,0:T(8,128)S(1)} %bitcast.535), channel_id=1, source_target_pairs={{4,0},{8,4},{12,8},{16,12},{20,16},{24,20},{28,24},{32,28},{36,32}... | collective-permute-start | bytes 3145736 | tf_op jit(solution)/shard_map/ppermute | solution.py:20
  641.9 106.7 %collective-permute-start.18 = (f32[512,512]{1,0:T(8,128)S(1)}, f32[512,512]{1,0:T(8,128)S(1)}, u32[]{:S(2)}, u32[]{:S(2)}) collective-permute-start(f32[512,512]{1,0:T(8,128)S(1)} %bitcast.534), channel_id=1, source_target_pairs={{8,0},{12,4},{16,8},{20,12},{24,16},{28,20},{32,24},{36,28},{40,32... | collective-permute-start | bytes 3145736 | tf_op jit(solution)/shard_map/ppermute | solution.py:20
  644.6 254.0 %collective-permute-start.19 = (f32[512,512]{1,0:T(8,128)S(1)}, f32[512,512]{1,0:T(8,128)S(1)}, u32[]{:S(2)}, u32[]{:S(2)}) collective-permute-start(f32[512,512]{1,0:T(8,128)S(1)} %bitcast.533), channel_id=1, source_target_pairs={{12,0},{16,4},{20,8},{24,12},{28,16},{32,20},{36,24},{40,28},{44,3... | collective-permute-start | bytes 3145736 | tf_op jit(solution)/shard_map/ppermute | solution.py:20
  (33 other events, 124.0 us)
where the time goes:
time: 911 us; the launch traced here: 900 us
  waiting for transfers between devices  252 us (28%)
  starting transfers between devices  209 us (23%)
  local copies, waits for them, and re-layouts  204 us (22%)
  matrix products  114 us (13%)
  other arithmetic  113 us (12%)
    ppermute x6, waiting for transfers between devices, shifted(): return lax.ppermute(shard, axis, pairs)  158 us
    ppermute x6, starting transfers between devices, shifted(): return lax.ppermute(shard, axis, pairs)  112 us
    ppermute x14, starting transfers between devices, swapped(): lax.ppermute(shard, axis, [(i, i ^ 1 << apart) for i in range(lax.axis_si...  97.2 us
    ppermute x14, waiting for transfers between devices, swapped(): lax.ppermute(shard, axis, [(i, i ^ 1 << apart) for i in range(lax.axis_si...  94.2 us
    scatter-add x7, other arithmetic, one_turn(): query_grads.at[query_index]  59.6 us
    reshape x7, local copies, waits for them, and re-layouts, one_turn(): part_query.reshape(GROUP_PAIRS, BLOCK, features)  37.9 us
    dot_general x7, matrix products, one_turn(): jnp.einsum('pqhgd,pkhd->phgqk', outgrad_rows, value_rows, preferred_eleme...  31.3 us
    dot_general x7, matrix products, one_turn(): jnp.einsum('pqhgd,pkhd->phgqk', query_rows, key_rows, preferred_element_t...  25.5 us
  transfers between devices with their start and end apart: 20, of which 9 were waited for; matrix products, arithmetic and copies ran while one was open for 47% of the time, Pallas kernels for 0%

commit v1 on v0

v1 whole, which is shorter than its diff:
```python
import functools
import jax
import jax.numpy as jnp
from jax import lax
from jax.experimental import pallas as pl
from jax.experimental.pallas import tpu as pltpu
from jax.sharding import PartitionSpec as P

HEAD_DIM = 128
BLOCK = 128

NT = (((1,), (1,)), ((), ()))
TN = (((0,), (0,)), ((), ()))


def pair_kernel(pairs_ref, count_ref, q_ref, do_ref, norm_ref, delta_ref, qdoc_ref, qpos_ref,
                kdoc_ref, kpos_ref, kv_ref, dq_ref, dkv_ref):
    dq_ref[...] = jnp.zeros(dq_ref.shape, jnp.float32)
    dkv_ref[...] = jnp.zeros(dkv_ref.shape, jnp.float32)
    heads = norm_ref.shape[0]
    kv_features = kv_ref.shape[1] // 2
    kv_heads = kv_features // HEAD_DIM
    group = heads // kv_heads
    scale = HEAD_DIM ** (-0.5)

    def body(i, carry):
        qb = jnp.maximum(pairs_ref[2 * i], 0)
        kb = jnp.maximum(pairs_ref[2 * i + 1], 0)
        qrow = pl.multiple_of(qb * BLOCK, BLOCK)
        krow = pl.multiple_of(kb * BLOCK, BLOCK)
        qdoc = qdoc_ref[pl.ds(qb, 1), :]
        qpos = qpos_ref[pl.ds(qb, 1), :]
        kdoc = kdoc_ref[pl.ds(krow, BLOCK), :]
        kpos = kpos_ref[pl.ds(krow, BLOCK), :]
        allowed = (kdoc == qdoc) & (kpos <= qpos)
        for g in range(kv_heads):
            k = kv_ref[pl.ds(krow, BLOCK), pl.ds(g * HEAD_DIM, HEAD_DIM)]
            v = kv_ref[pl.ds(krow, BLOCK), pl.ds(kv_features + g * HEAD_DIM, HEAD_DIM)]
            dk = jnp.zeros((BLOCK, HEAD_DIM), jnp.float32)
            dv = jnp.zeros((BLOCK, HEAD_DIM), jnp.float32)
            for j in range(group):
                h = g * group + j
                cols = pl.ds(h * HEAD_DIM, HEAD_DIM)
                q = q_ref[pl.ds(qrow, BLOCK), cols]
                do = do_ref[pl.ds(qrow, BLOCK), cols]
                norm = norm_ref[pl.ds(h, 1), pl.ds(qrow, BLOCK)]
                dl = delta_ref[pl.ds(h, 1), pl.ds(qrow, BLOCK)]
                scores = lax.dot_general(k, q, NT, preferred_element_type=jnp.float32) * scale
                weights = jnp.where(allowed, jnp.exp(scores - norm), 0.0)
                weight_grads = lax.dot_general(v, do, NT, preferred_element_type=jnp.float32)
                score_grads = (weights * (weight_grads - dl)).astype(jnp.bfloat16)
                weights_low = weights.astype(jnp.bfloat16)
                dv = dv + jnp.dot(weights_low, do, preferred_element_type=jnp.float32)
                dk = dk + jnp.dot(score_grads, q, preferred_element_type=jnp.float32)
                part_query = lax.dot_general(score_grads, k, TN, preferred_element_type=jnp.float32)
                dq_ref[pl.ds(qrow, BLOCK), cols] += part_query * scale
            dkv_ref[pl.ds(krow, BLOCK), pl.ds(g * HEAD_DIM, HEAD_DIM)] += dk * scale
            dkv_ref[pl.ds(krow, BLOCK), pl.ds(kv_features + g * HEAD_DIM, HEAD_DIM)] += dv
        return carry

    lax.fori_loop(0, count_ref[0], body, 0)


def run_pairs(pairs, count, queries, outgrads, norms, deltas, query_pos, keyval, key_pos, doc_bounds):
    q_doc = doc_index(query_pos, doc_bounds)
    k_doc = doc_index(key_pos, doc_bounds)
    tokens, features = queries.shape
    window, both = keyval.shape
    vmem = pltpu.MemorySpace.VMEM
    smem = pltpu.MemorySpace.SMEM
    args = (
        pairs.reshape(-1).astype(jnp.int32),
        jnp.reshape(count, (1,)).astype(jnp.int32),
        queries, outgrads, norms, deltas,
        q_doc, query_pos,
        k_doc.reshape(window, 1), key_pos.reshape(window, 1),
        keyval,
    )
    specs = [pl.BlockSpec(memory_space=smem)] * 2 + [pl.BlockSpec(memory_space=vmem)] * 9
    return pl.pallas_call(
        pair_kernel,
        out_shape=(
            jax.ShapeDtypeStruct((tokens, features), jnp.float32),
            jax.ShapeDtypeStruct((window, both), jnp.float32),
        ),
        in_specs=specs,
        out_specs=(pl.BlockSpec(memory_space=vmem), pl.BlockSpec(memory_space=vmem)),
        compiler_params=pltpu.CompilerParams(vmem_limit_bytes=48 * 1024 * 1024),
    )(*args)


SHIP_SLOTS = 8
ROUNDS = 2
REACH = 3
WIN_BLOCKS = 16


def shifted(shard, axis, by):
    length = lax.axis_size(axis)
    pairs = [(i, i + by) for i in range(length) if 0 <= i + by < length]
    return lax.ppermute(shard, axis, pairs)


def swapped(shard, axis, apart):
    return lax.ppermute(shard, axis, [(i, i ^ 1 << apart) for i in range(lax.axis_size(axis))])


def doc_index(positions, doc_bounds):
    flat = positions.reshape(-1)
    edges = doc_bounds[1:]
    counts = jnp.sum((edges[None, :] <= flat[:, None]).astype(jnp.int32), axis=1)
    return counts.reshape(positions.shape)


def local(query, key, value, attn_out, grad_out, log_norm, doc_bounds, local_pairs, ship_table):
    position = lax.axis_index("ctx")
    tokens, features = query.shape
    kv_features = key.shape[1]
    heads = log_norm.shape[0]
    own_blocks = tokens // BLOCK
    offsets = jnp.arange(BLOCK, dtype=jnp.int32)
    delta = jnp.einsum(
        "thd,thd->ht",
        grad_out.reshape(tokens, heads, HEAD_DIM),
        attn_out.reshape(tokens, heads, HEAD_DIM),
        preferred_element_type=jnp.float32,
    )
    own_keyval = jnp.concatenate([key, value], axis=1)
    pieces = []
    for hop in range(REACH, 0, -1):
        pieces.append(shifted(own_keyval, "ctx", hop))
    keyval_window = jnp.concatenate(pieces + [own_keyval], axis=0)
    first_block = position * own_blocks
    query_pos = (first_block + jnp.arange(own_blocks, dtype=jnp.int32))[:, None] * BLOCK + offsets
    window_first = first_block - REACH * own_blocks
    key_pos = (window_first * BLOCK + jnp.arange(WIN_BLOCKS * BLOCK, dtype=jnp.int32))
    local_count = jnp.sum((local_pairs[:, 0] >= 0).astype(jnp.int32))
    query_grads, keyval_grads = run_pairs(
        local_pairs, local_count, query, grad_out, log_norm, delta, query_pos,
        keyval_window, key_pos, doc_bounds,
    )
    query_grads = query_grads.reshape(own_blocks, BLOCK, features)
    keyval_grads = keyval_grads.reshape(WIN_BLOCKS, BLOCK, 2 * kv_features)
    queries = query.reshape(own_blocks, BLOCK, features)
    outgrads = grad_out.reshape(own_blocks, BLOCK, features)
    window_blocks = keyval_window.reshape(WIN_BLOCKS, BLOCK, 2 * kv_features)
    head_bits = lax.axis_size("head").bit_length() - 1
    all_bits = lax.axis_size(("ctx", "head")).bit_length() - 1
    slot_range = jnp.arange(SHIP_SLOTS, dtype=jnp.int32)
    for section in range(ROUNDS):
        my_row = ship_table[position, section]
        bit = all_bits - 1 - section
        partner = jnp.bitwise_xor(position, 1 << bit - head_bits)
        far_row = ship_table[partner, section]
        sent = jnp.maximum(my_row[0], 0)
        my_slots = jnp.maximum(my_row[1:], 0)
        sent_norms = lax.dynamic_slice_in_dim(log_norm, sent * BLOCK, BLOCK, 1)
        sent_delta = lax.dynamic_slice_in_dim(delta, sent * BLOCK, BLOCK, 1)
        got_norms, got_delta = swapped((sent_norms, sent_delta), ("ctx", "head"), bit)
        got_query, got_grad, got_keyval = swapped(
            (queries[sent], outgrads[sent], window_blocks[my_slots]), ("ctx", "head"), bit
        )
        far_count = jnp.sum((far_row[1:] >= 0).astype(jnp.int32))
        far_pairs = jnp.stack([jnp.zeros_like(slot_range), slot_range], axis=1)
        far_query_pos = ((partner * own_blocks + jnp.maximum(far_row[0], 0)) * BLOCK + offsets)[None]
        far_first = (partner - REACH) * own_blocks
        far_key_pos = (
            (far_first + jnp.maximum(far_row[1:], 0))[:, None] * BLOCK + offsets
        ).reshape(-1)
        back_query, back_keyval = run_pairs(
            far_pairs, far_count, got_query, got_grad, got_norms, got_delta, far_query_pos,
            got_keyval.reshape(SHIP_SLOTS * BLOCK, 2 * kv_features), far_key_pos, doc_bounds,
        )
        returned = swapped(
            (back_query, back_keyval.reshape(SHIP_SLOTS, BLOCK, 2 * kv_features)),
            ("ctx", "head"), bit,
        )
        query_grads = query_grads.at[sent].add(returned[0])
        keyval_grads = keyval_grads.at[my_slots].add(returned[1])
    segments = keyval_grads.reshape(REACH + 1, own_blocks * BLOCK, 2 * kv_features)
    own_grads = segments[REACH]
    for hop in range(1, REACH + 1):
        own_grads = own_grads + shifted(segments[REACH - hop], "ctx", -hop)
    grad_query = query_grads.reshape(tokens, features).astype(jnp.bfloat16)
    grad_key = own_grads[:, :kv_features].astype(jnp.bfloat16)
    grad_value = own_grads[:, kv_features:].astype(jnp.bfloat16)
    return (grad_query, grad_key, grad_value)


def solution(mesh):
    in_specs = (
        P("ctx", "head"),
        P("ctx", "head"),
        P("ctx", "head"),
        P("ctx", "head"),
        P("ctx", "head"),
        P("head", "ctx"),
        P(),
        P("ctx", None),
        P(),
    )
    out_specs = (P("ctx", "head"), P("ctx", "head"), P("ctx", "head"))
    return jax.shard_map(local, mesh=mesh, in_specs=in_specs, out_specs=out_specs, check_vma=False)
```

time: 911 us -> 712 us (0.78)
  the two profiles are of different devices: /device:TPU:23 before, /device:TPU:62 now
where the time goes in v1:
time: 712 us; the launch traced here: 701 us
  waiting for transfers between devices  498 us (70%)
  Pallas kernels  74.4 us (10%)
  starting transfers between devices  72.1 us (10%)
  local copies, waits for them, and re-layouts  29.6 us (4%)
  other arithmetic  23.1 us (3%)
    ppermute x14, waiting for transfers between devices, swapped(): lax.ppermute(shard, axis, [(i, i ^ 1 << apart) for i in range(lax.axis_si...  423 us
    ppermute x6, waiting for transfers between devices, shifted(): return lax.ppermute(shard, axis, pairs)  74.5 us
    pallas_call x3, Pallas kernels, run_pairs(): pl.pallas_call(pair_kernel, out_shape=(jax.ShapeDtypeStruct((tokens, feat...  74.4 us
    ppermute x14, starting transfers between devices, swapped(): lax.ppermute(shard, axis, [(i, i ^ 1 << apart) for i in range(lax.axis_si...  56 us
    ppermute x6, starting transfers between devices, shifted(): return lax.ppermute(shard, axis, pairs)  16.1 us
  transfers between devices with their start and end apart: 20, of which 8 were waited for; matrix products, arithmetic and copies ran while one was open for 6% of the time, Pallas kernels for 11%

profile of v1, /device:TPU:62, one launch (start us, length us, event | category | flops | bytes accessed | tf_op | source)
XLA Modules:
  0.0 700.6 jit_solution(6839671329587327240)
XLA Ops:
  2.6 2.9 collective-permute-start
  5.5 3.5 collective-permute-start.1
  9.0 3.9 collective-permute-start.2
  12.9 2.3 copy.33
  19.3 5.5 collective-permute-start.6
  27.7 6.5 collective-permute-done.1
  35.6 2.7 pad_maximum_fusion.kv_ref
  38.3 3.2 gather_fusion
  41.5 6.3 collective-permute-start.7
  47.8 3.2 gather_fusion.1
  55.3 2.1 dynamic-slice_bitcast_fusion
  57.5 4.5 collective-permute-start.4
  62.1 14.4 %collective-permute-done.5.norm_ref = f32[16,128]{1,0:T(8,128)S(1)} collective-permute-done((f32[16,128]{1,0:T(8,128)S(1)}, f32[16,128]{1,0:T(8,128)S(1)}, u32[]{:S(2)}, u32[]{:S(2)}) %collective-permute-start.5) | collective-permute-done | bytes 8224 | tf_op jit(solution)/shard_map/ppermute | solution.py:105
  76.5 17.4 %collective-permute-start.10 = (bf16[128,2048]{1,0:T(8,128)(2,1)}, bf16[128,2048]{1,0:T(8,128)(2,1)}, u32[]{:S(2)}, u32[]{:S(2)}) collective-permute-start(bf16[128,2048]{1,0:T(8,128)(2,1)} %get-tuple-element.55), channel_id=1, source_target_pairs={{0,64},{1,65},{2,66},{3,67},{4,68},{5,69},{6,70},{7,71},{8,72},{9,... | collective-permute-start | bytes 1572872 | tf_op jit(solution)/shard_map/ppermute | solution.py:105
  95.0 5.4 collective-permute-start.12
  107.4 6.8 shard_map.113
  115.2 303.1 %collective-permute-done.12.delta_ref = f32[16,128]{1,0:T(8,128)S(1)} collective-permute-done((f32[16,128]{1,0:T(8,128)S(1)}, f32[16,128]{1,0:T(8,128)S(1)}, u32[]{:S(2)}, u32[]{:S(2)}) %collective-permute-start.12) | collective-permute-done | bytes 8224 | tf_op jit(solution)/shard_map/ppermute | solution.py:105
  418.3 6.2 collective-permute-start.15
  424.5 7.3 %shard_map.114 = (f32[128,2048]{1,0:T(8,128)S(1)}, f32[1024,512]{1,0:T(8,128)}) custom-call(s32[16]{0:T(128)S(1)} %copy-done.8, s32[1]{0:T(128)} %bitcast.24.count_ref, bf16[128,2048]{1,0:T(8,128)(2,1)} %collective-permute-done.9.q_ref, bf16[128,2048]{1,0:T(8,128)(2,1)} %collective-permute-done.10.do_ref, f32[16,128]{1,0:T(8,128)S(1)} %collective-permute-done.11.norm_ref, ...), custom_call_target="tpu_custom_call" | custom-call | tf_op jit(solution)/shard_map/pallas_call | solution.py:80
  432.9 7.0 collective-permute-start.16
  441.6 60.3 %shard_map.112 = (f32[512,2048]{1,0:T(8,128)}, f32[2048,512]{1,0:T(8,128)}) custom-call(s32[88]{0:T(128)S(1)} %reshape.332.pairs_ref, s32[1]{0:T(128)} %bitcast.2.count_ref, bf16[512,2048]{1,0:T(8,128)(2,1)S(1)} %copy-done, bf16[512,2048]{1,0:T(8,128)(2,1)} %do_ref.1, f32[16,512]{1,0:T(8,128)S(1)} %copy-done.7, f32[16,512]{1,0:T(8,128)S(1)} %copy.31.delta_ref, ...), custom_call_target="tpu_custom_call" | custom-call | tf_op jit(solution)/shard_map/pallas_call | solution.py:80
  501.9 4.9 scatter_fusion
  506.9 78.0 %collective-permute-done.16 = f32[8,128,512]{2,1,0:T(8,128)} collective-permute-done((f32[8,128,512]{2,1,0:T(8,128)}, f32[8,128,512]{2,1,0:T(8,128)}, u32[]{:S(2)}, u32[]{:S(2)}) %collective-permute-start.16) | collective-permute-done | bytes 2097184 | tf_op jit(solution)/shard_map/ppermute | solution.py:105
  584.9 4.8 scatter_fusion.1
  589.7 3.0 fusion.15
  592.7 1.9 collective-permute-start.17
  594.6 1.9 collective-permute-start.18
  599.2 2.1 fusion.1
  601.3 27.7 %collective-permute-done.14 = f32[128,2048]{1,0:T(8,128)} collective-permute-done((f32[128,2048]{1,0:T(8,128)}, f32[128,2048]{1,0:T(8,128)}, u32[]{:S(2)}, u32[]{:S(2)}) %collective-permute-start.14) | collective-permute-done | bytes 1048608 | tf_op jit(solution)/shard_map/ppermute | solution.py:105
  629.0 2.0 fusion.2
  632.7 63.2 %collective-permute-done.18 = f32[512,512]{1,0:T(8,128)S(1)} collective-permute-done((f32[512,512]{1,0:T(8,128)S(1)}, f32[512,512]{1,0:T(8,128)S(1)}, u32[]{:S(2)}, u32[]{:S(2)}) %collective-permute-start.18) | collective-permute-done | bytes 1048608 | tf_op jit(solution)/shard_map/ppermute | solution.py:101
  695.8 3.4 collective-permute-done.19
  (92 shorter events, 29.4 us)
Async XLA Ops:
  2.6 25.1 %collective-permute-start = (bf16[512,512]{1,0:T(8,128)(2,1)S(1)}, bf16[512,512]{1,0:T(8,128)(2,1)S(1)}, u32[]{:S(2)}, u32[]{:S(2)}) collective-permute-start(bf16[512,512]{1,0:T(8,128)(2,1)S(1)} %constant_dynamic-update-slice_fusion), channel_id=1, source_target_pairs={{0,12},{4,16},{8,20},{12,24},{16,28},{20,32},{24,36},{28,40},{32,4... | collective-permute-start | bytes 1572872 | tf_op jit(solution)/shard_map/ppermute | solution.py:101
  5.5 28.6 %collective-permute-start.1 = (bf16[512,512]{1,0:T(8,128)(2,1)S(1)}, bf16[512,512]{1,0:T(8,128)(2,1)}, u32[]{:S(2)}, u32[]{:S(2)}) collective-permute-start(bf16[512,512]{1,0:T(8,128)(2,1)S(1)} %constant_dynamic-update-slice_fusion), channel_id=1, source_target_pairs={{0,8},{4,12},{8,16},{12,20},{16,24},{20,28},{24,32},{28,36},{32,40... | collective-permute-start | bytes 1572872 | tf_op jit(solution)/shard_map/ppermute | solution.py:101
  9.0 26.6 %collective-permute-start.2 = (bf16[512,512]{1,0:T(8,128)(2,1)S(1)}, bf16[512,512]{1,0:T(8,128)(2,1)}, u32[]{:S(2)}, u32[]{:S(2)}) collective-permute-start(bf16[512,512]{1,0:T(8,128)(2,1)S(1)} %constant_dynamic-update-slice_fusion), channel_id=1, source_target_pairs={{0,4},{4,8},{8,12},{12,16},{16,20},{20,24},{24,28},{28,32},{32,36}... | collective-permute-start | bytes 1572872 | tf_op jit(solution)/shard_map/ppermute | solution.py:101
  12.9 2.4 copy-start.12
  15.9 1.2 copy-start.13
  15.9 8.8 %copy-start = (bf16[512,2048]{1,0:T(8,128)(2,1)S(1)}, bf16[512,2048]{1,0:T(8,128)(2,1)}, u32[]{:S(2)}) copy-start(bf16[512,2048]{1,0:T(8,128)(2,1)} %q_ref.1) | copy-start | bytes 6291460
  19.3 38.2 %collective-permute-start.6 = (f32[16,128]{1,0:T(8,128)S(1)}, f32[16,128]{1,0:T(8,128)S(1)}, u32[]{:S(2)}, u32[]{:S(2)}) collective-permute-start(f32[16,128]{1,0:T(8,128)S(1)} %get-tuple-element.62), channel_id=1, source_target_pairs={{0,128},{1,129},{2,130},{3,131},{4,132},{5,133},{6,134},{7,135},{8... | collective-permute-start | bytes 24584 | tf_op jit(solution)/shard_map/ppermute | solution.py:105
  25.8 68.1 %collective-permute-start.3 = (bf16[128,2048]{1,0:T(8,128)(2,1)}, bf16[128,2048]{1,0:T(8,128)(2,1)}, u32[]{:S(2)}, u32[]{:S(2)}) collective-permute-start(bf16[128,2048]{1,0:T(8,128)(2,1)} %get-tuple-element.58), channel_id=1, source_target_pairs={{0,128},{1,129},{2,130},{3,131},{4,132},{5,133},{6,134},{7,135},{8... | collective-permute-start | bytes 1572872 | tf_op jit(solution)/shard_map/ppermute | solution.py:105
  38.3 14.2 %copy-start.7 = (f32[16,512]{1,0:T(8,128)S(1)}, f32[16,512]{1,0:T(8,128)}, u32[]{:S(2)}) copy-start(f32[16,512]{1,0:T(8,128)} %norm_ref.1) | copy-start | bytes 98308
  41.5 58.9 %collective-permute-start.7 = (bf16[8,128,512]{2,1,0:T(8,128)(2,1)}, bf16[8,128,512]{2,1,0:T(8,128)(2,1)S(1)}, u32[]{:S(2)}, u32[]{:S(2)}) collective-permute-start(bf16[8,128,512]{2,1,0:T(8,128)(2,1)} %gather_fusion), channel_id=1, source_target_pairs={{0,128},{1,129},{2,130},{3,131},{4,132},{5,133},{6,134},{7,135},{8... | collective-permute-start | bytes 3145736 | tf_op jit(solution)/shard_map/ppermute | solution.py:105
  47.8 9.6 %copy-start.16 = (s32[40]{0:T(128)S(1)}, s32[40]{0:T(128)}, u32[]{:S(2)}) copy-start(s32[40]{0:T(128)} %param.19) | copy-start | bytes 484
  51.0 373.5 %collective-permute-start.13 = (bf16[8,128,512]{2,1,0:T(8,128)(2,1)}, bf16[8,128,512]{2,1,0:T(8,128)(2,1)}, u32[]{:S(2)}, u32[]{:S(2)}) collective-permute-start(bf16[8,128,512]{2,1,0:T(8,128)(2,1)} %gather_fusion.1), channel_id=1, source_target_pairs={{0,64},{1,65},{2,66},{3,67},{4,68},{5,69},{6,70},{7,71},{8,72},{9,... | collective-permute-start | bytes 3145736 | tf_op jit(solution)/shard_map/ppermute | solution.py:105
  52.5 24.0 %collective-permute-start.5 = (f32[16,128]{1,0:T(8,128)S(1)}, f32[16,128]{1,0:T(8,128)S(1)}, u32[]{:S(2)}, u32[]{:S(2)}) collective-permute-start(f32[16,128]{1,0:T(8,128)S(1)} %get-tuple-element.64), channel_id=1, source_target_pairs={{0,128},{1,129},{2,130},{3,131},{4,132},{5,133},{6,134},{7,135},{8... | collective-permute-start | bytes 24584 | tf_op jit(solution)/shard_map/ppermute | solution.py:105
  55.3 47.8 %copy-start.8 = (s32[16]{0:T(128)S(1)}, s32[16]{0:T(128)}, u32[]{:S(2)}) copy-start(s32[16]{0:T(128)} %constant.84.clone.1.pairs_ref) | copy-start | bytes 196
  57.5 36.7 %collective-permute-start.4 = (bf16[128,2048]{1,0:T(8,128)(2,1)S(1)}, bf16[128,2048]{1,0:T(8,128)(2,1)S(1)}, u32[]{:S(2)}, u32[]{:S(2)}) collective-permute-start(bf16[128,2048]{1,0:T(8,128)(2,1)S(1)} %get-tuple-element.56), channel_id=1, source_target_pairs={{0,128},{1,129},{2,130},{3,131},{4,132},{5,133},{6,134},{7,135},{8... | collective-permute-start | bytes 1572872 | tf_op jit(solution)/shard_map/ppermute | solution.py:105
  76.5 348.0 %collective-permute-start.10 = (bf16[128,2048]{1,0:T(8,128)(2,1)}, bf16[128,2048]{1,0:T(8,128)(2,1)}, u32[]{:S(2)}, u32[]{:S(2)}) collective-permute-start(bf16[128,2048]{1,0:T(8,128)(2,1)} %get-tuple-element.55), channel_id=1, source_target_pairs={{0,64},{1,65},{2,66},{3,67},{4,68},{5,69},{6,70},{7,71},{8,72},{9,... | collective-permute-start | bytes 1572872 | tf_op jit(solution)/shard_map/ppermute | solution.py:105
  93.9 330.6 %collective-permute-start.9 = (bf16[128,2048]{1,0:T(8,128)(2,1)}, bf16[128,2048]{1,0:T(8,128)(2,1)}, u32[]{:S(2)}, u32[]{:S(2)}) collective-permute-start(bf16[128,2048]{1,0:T(8,128)(2,1)} %get-tuple-element.57), channel_id=1, source_target_pairs={{0,64},{1,65},{2,66},{3,67},{4,68},{5,69},{6,70},{7,71},{8,72},{9,... | collective-permute-start | bytes 1572872 | tf_op jit(solution)/shard_map/ppermute | solution.py:105
  95.0 323.3 %collective-permute-start.12 = (f32[16,128]{1,0:T(8,128)S(1)}, f32[16,128]{1,0:T(8,128)S(1)}, u32[]{:S(2)}, u32[]{:S(2)}) collective-permute-start(f32[16,128]{1,0:T(8,128)S(1)} %get-tuple-element.61), channel_id=1, source_target_pairs={{0,64},{1,65},{2,66},{3,67},{4,68},{5,69},{6,70},{7,71},{8,72},{9,... | collective-permute-start | bytes 24584 | tf_op jit(solution)/shard_map/ppermute | solution.py:105
  100.3 2.2 copy-start.3
  100.3 324.2 %collective-permute-start.11 = (f32[16,128]{1,0:T(8,128)S(1)}, f32[16,128]{1,0:T(8,128)S(1)}, u32[]{:S(2)}, u32[]{:S(2)}) collective-permute-start(f32[16,128]{1,0:T(8,128)S(1)} %get-tuple-element.63), channel_id=1, source_target_pairs={{0,64},{1,65},{2,66},{3,67},{4,68},{5,69},{6,70},{7,71},{8,72},{9,... | collective-permute-start | bytes 24584 | tf_op jit(solution)/shard_map/ppermute | solution.py:105
  103.0 1.0 copy-start.1
  105.1 1.2 copy-start.4
  418.3 83.7 %collective-permute-start.15 = (f32[8,128,512]{2,1,0:T(8,128)}, f32[8,128,512]{2,1,0:T(8,128)}, u32[]{:S(2)}, u32[]{:S(2)}) collective-permute-start(f32[8,128,512]{2,1,0:T(8,128)} %bitcast.87), channel_id=1, source_target_pairs={{0,128},{1,129},{2,130},{3,131},{4,132},{5,133},{6,134},{7,135},{8... | collective-permute-start | bytes 6291464 | tf_op jit(solution)/shard_map/ppermute | solution.py:105
  424.5 16.0 %copy-start.14 = (s32[44,2]{0,1:T(2,128)S(1)}, s32[44,2]{0,1:T(2,128)}, u32[]{:S(2)}) copy-start(s32[44,2]{0,1:T(2,128)} %param.20) | copy-start | bytes 1060
  432.9 152.0 %collective-permute-start.16 = (f32[8,128,512]{2,1,0:T(8,128)}, f32[8,128,512]{2,1,0:T(8,128)}, u32[]{:S(2)}, u32[]{:S(2)}) collective-permute-start(f32[8,128,512]{2,1,0:T(8,128)} %bitcast.88), channel_id=1, source_target_pairs={{0,64},{1,65},{2,66},{3,67},{4,68},{5,69},{6,70},{7,71},{8,72},{9,... | collective-permute-start | bytes 6291464 | tf_op jit(solution)/shard_map/ppermute | solution.py:105
  440.0 159.2 %collective-permute-start.8 = (f32[128,2048]{1,0:T(8,128)}, f32[128,2048]{1,0:T(8,128)}, u32[]{:S(2)}, u32[]{:S(2)}) collective-permute-start(f32[128,2048]{1,0:T(8,128)} %copy-done.9), channel_id=1, source_target_pairs={{0,128},{1,129},{2,130},{3,131},{4,132},{5,133},{6,134},{7,135},{8... | collective-permute-start | bytes 3145736 | tf_op jit(solution)/shard_map/ppermute | solution.py:105
  440.9 188.1 %collective-permute-start.14 = (f32[128,2048]{1,0:T(8,128)}, f32[128,2048]{1,0:T(8,128)}, u32[]{:S(2)}, u32[]{:S(2)}) collective-permute-start(f32[128,2048]{1,0:T(8,128)} %copy-done.10), channel_id=1, source_target_pairs={{0,64},{1,65},{2,66},{3,67},{4,68},{5,69},{6,70},{7,71},{8,72},{9,... | collective-permute-start | bytes 3145736 | tf_op jit(solution)/shard_map/ppermute | solution.py:105
  589.6 8.8 %copy-start.15 = (s32[3]{0:T(128)S(1)}, s32[3]{0:T(128)}, u32[]{:S(2)}) copy-start(s32[3]{0:T(128)} %constant.82.clone.1) | copy-start | bytes 40
  589.6 9.5 %copy-start.11 = (f32[512,2048]{1,0:T(8,128)S(1)}, f32[512,2048]{1,0:T(8,128)}, u32[]{:S(2)}) copy-start(f32[512,2048]{1,0:T(8,128)} %get-tuple-element.33) | copy-start | bytes 12582916
  592.7 40.0 %collective-permute-start.17 = (f32[512,512]{1,0:T(8,128)S(1)}, f32[512,512]{1,0:T(8,128)S(1)}, u32[]{:S(2)}, u32[]{:S(2)}) collective-permute-start(f32[512,512]{1,0:T(8,128)S(1)} %bitcast.81), channel_id=1, source_target_pairs={{4,0},{8,4},{12,8},{16,12},{20,16},{24,20},{28,24},{32,28},{36,32}... | collective-permute-start | bytes 3145736 | tf_op jit(solution)/shard_map/ppermute | solution.py:101
  594.6 101.2 %collective-permute-start.18 = (f32[512,512]{1,0:T(8,128)S(1)}, f32[512,512]{1,0:T(8,128)S(1)}, u32[]{:S(2)}, u32[]{:S(2)}) collective-permute-start(f32[512,512]{1,0:T(8,128)S(1)} %bitcast.80), channel_id=1, source_target_pairs={{8,0},{12,4},{16,8},{20,12},{24,16},{28,20},{32,24},{36,28},{40,32... | collective-permute-start | bytes 3145736 | tf_op jit(solution)/shard_map/ppermute | solution.py:101
  596.5 102.7 %collective-permute-start.19 = (f32[512,512]{1,0:T(8,128)S(1)}, f32[512,512]{1,0:T(8,128)S(1)}, u32[]{:S(2)}, u32[]{:S(2)}) collective-permute-start(f32[512,512]{1,0:T(8,128)S(1)} %bitcast.79), channel_id=1, source_target_pairs={{12,0},{16,4},{20,8},{24,12},{28,16},{32,20},{36,24},{40,28},{44,3... | collective-permute-start | bytes 3145736 | tf_op jit(solution)/shard_map/ppermute | solution.py:101
  (5 other events, 4.9 us)

commit v2 on v1

--- a/solution.py
+++ b/solution.py
@@ -13,7 +13,7 @@
 TN = (((0,), (0,)), ((), ()))
 
 
-def pair_kernel(pairs_ref, count_ref, q_ref, do_ref, norm_ref, delta_ref, qdoc_ref, qpos_ref,
+def pair_kernel(pairs_ref, q_ref, do_ref, norm_ref, delta_ref, qdoc_ref, qpos_ref,
                 kdoc_ref, kpos_ref, kv_ref, dq_ref, dkv_ref):
     dq_ref[...] = jnp.zeros(dq_ref.shape, jnp.float32)
     dkv_ref[...] = jnp.zeros(dkv_ref.shape, jnp.float32)
@@ -24,8 +24,12 @@
     scale = HEAD_DIM ** (-0.5)
 
     def body(i, carry):
-        qb = jnp.maximum(pairs_ref[2 * i], 0)
-        kb = jnp.maximum(pairs_ref[2 * i + 1], 0)
+        qb_raw = pairs_ref[2 * i]
+        kb_raw = pairs_ref[2 * i + 1]
+        pl.when((qb_raw >= 0) & (kb_raw >= 0))(lambda: one_pair(jnp.maximum(qb_raw, 0), jnp.maximum(kb_raw, 0)))
+        return carry
+
+    def one_pair(qb, kb):
         qrow = pl.multiple_of(qb * BLOCK, BLOCK)
         krow = pl.multiple_of(kb * BLOCK, BLOCK)
         qdoc = qdoc_ref[pl.ds(qb, 1), :]
@@ -56,12 +60,11 @@
                 dq_ref[pl.ds(qrow, BLOCK), cols] += part_query * scale
             dkv_ref[pl.ds(krow, BLOCK), pl.ds(g * HEAD_DIM, HEAD_DIM)] += dk * scale
             dkv_ref[pl.ds(krow, BLOCK), pl.ds(kv_features + g * HEAD_DIM, HEAD_DIM)] += dv
-        return carry
 
-    lax.fori_loop(0, count_ref[0], body, 0)
+    lax.fori_loop(0, pairs_ref.shape[0] // 2, body, 0)
 
 
-def run_pairs(pairs, count, queries, outgrads, norms, deltas, query_pos, keyval, key_pos, doc_bounds):
+def run_pairs(pairs, queries, outgrads, norms, deltas, query_pos, keyval, key_pos, doc_bounds):
     q_doc = doc_index(query_pos, doc_bounds)
     k_doc = doc_index(key_pos, doc_bounds)
     tokens, features = queries.shape
@@ -70,13 +73,12 @@
     smem = pltpu.MemorySpace.SMEM
     args = (
         pairs.reshape(-1).astype(jnp.int32),
-        jnp.reshape(count, (1,)).astype(jnp.int32),
         queries, outgrads, norms, deltas,
         q_doc, query_pos,
         k_doc.reshape(window, 1), key_pos.reshape(window, 1),
         keyval,
     )
-    specs = [pl.BlockSpec(memory_space=smem)] * 2 + [pl.BlockSpec(memory_space=vmem)] * 9
+    specs = [pl.BlockSpec(memory_space=smem)] + [pl.BlockSpec(memory_space=vmem)] * 9
     return pl.pallas_call(
         pair_kernel,
         out_shape=(
@@ -89,8 +91,6 @@
     )(*args)
 
 
-SHIP_SLOTS = 8
-ROUNDS = 2
 REACH = 3
 WIN_BLOCKS = 16
 
@@ -99,10 +99,6 @@
     length = lax.axis_size(axis)
     pairs = [(i, i + by) for i in range(length) if 0 <= i + by < length]
     return lax.ppermute(shard, axis, pairs)
-
-
-def swapped(shard, axis, apart):
-    return lax.ppermute(shard, axis, [(i, i ^ 1 << apart) for i in range(lax.axis_size(axis))])
 
 
 def doc_index(positions, doc_bounds):
@@ -134,49 +130,15 @@
     query_pos = (first_block + jnp.arange(own_blocks, dtype=jnp.int32))[:, None] * BLOCK + offsets
     window_first = first_block - REACH * own_blocks
     key_pos = (window_first * BLOCK + jnp.arange(WIN_BLOCKS * BLOCK, dtype=jnp.int32))
-    local_count = jnp.sum((local_pairs[:, 0] >= 0).astype(jnp.int32))
+    own_ship = ship_table[position]
+    ship_keys = own_ship[:, 1:]
+    ship_queries = jnp.where(ship_keys >= 0, own_ship[:, :1], -1)
+    ship_pairs = jnp.stack([ship_queries, ship_keys], axis=2).reshape(-1, 2)
+    pairs = jnp.concatenate([local_pairs, ship_pairs], axis=0)
     query_grads, keyval_grads = run_pairs(
-        local_pairs, local_count, query, grad_out, log_norm, delta, query_pos,
+        pairs, query, grad_out, log_norm, delta, query_pos,
         keyval_window, key_pos, doc_bounds,
     )
-    query_grads = query_grads.reshape(own_blocks, BLOCK, features)
-    keyval_grads = keyval_grads.reshape(WIN_BLOCKS, BLOCK, 2 * kv_features)
-    queries = query.reshape(own_blocks, BLOCK, features)
-    outgrads = grad_out.reshape(own_blocks, BLOCK, features)
-    window_blocks = keyval_window.reshape(WIN_BLOCKS, BLOCK, 2 * kv_features)
-    head_bits = lax.axis_size("head").bit_length() - 1
-    all_bits = lax.axis_size(("ctx", "head")).bit_length() - 1
-    slot_range = jnp.arange(SHIP_SLOTS, dtype=jnp.int32)
-    for section in range(ROUNDS):
-        my_row = ship_table[position, section]
-        bit = all_bits - 1 - section
-        partner = jnp.bitwise_xor(position, 1 << bit - head_bits)
-        far_row = ship_table[partner, section]
-        sent = jnp.maximum(my_row[0], 0)
-        my_slots = jnp.maximum(my_row[1:], 0)
-        sent_norms = lax.dynamic_slice_in_dim(log_norm, sent * BLOCK, BLOCK, 1)
-        sent_delta = lax.dynamic_slice_in_dim(delta, sent * BLOCK, BLOCK, 1)
-        got_norms, got_delta = swapped((sent_norms, sent_delta), ("ctx", "head"), bit)
-        got_query, got_grad, got_keyval = swapped(
-            (queries[sent], outgrads[sent], window_blocks[my_slots]), ("ctx", "head"), bit
-        )
-        far_count = jnp.sum((far_row[1:] >= 0).astype(jnp.int32))
-        far_pairs = jnp.stack([jnp.zeros_like(slot_range), slot_range], axis=1)
-        far_query_pos = ((partner * own_blocks + jnp.maximum(far_row[0], 0)) * BLOCK + offsets)[None]
-        far_first = (partner - REACH) * own_blocks
-        far_key_pos = (
-            (far_first + jnp.maximum(far_row[1:], 0))[:, None] * BLOCK + offsets
-        ).reshape(-1)
-        back_query, back_keyval = run_pairs(
-            far_pairs, far_count, got_query, got_grad, got_norms, got_delta, far_query_pos,
-            got_keyval.reshape(SHIP_SLOTS * BLOCK, 2 * kv_features), far_key_pos, doc_bounds,
-        )
-        returned = swapped(
-            (back_query, back_keyval.reshape(SHIP_SLOTS, BLOCK, 2 * kv_features)),
-            ("ctx", "head"), bit,
-        )
-        query_grads = query_grads.at[sent].add(returned[0])
-        keyval_grads = keyval_grads.at[my_slots].add(returned[1])
     segments = keyval_grads.reshape(REACH + 1, own_blocks * BLOCK, 2 * kv_features)
     own_grads = segments[REACH]
     for hop in range(1, REACH + 1):

time: 712 us -> 242 us (0.34); the launches traced: 701 us -> 242 us
  waiting for transfers between devices: 498 us -> 110 us
  Pallas kernels: 74.4 us -> 49.8 us
  local copies, waits for them, and re-layouts: 29.6 us -> 11.4 us
  other arithmetic: 23.1 us -> 8.65 us
  starting transfers between devices: 72.1 us -> 61.3 us
    ppermute x14 -> x0, waiting for transfers between devices: 423 us -> none  [swapped(): lax.ppermute(shard, axis, [(i, i ^ 1 << apart) for i in range(lax.axis_si...]
    ppermute x14 -> x0, starting transfers between devices: 56 us -> none  [swapped(): lax.ppermute(shard, axis, [(i, i ^ 1 << apart) for i in range(lax.axis_si...]
    ppermute x6, starting transfers between devices: 16.1 us -> 61.3 us  [shifted(): return lax.ppermute(shard, axis, pairs)]
    ppermute x6, waiting for transfers between devices: 74.5 us -> 110 us  [shifted(): return lax.ppermute(shard, axis, pairs)]
    pallas_call x3 -> x1, Pallas kernels: 74.4 us -> 49.8 us  [run_pairs(): pl.pallas_call(pair_kernel, out_shape=(jax.ShapeDtypeStruct((tokens, feat...]
    scatter-add x4 -> x0, other arithmetic: 13.8 us -> none  [the longest x2 9.69 us: local(): keyval_grads = keyval_grads.at[my_slots].add(returned[1])]
  transfers between devices with their start and end apart: 20 -> 6, of which waited for: 8 -> 5; matrix products, arithmetic and copies ran while one was open for 6% -> 4% of each run, Pallas kernels for 11% -> 0%
where the time goes in v2:
time: 242 us
  waiting for transfers between devices  110 us (45%)
  starting transfers between devices  61.3 us (25%)
  Pallas kernels  49.8 us (21%)
  local copies, waits for them, and re-layouts  11.4 us (5%)
  other arithmetic  8.65 us (4%)
    ppermute x6, waiting for transfers between devices, shifted(): return lax.ppermute(shard, axis, pairs)  110 us
    ppermute x6, starting transfers between devices, shifted(): return lax.ppermute(shard, axis, pairs)  61.3 us
    pallas_call x1, Pallas kernels, run_pairs(): pl.pallas_call(pair_kernel, out_shape=(jax.ShapeDtypeStruct((tokens, feat...  49.8 us
  transfers between devices with their start and end apart: 6, of which 5 were waited for; matrix products, arithmetic and copies ran while one was open for 4% of the time, Pallas kernels for 0%

profile of v2, /device:TPU:62, one launch (start us, length us, event | category | flops | bytes accessed | tf_op | source)
XLA Modules:
  0.0 241.9 jit_solution(3251945983154798444)
XLA Ops:
  0.7 1.8 constant_dynamic-update-slice_fusion.1
  2.5 1.7 constant_dynamic-update-slice_fusion
  4.2 1.9 collective-permute-start.2
  6.1 3.5 %collective-permute-start.1 = (bf16[512,512]{1,0:T(8,128)(2,1)}, bf16[512,512]{1,0:T(8,128)(2,1)}, u32[]{:S(2)}, u32[]{:S(2)}) collective-permute-start(bf16[512,512]{1,0:T(8,128)(2,1)} %constant_dynamic-update-slice_fusion), channel_id=1, source_target_pairs={{0,8},{4,12},{8,16},{12,20},{16,24},{20,28},{24,32},{28,36},{32,40... | collective-permute-start | bytes 1572872 | tf_op jit(solution)/shard_map/ppermute | solution.py:101
  9.6 4.5 %collective-permute-start = (bf16[512,512]{1,0:T(8,128)(2,1)}, bf16[512,512]{1,0:T(8,128)(2,1)}, u32[]{:S(2)}, u32[]{:S(2)}) collective-permute-start(bf16[512,512]{1,0:T(8,128)(2,1)} %constant_dynamic-update-slice_fusion), channel_id=1, source_target_pairs={{0,12},{4,16},{8,20},{12,24},{16,28},{20,32},{24,36},{28,40},{32,4... | collective-permute-start | bytes 1572872 | tf_op jit(solution)/shard_map/ppermute | solution.py:101
  14.1 0.7 slice.36
  14.9 0.1 copy.17
  15.0 0.1 slice_reduce_fusion
  15.4 0.8 add_add_fusion
  16.2 0.1 copy.18
  16.3 0.1 reshape.65.pairs_ref
  16.4 0.1 convert_reduce_fusion
  16.5 0.4 copy.19.kdoc_ref
  16.9 2.2 copy.29
  19.1 0.6 copy.28
  19.8 1.2 fusion
  21.0 0.1 copy.26.delta_ref
  21.1 0.1 convert_reduce_fusion.1
  21.3 1.7 collective-permute-done.2
  23.0 5.7 %collective-permute-done.1 = bf16[512,512]{1,0:T(8,128)(2,1)} collective-permute-done((bf16[512,512]{1,0:T(8,128)(2,1)}, bf16[512,512]{1,0:T(8,128)(2,1)}, u32[]{:S(2)}, u32[]{:S(2)}) %collective-permute-start.1) | collective-permute-done | bytes 524320 | tf_op jit(solution)/shard_map/ppermute | solution.py:101
  28.8 10.3 %collective-permute-done = bf16[512,512]{1,0:T(8,128)(2,1)} collective-permute-done((bf16[512,512]{1,0:T(8,128)(2,1)}, bf16[512,512]{1,0:T(8,128)(2,1)}, u32[]{:S(2)}, u32[]{:S(2)}) %collective-permute-start) | collective-permute-done | bytes 524320 | tf_op jit(solution)/shard_map/ppermute | solution.py:101
  39.0 3.0 %pad_maximum_fusion.kv_ref = bf16[2048,512]{1,0:T(8,128)(2,1)} fusion(bf16[512,512]{1,0:T(8,128)(2,1)} %constant_dynamic-update-slice_fusion, bf16[512,512]{1,0:T(8,128)(2,1)} %collective-permute-done.2, bf16[512,512]{1,0:T(8,128)(2,1)} %collective-permute-done.1, bf16[512,512]{1,0:T(8,128)(2,1)} %collective-permute-done), kind=kLoop, calls=%fused_computation.2 | loop fusion | flops 8388608 | bytes 4194304 | tf_op jit(solution)/shard_map/concatenate | solution.py:128
  42.0 49.8 %shard_map.112 = (f32[512,2048]{1,0:T(8,128)}, f32[2048,512]{1,0:T(8,128)}) custom-call(s32[120]{0:T(128)S(1)} %reshape.65.pairs_ref, bf16[512,2048]{1,0:T(8,128)(2,1)S(1)} %copy-done.1, bf16[512,2048]{1,0:T(8,128)(2,1)} %do_ref.1, f32[16,512]{1,0:T(8,128)S(1)} %copy-done.2, f32[16,512]{1,0:T(8,128)S(1)} %copy.26.delta_ref, s32[4,128]{1,0:T(4,128)S(1)} %bitcast.13, ...), custom_call_target="tpu_custom_call" | custom-call | tf_op jit(solution)/shard_map/pallas_call | solution.py:82
  91.8 2.3 fusion.2
  94.2 15.1 %collective-permute-start.3 = (f32[512,512]{1,0:T(8,128)S(1)}, f32[512,512]{1,0:T(8,128)S(1)}, u32[]{:S(2)}, u32[]{:S(2)}) collective-permute-start(f32[512,512]{1,0:T(8,128)S(1)} %get-tuple-element.7), channel_id=1, source_target_pairs={{4,0},{8,4},{12,8},{16,12},{20,16},{24,20},{28,24},{32,28},{36,32}... | collective-permute-start | bytes 3145736 | tf_op jit(solution)/shard_map/ppermute | solution.py:101
  109.3 17.0 %collective-permute-start.5 = (f32[512,512]{1,0:T(8,128)S(1)}, f32[512,512]{1,0:T(8,128)S(1)}, u32[]{:S(2)}, u32[]{:S(2)}) collective-permute-start(f32[512,512]{1,0:T(8,128)S(1)} %get-tuple-element.8), channel_id=1, source_target_pairs={{12,0},{16,4},{20,8},{24,12},{28,16},{32,20},{36,24},{40,28},{44,3... | collective-permute-start | bytes 3145736 | tf_op jit(solution)/shard_map/ppermute | solution.py:101
  126.2 19.4 %collective-permute-start.4 = (f32[512,512]{1,0:T(8,128)S(1)}, f32[512,512]{1,0:T(8,128)S(1)}, u32[]{:S(2)}, u32[]{:S(2)}) collective-permute-start(f32[512,512]{1,0:T(8,128)S(1)} %get-tuple-element.9), channel_id=1, source_target_pairs={{8,0},{12,4},{16,8},{20,12},{24,16},{28,20},{32,24},{36,28},{40,32... | collective-permute-start | bytes 3145736 | tf_op jit(solution)/shard_map/ppermute | solution.py:101
  145.6 1.6 convert_element_type.13
  147.3 59.8 %collective-permute-done.5 = f32[512,512]{1,0:T(8,128)S(1)} collective-permute-done((f32[512,512]{1,0:T(8,128)S(1)}, f32[512,512]{1,0:T(8,128)S(1)}, u32[]{:S(2)}, u32[]{:S(2)}) %collective-permute-start.5) | collective-permute-done | bytes 1048608 | tf_op jit(solution)/shard_map/ppermute | solution.py:101
  207.0 32.4 %collective-permute-done.4 = f32[512,512]{1,0:T(8,128)S(1)} collective-permute-done((f32[512,512]{1,0:T(8,128)S(1)}, f32[512,512]{1,0:T(8,128)S(1)}, u32[]{:S(2)}, u32[]{:S(2)}) %collective-permute-start.4) | collective-permute-done | bytes 1048608 | tf_op jit(solution)/shard_map/ppermute | solution.py:101
  239.4 1.7 add_convert_fusion
  241.0 0.8 fusion.3
  (19 shorter events, 0.5 us)
Async XLA Ops:
  0.6 14.2 %copy-start = (s32[64,2,9]{0,1,2:T(2,128)S(1)}, s32[64,2,9]{0,1,2:T(2,128)}, u32[]{:S(2)}) copy-start(s32[64,2,9]{0,1,2:T(2,128)} %param.17) | copy-start | bytes 13828
  0.6 18.5 %copy-start.3 = (bf16[512,2048]{1,0:T(8,128)(2,1)S(1)}, bf16[512,2048]{1,0:T(8,128)(2,1)}, u32[]{:S(2)}) copy-start(bf16[512,2048]{1,0:T(8,128)(2,1)} %do_ref.1) | copy-start | bytes 6291460
  4.2 18.8 %collective-permute-start.2 = (bf16[512,512]{1,0:T(8,128)(2,1)}, bf16[512,512]{1,0:T(8,128)(2,1)}, u32[]{:S(2)}, u32[]{:S(2)}) collective-permute-start(bf16[512,512]{1,0:T(8,128)(2,1)} %constant_dynamic-update-slice_fusion), channel_id=1, source_target_pairs={{0,4},{4,8},{8,12},{12,16},{16,20},{20,24},{24,28},{28,32},{32,36}... | collective-permute-start | bytes 1572872 | tf_op jit(solution)/shard_map/ppermute | solution.py:101
  6.1 22.6 %collective-permute-start.1 = (bf16[512,512]{1,0:T(8,128)(2,1)}, bf16[512,512]{1,0:T(8,128)(2,1)}, u32[]{:S(2)}, u32[]{:S(2)}) collective-permute-start(bf16[512,512]{1,0:T(8,128)(2,1)} %constant_dynamic-update-slice_fusion), channel_id=1, source_target_pairs={{0,8},{4,12},{8,16},{12,20},{16,24},{20,28},{24,32},{28,36},{32,40... | collective-permute-start | bytes 1572872 | tf_op jit(solution)/shard_map/ppermute | solution.py:101
  9.6 29.4 %collective-permute-start = (bf16[512,512]{1,0:T(8,128)(2,1)}, bf16[512,512]{1,0:T(8,128)(2,1)}, u32[]{:S(2)}, u32[]{:S(2)}) collective-permute-start(bf16[512,512]{1,0:T(8,128)(2,1)} %constant_dynamic-update-slice_fusion), channel_id=1, source_target_pairs={{0,12},{4,16},{8,20},{12,24},{16,28},{20,32},{24,36},{28,40},{32,4... | collective-permute-start | bytes 1572872 | tf_op jit(solution)/shard_map/ppermute | solution.py:101
  19.8 22.2 %copy-start.1 = (bf16[512,2048]{1,0:T(8,128)(2,1)S(1)}, bf16[512,2048]{1,0:T(8,128)(2,1)}, u32[]{:S(2)}) copy-start(bf16[512,2048]{1,0:T(8,128)(2,1)} %q_ref.1) | copy-start | bytes 6291460
  19.8 22.2 %copy-start.2 = (f32[16,512]{1,0:T(8,128)S(1)}, f32[16,512]{1,0:T(8,128)}, u32[]{:S(2)}) copy-start(f32[16,512]{1,0:T(8,128)} %norm_ref.1) | copy-start | bytes 98308
  91.8 53.8 %copy-start.4 = (f32[512,2048]{1,0:T(8,128)S(1)}, f32[512,2048]{1,0:T(8,128)}, u32[]{:S(2)}) copy-start(f32[512,2048]{1,0:T(8,128)} %get-tuple-element.5) | copy-start | bytes 12582916
  94.2 53.1 %collective-permute-start.3 = (f32[512,512]{1,0:T(8,128)S(1)}, f32[512,512]{1,0:T(8,128)S(1)}, u32[]{:S(2)}, u32[]{:S(2)}) collective-permute-start(f32[512,512]{1,0:T(8,128)S(1)} %get-tuple-element.7), channel_id=1, source_target_pairs={{4,0},{8,4},{12,8},{16,12},{20,16},{24,20},{28,24},{32,28},{36,32}... | collective-permute-start | bytes 3145736 | tf_op jit(solution)/shard_map/ppermute | solution.py:101
  109.3 97.8 %collective-permute-start.5 = (f32[512,512]{1,0:T(8,128)S(1)}, f32[512,512]{1,0:T(8,128)S(1)}, u32[]{:S(2)}, u32[]{:S(2)}) collective-permute-start(f32[512,512]{1,0:T(8,128)S(1)} %get-tuple-element.8), channel_id=1, source_target_pairs={{12,0},{16,4},{20,8},{24,12},{28,16},{32,20},{36,24},{40,28},{44,3... | collective-permute-start | bytes 3145736 | tf_op jit(solution)/shard_map/ppermute | solution.py:101
  126.2 113.2 %collective-permute-start.4 = (f32[512,512]{1,0:T(8,128)S(1)}, f32[512,512]{1,0:T(8,128)S(1)}, u32[]{:S(2)}, u32[]{:S(2)}) collective-permute-start(f32[512,512]{1,0:T(8,128)S(1)} %get-tuple-element.9), channel_id=1, source_target_pairs={{8,0},{12,4},{16,8},{20,12},{24,16},{28,20},{32,24},{36,28},{40,32... | collective-permute-start | bytes 3145736 | tf_op jit(solution)/shard_map/ppermute | solution.py:101

commit v3 on v2

--- a/solution.py
+++ b/solution.py
@@ -17,7 +17,7 @@
                 kdoc_ref, kpos_ref, kv_ref, dq_ref, dkv_ref):
     dq_ref[...] = jnp.zeros(dq_ref.shape, jnp.float32)
     dkv_ref[...] = jnp.zeros(dkv_ref.shape, jnp.float32)
-    heads = norm_ref.shape[0]
+    heads = norm_ref.shape[1] // BLOCK
     kv_features = kv_ref.shape[1] // 2
     kv_heads = kv_features // HEAD_DIM
     group = heads // kv_heads
@@ -37,27 +37,26 @@
         kdoc = kdoc_ref[pl.ds(krow, BLOCK), :]
         kpos = kpos_ref[pl.ds(krow, BLOCK), :]
         allowed = (kdoc == qdoc) & (kpos <= qpos)
+        wide_allowed = jnp.concatenate([allowed] * group, axis=1)
         for g in range(kv_heads):
             k = kv_ref[pl.ds(krow, BLOCK), pl.ds(g * HEAD_DIM, HEAD_DIM)]
             v = kv_ref[pl.ds(krow, BLOCK), pl.ds(kv_features + g * HEAD_DIM, HEAD_DIM)]
-            dk = jnp.zeros((BLOCK, HEAD_DIM), jnp.float32)
-            dv = jnp.zeros((BLOCK, HEAD_DIM), jnp.float32)
-            for j in range(group):
-                h = g * group + j
-                cols = pl.ds(h * HEAD_DIM, HEAD_DIM)
-                q = q_ref[pl.ds(qrow, BLOCK), cols]
-                do = do_ref[pl.ds(qrow, BLOCK), cols]
-                norm = norm_ref[pl.ds(h, 1), pl.ds(qrow, BLOCK)]
-                dl = delta_ref[pl.ds(h, 1), pl.ds(qrow, BLOCK)]
-                scores = lax.dot_general(k, q, NT, preferred_element_type=jnp.float32) * scale
-                weights = jnp.where(allowed, jnp.exp(scores - norm), 0.0)
-                weight_grads = lax.dot_general(v, do, NT, preferred_element_type=jnp.float32)
-                score_grads = (weights * (weight_grads - dl)).astype(jnp.bfloat16)
-                weights_low = weights.astype(jnp.bfloat16)
-                dv = dv + jnp.dot(weights_low, do, preferred_element_type=jnp.float32)
-                dk = dk + jnp.dot(score_grads, q, preferred_element_type=jnp.float32)
-                part_query = lax.dot_general(score_grads, k, TN, preferred_element_type=jnp.float32)
-                dq_ref[pl.ds(qrow, BLOCK), cols] += part_query * scale
+            head_cols = [pl.ds((g * group + j) * HEAD_DIM, HEAD_DIM) for j in range(group)]
+            q = jnp.concatenate([q_ref[pl.ds(qrow, BLOCK), c] for c in head_cols], axis=0)
+            do = jnp.concatenate([do_ref[pl.ds(qrow, BLOCK), c] for c in head_cols], axis=0)
+            group_cols = pl.ds(g * group * BLOCK, group * BLOCK)
+            norm = norm_ref[pl.ds(qb, 1), group_cols]
+            dl = delta_ref[pl.ds(qb, 1), group_cols]
+            scores = lax.dot_general(k, q, NT, preferred_element_type=jnp.float32) * scale
+            weights = jnp.where(wide_allowed, jnp.exp(scores - norm), 0.0)
+            weight_grads = lax.dot_general(v, do, NT, preferred_element_type=jnp.float32)
+            score_grads = (weights * (weight_grads - dl)).astype(jnp.bfloat16)
+            weights_low = weights.astype(jnp.bfloat16)
+            dv = jnp.dot(weights_low, do, preferred_element_type=jnp.float32)
+            dk = jnp.dot(score_grads, q, preferred_element_type=jnp.float32)
+            part_query = lax.dot_general(score_grads, k, TN, preferred_element_type=jnp.float32) * scale
+            for j, c in enumerate(head_cols):
+                dq_ref[pl.ds(qrow, BLOCK), c] += part_query[j * BLOCK:(j + 1) * BLOCK]
             dkv_ref[pl.ds(krow, BLOCK), pl.ds(g * HEAD_DIM, HEAD_DIM)] += dk * scale
             dkv_ref[pl.ds(krow, BLOCK), pl.ds(kv_features + g * HEAD_DIM, HEAD_DIM)] += dv
 
@@ -69,6 +68,10 @@
     k_doc = doc_index(key_pos, doc_bounds)
     tokens, features = queries.shape
     window, both = keyval.shape
+    heads = norms.shape[0]
+    blocks = tokens // BLOCK
+    norms = norms.reshape(heads, blocks, BLOCK).transpose(1, 0, 2).reshape(blocks, heads * BLOCK)
+    deltas = deltas.reshape(heads, blocks, BLOCK).transpose(1, 0, 2).reshape(blocks, heads * BLOCK)
     vmem = pltpu.MemorySpace.VMEM
     smem = pltpu.MemorySpace.SMEM
     args = (

time: 242 us -> 155 us (0.64)
  Pallas kernels: 49.8 us -> 18.9 us
  waiting for transfers between devices: 110 us -> 80.8 us
  starting transfers between devices: 61.3 us -> 33.1 us
    pallas_call x1, Pallas kernels: 49.8 us -> 18.9 us  [run_pairs(): pl.pallas_call(pair_kernel, out_shape=(jax.ShapeDtypeStruct((tokens, feat...]
    ppermute x6, waiting for transfers between devices: 110 us -> 80.8 us  [shifted(): return lax.ppermute(shard, axis, pairs)]
    ppermute x6, starting transfers between devices: 61.3 us -> 33.1 us  [shifted(): return lax.ppermute(shard, axis, pairs)]
  transfers between devices with their start and end apart: 6 -> 6, of which waited for: 5 -> 5; matrix products, arithmetic and copies ran while one was open for 4% -> 6% of each run, Pallas kernels for 0% -> 0%
where the time goes in v3:
time: 155 us; the launch traced here: 154 us
  waiting for transfers between devices  80.8 us (52%)
  starting transfers between devices  33.1 us (21%)
  Pallas kernels  18.9 us (12%)
  local copies, waits for them, and re-layouts  12.1 us (8%)
  other arithmetic  8.61 us (6%)
    ppermute x6, waiting for transfers between devices, shifted(): return lax.ppermute(shard, axis, pairs)  80.8 us
    ppermute x6, starting transfers between devices, shifted(): return lax.ppermute(shard, axis, pairs)  33.1 us
    pallas_call x1, Pallas kernels, run_pairs(): pl.pallas_call(pair_kernel, out_shape=(jax.ShapeDtypeStruct((tokens, feat...  18.9 us
    unnamed x13, local copies, waits for them, and re-layouts  4.7 us
  transfers between devices with their start and end apart: 6, of which 5 were waited for; matrix products, arithmetic and copies ran while one was open for 6% of the time, Pallas kernels for 0%

profile of v3, /device:TPU:62, one launch (start us, length us, event | category | flops | bytes accessed | tf_op | source)
XLA Modules:
  0.0 154.3 jit_solution(13389879278823058548)
XLA Ops:
  0.7 1.8 %constant_dynamic-update-slice_fusion.1 = bf16[512,512]{1,0:T(8,128)(2,1)} fusion(bf16[512,256]{1,0:T(8,128)(2,1)} %param.10), kind=kLoop, calls=%fused_computation.11 | loop fusion | bytes 524288
  2.5 1.7 %constant_dynamic-update-slice_fusion = bf16[512,512]{1,0:T(8,128)(2,1)} fusion(bf16[512,512]{1,0:T(8,128)(2,1)} %constant_dynamic-update-slice_fusion.1, bf16[512,256]{1,0:T(8,128)(2,1)} %param.11), kind=kLoop, calls=%fused_computation.10 | loop fusion | bytes 524288 | tf_op jit(solution)/shard_map/concatenate | solution.py:127
  4.2 1.9 %collective-permute-start.2 = (bf16[512,512]{1,0:T(8,128)(2,1)}, bf16[512,512]{1,0:T(8,128)(2,1)}, u32[]{:S(2)}, u32[]{:S(2)}) collective-permute-start(bf16[512,512]{1,0:T(8,128)(2,1)} %constant_dynamic-update-slice_fusion), channel_id=1, source_target_pairs={{0,4},{4,8},{8,12},{12,16},{16,20},{20,24},{24,28},{28,32},{32,36}... | collective-permute-start | bytes 1572872 | tf_op jit(solution)/shard_map/ppermute | solution.py:104
  6.1 3.5 %collective-permute-start.1 = (bf16[512,512]{1,0:T(8,128)(2,1)}, bf16[512,512]{1,0:T(8,128)(2,1)}, u32[]{:S(2)}, u32[]{:S(2)}) collective-permute-start(bf16[512,512]{1,0:T(8,128)(2,1)} %constant_dynamic-update-slice_fusion), channel_id=1, source_target_pairs={{0,8},{4,12},{8,16},{12,20},{16,24},{20,28},{24,32},{28,36},{32,40... | collective-permute-start | bytes 1572872 | tf_op jit(solution)/shard_map/ppermute | solution.py:104
  9.6 4.5 %collective-permute-start = (bf16[512,512]{1,0:T(8,128)(2,1)}, bf16[512,512]{1,0:T(8,128)(2,1)}, u32[]{:S(2)}, u32[]{:S(2)}) collective-permute-start(bf16[512,512]{1,0:T(8,128)(2,1)} %constant_dynamic-update-slice_fusion), channel_id=1, source_target_pairs={{0,12},{4,16},{8,20},{12,24},{16,28},{20,32},{24,36},{28,40},{32,4... | collective-permute-start | bytes 1572872 | tf_op jit(solution)/shard_map/ppermute | solution.py:104
  14.1 0.7 slice.36
  14.8 0.8 constant_dynamic-slice_fusion
  15.7 0.1 slice_reduce_fusion
  16.1 0.8 add_add_fusion
  16.8 0.1 copy.20
  17.0 0.1 reshape.77.pairs_ref
  17.1 0.1 convert_reduce_fusion
  17.3 0.4 copy.22.kdoc_ref
  17.6 2.2 %copy.35 = bf16[64,8,16,128]{3,2,1,0:T(8,128)(2,1)S(1)} copy(bf16[64,8,16,128]{3,1,2,0:T(8,128)(2,1)} %bitcast.34) | data formatting | bytes 4194304
  19.8 0.6 copy.34
  20.5 1.2 fusion
  21.7 0.1 copy.31
  21.8 0.1 convert_reduce_fusion.1
  22.0 1.0 collective-permute-done.2
  23.0 5.7 %collective-permute-done.1 = bf16[512,512]{1,0:T(8,128)(2,1)} collective-permute-done((bf16[512,512]{1,0:T(8,128)(2,1)}, bf16[512,512]{1,0:T(8,128)(2,1)}, u32[]{:S(2)}, u32[]{:S(2)}) %collective-permute-start.1) | collective-permute-done | bytes 524320 | tf_op jit(solution)/shard_map/ppermute | solution.py:104
  28.7 10.3 %collective-permute-done = bf16[512,512]{1,0:T(8,128)(2,1)} collective-permute-done((bf16[512,512]{1,0:T(8,128)(2,1)}, bf16[512,512]{1,0:T(8,128)(2,1)}, u32[]{:S(2)}, u32[]{:S(2)}) %collective-permute-start) | collective-permute-done | bytes 524320 | tf_op jit(solution)/shard_map/ppermute | solution.py:104
  39.0 3.0 %pad_maximum_fusion.kv_ref = bf16[2048,512]{1,0:T(8,128)(2,1)} fusion(bf16[512,512]{1,0:T(8,128)(2,1)} %constant_dynamic-update-slice_fusion, bf16[512,512]{1,0:T(8,128)(2,1)} %collective-permute-done.2, bf16[512,512]{1,0:T(8,128)(2,1)} %collective-permute-done.1, bf16[512,512]{1,0:T(8,128)(2,1)} %collective-permute-done), kind=kLoop, calls=%fused_computation.2 | loop fusion | flops 8388608 | bytes 4194304 | tf_op jit(solution)/shard_map/concatenate | solution.py:131
  42.0 18.9 %shard_map.112 = (f32[512,2048]{1,0:T(8,128)}, f32[2048,512]{1,0:T(8,128)}) custom-call(s32[120]{0:T(128)S(1)} %reshape.77.pairs_ref, bf16[512,2048]{1,0:T(8,128)(2,1)S(1)} %copy-done.1, bf16[512,2048]{1,0:T(8,128)(2,1)} %do_ref.1, f32[4,2048]{1,0:T(4,128)S(1)} %bitcast.29, f32[4,2048]{1,0:T(4,128)S(1)} %bitcast.28, s32[4,128]{1,0:T(4,128)S(1)} %bitcast.30, ...), custom_call_target="tpu_custom_call" | custom-call | tf_op jit(solution)/shard_map/pallas_call | solution.py:85
  60.8 2.3 %fusion.2 = (f32[512,512]{1,0:T(8,128)S(1)}, f32[512,512]{1,0:T(8,128)S(1)}, f32[512,512]{1,0:T(8,128)S(1)}) fusion(f32[2048,512]{1,0:T(8,128)} %get-tuple-element.6), kind=kLoop, calls=%fused_computation.19 | loop fusion | bytes 6291456 | tf_op jit(solution)/shard_map/slice | solution.py:148
  63.2 4.7 %collective-permute-start.3 = (f32[512,512]{1,0:T(8,128)S(1)}, f32[512,512]{1,0:T(8,128)S(1)}, u32[]{:S(2)}, u32[]{:S(2)}) collective-permute-start(f32[512,512]{1,0:T(8,128)S(1)} %get-tuple-element.7), channel_id=1, source_target_pairs={{4,0},{8,4},{12,8},{16,12},{20,16},{24,20},{28,24},{32,28},{36,32}... | collective-permute-start | bytes 3145736 | tf_op jit(solution)/shard_map/ppermute | solution.py:104
  67.9 11.8 %collective-permute-start.5 = (f32[512,512]{1,0:T(8,128)S(1)}, f32[512,512]{1,0:T(8,128)S(1)}, u32[]{:S(2)}, u32[]{:S(2)}) collective-permute-start(f32[512,512]{1,0:T(8,128)S(1)} %get-tuple-element.8), channel_id=1, source_target_pairs={{12,0},{16,4},{20,8},{24,12},{28,16},{32,20},{36,24},{40,28},{44,3... | collective-permute-start | bytes 3145736 | tf_op jit(solution)/shard_map/ppermute | solution.py:104
  79.7 6.7 %collective-permute-start.4 = (f32[512,512]{1,0:T(8,128)S(1)}, f32[512,512]{1,0:T(8,128)S(1)}, u32[]{:S(2)}, u32[]{:S(2)}) collective-permute-start(f32[512,512]{1,0:T(8,128)S(1)} %get-tuple-element.9), channel_id=1, source_target_pairs={{8,0},{12,4},{16,8},{20,12},{24,16},{28,20},{32,24},{36,28},{40,32... | collective-permute-start | bytes 3145736 | tf_op jit(solution)/shard_map/ppermute | solution.py:104
  86.5 1.6 %convert_element_type.13 = bf16[512,2048]{1,0:T(8,128)(2,1)} convert(f32[512,2048]{1,0:T(8,128)S(1)} %copy-done.3) | non-fusion elementwise | flops 1048576 | bytes 6291456 | tf_op jit(solution)/shard_map/convert_element_type | solution.py:149
  88.1 31.8 %collective-permute-done.5 = f32[512,512]{1,0:T(8,128)S(1)} collective-permute-done((f32[512,512]{1,0:T(8,128)S(1)}, f32[512,512]{1,0:T(8,128)S(1)}, u32[]{:S(2)}, u32[]{:S(2)}) %collective-permute-start.5) | collective-permute-done | bytes 1048608 | tf_op jit(solution)/shard_map/ppermute | solution.py:104
  119.9 32.0 %collective-permute-done.4 = f32[512,512]{1,0:T(8,128)S(1)} collective-permute-done((f32[512,512]{1,0:T(8,128)S(1)}, f32[512,512]{1,0:T(8,128)S(1)}, u32[]{:S(2)}, u32[]{:S(2)}) %collective-permute-start.4) | collective-permute-done | bytes 1048608 | tf_op jit(solution)/shard_map/ppermute | solution.py:104
  151.9 1.6 %add_convert_fusion = bf16[512,512]{1,0:T(8,128)(2,1)S(1)} fusion(f32[512,512]{1,0:T(8,128)S(1)} %collective-permute-done.5, f32[512,512]{1,0:T(8,128)S(1)} %collective-permute-done.4, f32[512,512]{1,0:T(8,128)S(1)} %collective-permute-done.3, f32[2048,512]{1,0:T(8,128)} %get-tuple-element.6), kind=kLoop, calls=%fused_computation.3 | loop fusion | flops 1048576 | bytes 4718592 | tf_op jit(solution)/shard_map/convert.1
  153.5 0.8 fusion.3
  (19 shorter events, 0.5 us)
Async XLA Ops:
  0.6 16.5 %copy-start = (f32[16,512]{1,0:T(8,128)S(1)}, f32[16,512]{1,0:T(8,128)}, u32[]{:S(2)}) copy-start(f32[16,512]{1,0:T(8,128)} %param.14) | copy-start | bytes 98308
  0.6 19.2 %copy-start.2 = (bf16[512,2048]{1,0:T(8,128)(2,1)S(1)}, bf16[512,2048]{1,0:T(8,128)(2,1)}, u32[]{:S(2)}) copy-start(bf16[512,2048]{1,0:T(8,128)(2,1)} %do_ref.1) | copy-start | bytes 6291460
  4.2 18.8 %collective-permute-start.2 = (bf16[512,512]{1,0:T(8,128)(2,1)}, bf16[512,512]{1,0:T(8,128)(2,1)}, u32[]{:S(2)}, u32[]{:S(2)}) collective-permute-start(bf16[512,512]{1,0:T(8,128)(2,1)} %constant_dynamic-update-slice_fusion), channel_id=1, source_target_pairs={{0,4},{4,8},{8,12},{12,16},{16,20},{20,24},{24,28},{28,32},{32,36}... | collective-permute-start | bytes 1572872 | tf_op jit(solution)/shard_map/ppermute | solution.py:104
  6.1 22.6 %collective-permute-start.1 = (bf16[512,512]{1,0:T(8,128)(2,1)}, bf16[512,512]{1,0:T(8,128)(2,1)}, u32[]{:S(2)}, u32[]{:S(2)}) collective-permute-start(bf16[512,512]{1,0:T(8,128)(2,1)} %constant_dynamic-update-slice_fusion), channel_id=1, source_target_pairs={{0,8},{4,12},{8,16},{12,20},{16,24},{20,28},{24,32},{28,36},{32,40... | collective-permute-start | bytes 1572872 | tf_op jit(solution)/shard_map/ppermute | solution.py:104
  9.6 29.4 %collective-permute-start = (bf16[512,512]{1,0:T(8,128)(2,1)}, bf16[512,512]{1,0:T(8,128)(2,1)}, u32[]{:S(2)}, u32[]{:S(2)}) collective-permute-start(bf16[512,512]{1,0:T(8,128)(2,1)} %constant_dynamic-update-slice_fusion), channel_id=1, source_target_pairs={{0,12},{4,16},{8,20},{12,24},{16,28},{20,32},{24,36},{28,40},{32,4... | collective-permute-start | bytes 1572872 | tf_op jit(solution)/shard_map/ppermute | solution.py:104
  20.5 21.5 %copy-start.1 = (bf16[512,2048]{1,0:T(8,128)(2,1)S(1)}, bf16[512,2048]{1,0:T(8,128)(2,1)}, u32[]{:S(2)}) copy-start(bf16[512,2048]{1,0:T(8,128)(2,1)} %q_ref.1) | copy-start | bytes 6291460
  60.8 25.6 %copy-start.3 = (f32[512,2048]{1,0:T(8,128)S(1)}, f32[512,2048]{1,0:T(8,128)}, u32[]{:S(2)}) copy-start(f32[512,2048]{1,0:T(8,128)} %get-tuple-element.5) | copy-start | bytes 12582916
  63.2 24.9 %collective-permute-start.3 = (f32[512,512]{1,0:T(8,128)S(1)}, f32[512,512]{1,0:T(8,128)S(1)}, u32[]{:S(2)}, u32[]{:S(2)}) collective-permute-start(f32[512,512]{1,0:T(8,128)S(1)} %get-tuple-element.7), channel_id=1, source_target_pairs={{4,0},{8,4},{12,8},{16,12},{20,16},{24,20},{28,24},{32,28},{36,32}... | collective-permute-start | bytes 3145736 | tf_op jit(solution)/shard_map/ppermute | solution.py:104
  67.9 52.0 %collective-permute-start.5 = (f32[512,512]{1,0:T(8,128)S(1)}, f32[512,512]{1,0:T(8,128)S(1)}, u32[]{:S(2)}, u32[]{:S(2)}) collective-permute-start(f32[512,512]{1,0:T(8,128)S(1)} %get-tuple-element.8), channel_id=1, source_target_pairs={{12,0},{16,4},{20,8},{24,12},{28,16},{32,20},{36,24},{40,28},{44,3... | collective-permute-start | bytes 3145736 | tf_op jit(solution)/shard_map/ppermute | solution.py:104
  79.7 72.1 %collective-permute-start.4 = (f32[512,512]{1,0:T(8,128)S(1)}, f32[512,512]{1,0:T(8,128)S(1)}, u32[]{:S(2)}, u32[]{:S(2)}) collective-permute-start(f32[512,512]{1,0:T(8,128)S(1)} %get-tuple-element.9), channel_id=1, source_target_pairs={{8,0},{12,4},{16,8},{20,12},{24,16},{28,20},{32,24},{36,28},{40,32... | collective-permute-start | bytes 3145736 | tf_op jit(solution)/shard_map/ppermute | solution.py:104

commit v4 on v3

--- a/solution.py
+++ b/solution.py
@@ -95,6 +95,7 @@
 
 
 REACH = 3
+DOC_BLOCKS = 10
 WIN_BLOCKS = 16
 
 
@@ -125,9 +126,15 @@
         preferred_element_type=jnp.float32,
     )
     own_keyval = jnp.concatenate([key, value], axis=1)
+    first_used = min(max(REACH * own_blocks - DOC_BLOCKS, 0), own_blocks) * BLOCK
     pieces = []
     for hop in range(REACH, 0, -1):
-        pieces.append(shifted(own_keyval, "ctx", hop))
+        if hop == REACH:
+            tail = shifted(own_keyval[first_used:], "ctx", hop)
+            pieces.append(jnp.zeros((first_used, 2 * kv_features), own_keyval.dtype))
+            pieces.append(tail)
+        else:
+            pieces.append(shifted(own_keyval, "ctx", hop))
     keyval_window = jnp.concatenate(pieces + [own_keyval], axis=0)
     first_block = position * own_blocks
     query_pos = (first_block + jnp.arange(own_blocks, dtype=jnp.int32))[:, None] * BLOCK + offsets
@@ -144,8 +151,10 @@
     )
     segments = keyval_grads.reshape(REACH + 1, own_blocks * BLOCK, 2 * kv_features)
     own_grads = segments[REACH]
-    for hop in range(1, REACH + 1):
+    for hop in range(1, REACH):
         own_grads = own_grads + shifted(segments[REACH - hop], "ctx", -hop)
+    far_grads = shifted(segments[0][first_used:], "ctx", -REACH)
+    own_grads = own_grads.at[first_used:].add(far_grads)
     grad_query = query_grads.reshape(tokens, features).astype(jnp.bfloat16)
     grad_key = own_grads[:, :kv_features].astype(jnp.bfloat16)
     grad_value = own_grads[:, kv_features:].astype(jnp.bfloat16)

time: 155 us -> 129 us (0.83)
  the two profiles are of different devices: /device:TPU:62 before, /device:TPU:10 now
where the time goes in v4:
time: 129 us; the launch traced here: 128 us
  waiting for transfers between devices  62.3 us (48%)
  Pallas kernels  24.8 us (19%)
  local copies, waits for them, and re-layouts  19.6 us (15%)
  starting transfers between devices  15.5 us (12%)
  other arithmetic  5.11 us (4%)
    ppermute x6, waiting for transfers between devices, shifted(): return lax.ppermute(shard, axis, pairs)  62.3 us
    pallas_call x1, Pallas kernels, run_pairs(): pl.pallas_call(pair_kernel, out_shape=(jax.ShapeDtypeStruct((tokens, feat...  24.8 us
    ppermute x6, starting transfers between devices, shifted(): return lax.ppermute(shard, axis, pairs)  15.5 us
    unnamed x28, local copies, waits for them, and re-layouts  9.89 us
  transfers between devices with their start and end apart: 6, of which 3 were waited for; matrix products, arithmetic and copies ran while one was open for 12% of the time, Pallas kernels for 0%

profile of v4, /device:TPU:10, one launch (start us, length us, event | category | flops | bytes accessed | tf_op | source)
XLA Modules:
  0.0 128.3 jit_solution(5071871385262950063)
XLA Ops:
  0.6 1.7 %constant_dynamic-update-slice_fusion.1 = bf16[512,512]{1,0:T(8,128)(2,1)} fusion(bf16[512,256]{1,0:T(8,128)(2,1)} %param.12), kind=kLoop, calls=%fused_computation.12 | loop fusion | bytes 524288
  2.3 1.7 %constant_dynamic-update-slice_fusion = bf16[512,512]{1,0:T(8,128)(2,1)} fusion(bf16[512,512]{1,0:T(8,128)(2,1)} %constant_dynamic-update-slice_fusion.1, bf16[512,256]{1,0:T(8,128)(2,1)} %param.13), kind=kLoop, calls=%fused_computation.11 | loop fusion | bytes 524288 | tf_op jit(solution)/shard_map/concatenate | solution.py:128
  4.0 1.9 %collective-permute-start.2 = (bf16[512,512]{1,0:T(8,128)(2,1)}, bf16[512,512]{1,0:T(8,128)(2,1)}, u32[]{:S(2)}, u32[]{:S(2)}) collective-permute-start(bf16[512,512]{1,0:T(8,128)(2,1)} %constant_dynamic-update-slice_fusion), channel_id=1, source_target_pairs={{0,4},{4,8},{8,12},{12,16},{16,20},{20,24},{24,28},{28,32},{32,36}... | collective-permute-start | bytes 1572872 | tf_op jit(solution)/shard_map/ppermute | solution.py:105
  5.9 3.5 %collective-permute-start.1 = (bf16[512,512]{1,0:T(8,128)(2,1)}, bf16[512,512]{1,0:T(8,128)(2,1)}, u32[]{:S(2)}, u32[]{:S(2)}) collective-permute-start(bf16[512,512]{1,0:T(8,128)(2,1)} %constant_dynamic-update-slice_fusion), channel_id=1, source_target_pairs={{0,8},{4,12},{8,16},{12,20},{16,24},{20,28},{24,32},{28,36},{32,40... | collective-permute-start | bytes 1572872 | tf_op jit(solution)/shard_map/ppermute | solution.py:105
  9.4 1.7 %slice.70 = bf16[256,512]{1,0:T(8,128)(2,1)} slice(bf16[512,512]{1,0:T(8,128)(2,1)} %constant_dynamic-update-slice_fusion), slice={[256:512], [0:512]} | slice | bytes 524288 | tf_op jit(solution)/shard_map/slice | solution.py:133
  11.1 4.9 %collective-permute-start = (bf16[256,512]{1,0:T(8,128)(2,1)}, bf16[256,512]{1,0:T(8,128)(2,1)}, u32[]{:S(2)}, u32[]{:S(2)}) collective-permute-start(bf16[256,512]{1,0:T(8,128)(2,1)} %slice.70), channel_id=1, source_target_pairs={{0,12},{4,16},{8,20},{12,24},{16,28},{20,32},{24,36},{28,40},{32,4... | collective-permute-start | bytes 786440 | tf_op jit(solution)/shard_map/ppermute | solution.py:105
  16.0 0.7 broadcast_dynamic-update-slice_fusion
  16.7 0.7 slice.61
  17.5 0.8 constant_dynamic-slice_fusion
  18.6 2.3 %copy.35 = bf16[64,8,16,128]{3,2,1,0:T(8,128)(2,1)S(1)} copy(bf16[64,8,16,128]{3,1,2,0:T(8,128)(2,1)} %bitcast.34) | data formatting | bytes 4194304
  21.0 0.6 copy.34
  21.6 0.1 convert_reduce_fusion
  21.7 1.2 fusion
  23.4 0.1 reshape.104.pairs_ref
  23.5 0.4 copy.22.kdoc_ref
  24.1 3.5 %collective-permute-done = bf16[256,512]{1,0:T(8,128)(2,1)} collective-permute-done((bf16[256,512]{1,0:T(8,128)(2,1)}, bf16[256,512]{1,0:T(8,128)(2,1)}, u32[]{:S(2)}, u32[]{:S(2)}) %collective-permute-start) | collective-permute-done | bytes 262176 | tf_op jit(solution)/shard_map/ppermute | solution.py:105
  27.7 1.0 constant_dynamic-update-slice_fusion.5
  28.6 1.1 constant_dynamic-update-slice_fusion.4
  29.7 1.1 constant_dynamic-update-slice_fusion.3
  30.9 1.3 %copy-done.5 = bf16[2048,512]{1,0:T(8,128)(2,1)} copy-done((bf16[2048,512]{1,0:T(8,128)(2,1)}, bf16[2048,512]{1,0:T(8,128)(2,1)S(1)}, u32[]{:S(2)}) %copy-start.5) | copy-done | bytes 2097176
  32.2 24.8 %shard_map.112 = (f32[512,2048]{1,0:T(8,128)}, f32[2048,512]{1,0:T(8,128)}) custom-call(s32[120]{0:T(128)S(1)} %reshape.104.pairs_ref, bf16[512,2048]{1,0:T(8,128)(2,1)S(1)} %copy-done.1, bf16[512,2048]{1,0:T(8,128)(2,1)} %do_ref.1, f32[4,2048]{1,0:T(4,128)S(1)} %bitcast.29, f32[4,2048]{1,0:T(4,128)S(1)} %bitcast.28, s32[4,128]{1,0:T(4,128)S(1)} %bitcast.30, ...), custom_call_target="tpu_custom_call" | custom-call | tf_op jit(solution)/shard_map/pallas_call | solution.py:85
  57.0 1.9 %fusion.3 = (f32[512,512]{1,0:T(8,128)S(1)}, f32[512,512]{1,0:T(8,128)S(1)}) fusion(f32[2048,512]{1,0:T(8,128)} %get-tuple-element.18), kind=kLoop, calls=%fused_computation.26 | loop fusion | bytes 4194304 | tf_op jit(solution)/shard_map/slice | solution.py:155
  58.9 2.1 %collective-permute-start.3 = (f32[512,512]{1,0:T(8,128)S(1)}, f32[512,512]{1,0:T(8,128)S(1)}, u32[]{:S(2)}, u32[]{:S(2)}) collective-permute-start(f32[512,512]{1,0:T(8,128)S(1)} %get-tuple-element.19), channel_id=1, source_target_pairs={{4,0},{8,4},{12,8},{16,12},{20,16},{24,20},{28,24},{32,28},{36,32}... | collective-permute-start | bytes 3145736 | tf_op jit(solution)/shard_map/ppermute | solution.py:105
  61.0 1.9 %collective-permute-start.4 = (f32[512,512]{1,0:T(8,128)S(1)}, f32[512,512]{1,0:T(8,128)S(1)}, u32[]{:S(2)}, u32[]{:S(2)}) collective-permute-start(f32[512,512]{1,0:T(8,128)S(1)} %get-tuple-element.20), channel_id=1, source_target_pairs={{8,0},{12,4},{16,8},{20,12},{24,16},{28,20},{32,24},{36,28},{40,32... | collective-permute-start | bytes 3145736 | tf_op jit(solution)/shard_map/ppermute | solution.py:105
  62.9 1.1 slice.67
  64.0 1.3 %collective-permute-start.5 = (f32[256,512]{1,0:T(8,128)S(1)}, f32[256,512]{1,0:T(8,128)S(1)}, u32[]{:S(2)}, u32[]{:S(2)}) collective-permute-start(f32[256,512]{1,0:T(8,128)S(1)} %slice.67), channel_id=1, source_target_pairs={{12,0},{16,4},{20,8},{24,12},{28,16},{32,20},{36,24},{40,28},{44,3... | collective-permute-start | bytes 1572872 | tf_op jit(solution)/shard_map/ppermute | solution.py:105
  65.3 1.6 %convert_element_type.13 = bf16[512,2048]{1,0:T(8,128)(2,1)} convert(f32[512,2048]{1,0:T(8,128)S(1)} %copy-done.3) | non-fusion elementwise | flops 1048576 | bytes 6291456 | tf_op jit(solution)/shard_map/convert_element_type | solution.py:158
  66.9 12.8 %collective-permute-done.3 = f32[512,512]{1,0:T(8,128)S(1)} collective-permute-done((f32[512,512]{1,0:T(8,128)S(1)}, f32[512,512]{1,0:T(8,128)S(1)}, u32[]{:S(2)}, u32[]{:S(2)}) %collective-permute-start.3) | collective-permute-done | bytes 1048608 | tf_op jit(solution)/shard_map/ppermute | solution.py:105
  79.8 45.9 %collective-permute-done.4 = f32[512,512]{1,0:T(8,128)S(1)} collective-permute-done((f32[512,512]{1,0:T(8,128)S(1)}, f32[512,512]{1,0:T(8,128)S(1)}, u32[]{:S(2)}, u32[]{:S(2)}) %collective-permute-start.4) | collective-permute-done | bytes 1048608 | tf_op jit(solution)/shard_map/ppermute | solution.py:105
  125.7 1.6 %add_add_fusion = f32[512,512]{1,0:T(8,128)S(1)} fusion(f32[512,512]{1,0:T(8,128)S(1)} %collective-permute-done.4, f32[512,512]{1,0:T(8,128)S(1)} %collective-permute-done.3, f32[2048,512]{1,0:T(8,128)} %get-tuple-element.18), kind=kLoop, calls=%fused_computation.2 | loop fusion | flops 524288 | bytes 4194304 | tf_op jit(solution)/shard_map/add | solution.py:155
  127.3 0.1 fusion.1
  127.5 0.8 fusion.4
  (38 shorter events, 1.2 us)
Async XLA Ops:
  0.6 17.9 %copy-start = (f32[16,512]{1,0:T(8,128)S(1)}, f32[16,512]{1,0:T(8,128)}, u32[]{:S(2)}) copy-start(f32[16,512]{1,0:T(8,128)} %param.16) | copy-start | bytes 98308
  4.0 25.7 %collective-permute-start.2 = (bf16[512,512]{1,0:T(8,128)(2,1)}, bf16[512,512]{1,0:T(8,128)(2,1)}, u32[]{:S(2)}, u32[]{:S(2)}) collective-permute-start(bf16[512,512]{1,0:T(8,128)(2,1)} %constant_dynamic-update-slice_fusion), channel_id=1, source_target_pairs={{0,4},{4,8},{8,12},{12,16},{16,20},{20,24},{24,28},{28,32},{32,36}... | collective-permute-start | bytes 1572872 | tf_op jit(solution)/shard_map/ppermute | solution.py:105
  5.9 22.7 %collective-permute-start.1 = (bf16[512,512]{1,0:T(8,128)(2,1)}, bf16[512,512]{1,0:T(8,128)(2,1)}, u32[]{:S(2)}, u32[]{:S(2)}) collective-permute-start(bf16[512,512]{1,0:T(8,128)(2,1)} %constant_dynamic-update-slice_fusion), channel_id=1, source_target_pairs={{0,8},{4,12},{8,16},{12,20},{16,24},{20,28},{24,32},{28,36},{32,40... | collective-permute-start | bytes 1572872 | tf_op jit(solution)/shard_map/ppermute | solution.py:105
  11.1 16.5 %collective-permute-start = (bf16[256,512]{1,0:T(8,128)(2,1)}, bf16[256,512]{1,0:T(8,128)(2,1)}, u32[]{:S(2)}, u32[]{:S(2)}) collective-permute-start(bf16[256,512]{1,0:T(8,128)(2,1)} %slice.70), channel_id=1, source_target_pairs={{0,12},{4,16},{8,20},{12,24},{16,28},{20,32},{24,36},{28,40},{32,4... | collective-permute-start | bytes 786440 | tf_op jit(solution)/shard_map/ppermute | solution.py:105
  18.6 2.4 %copy-start.2 = (bf16[512,2048]{1,0:T(8,128)(2,1)S(1)}, bf16[512,2048]{1,0:T(8,128)(2,1)}, u32[]{:S(2)}) copy-start(bf16[512,2048]{1,0:T(8,128)(2,1)} %do_ref.1) | copy-start | bytes 6291460
  21.7 1.5 %copy-start.8 = (s32[44,2]{0,1:T(2,128)S(1)}, s32[44,2]{0,1:T(2,128)}, u32[]{:S(2)}) copy-start(s32[44,2]{0,1:T(2,128)} %param.18) | copy-start | bytes 1060
  22.9 4.7 %copy-start.4 = (bf16[2048,512]{1,0:T(8,128)(2,1)S(1)}, bf16[2048,512]{1,0:T(8,128)(2,1)}, u32[]{:S(2)}) copy-start(bf16[2048,512]{1,0:T(8,128)(2,1)} %broadcast_dynamic-update-slice_fusion) | copy-start | bytes 6291460
  24.0 6.8 %copy-start.6 = (bf16[512,256]{1,0:T(8,128)(2,1)S(1)}, bf16[512,256]{1,0:T(8,128)(2,1)}, u32[]{:S(2)}) copy-start(bf16[512,256]{1,0:T(8,128)(2,1)} %param.12) | copy-start | bytes 786436
  24.0 6.8 %copy-start.7 = (bf16[512,256]{1,0:T(8,128)(2,1)S(1)}, bf16[512,256]{1,0:T(8,128)(2,1)}, u32[]{:S(2)}) copy-start(bf16[512,256]{1,0:T(8,128)(2,1)} %param.13) | copy-start | bytes 786436
  24.1 8.1 %copy-start.1 = (bf16[512,2048]{1,0:T(8,128)(2,1)S(1)}, bf16[512,2048]{1,0:T(8,128)(2,1)}, u32[]{:S(2)}) copy-start(bf16[512,2048]{1,0:T(8,128)(2,1)} %q_ref.1) | copy-start | bytes 6291460
  30.9 1.3 %copy-start.5 = (bf16[2048,512]{1,0:T(8,128)(2,1)}, bf16[2048,512]{1,0:T(8,128)(2,1)S(1)}, u32[]{:S(2)}) copy-start(bf16[2048,512]{1,0:T(8,128)(2,1)S(1)} %constant_dynamic-update-slice_fusion.6.kv_ref) | copy-start | bytes 6291460
  57.0 8.2 %copy-start.3 = (f32[512,2048]{1,0:T(8,128)S(1)}, f32[512,2048]{1,0:T(8,128)}, u32[]{:S(2)}) copy-start(f32[512,2048]{1,0:T(8,128)} %get-tuple-element.17) | copy-start | bytes 12582916
  58.9 20.9 %collective-permute-start.3 = (f32[512,512]{1,0:T(8,128)S(1)}, f32[512,512]{1,0:T(8,128)S(1)}, u32[]{:S(2)}, u32[]{:S(2)}) collective-permute-start(f32[512,512]{1,0:T(8,128)S(1)} %get-tuple-element.19), channel_id=1, source_target_pairs={{4,0},{8,4},{12,8},{16,12},{20,16},{24,20},{28,24},{32,28},{36,32}... | collective-permute-start | bytes 3145736 | tf_op jit(solution)/shard_map/ppermute | solution.py:105
  61.0 64.7 %collective-permute-start.4 = (f32[512,512]{1,0:T(8,128)S(1)}, f32[512,512]{1,0:T(8,128)S(1)}, u32[]{:S(2)}, u32[]{:S(2)}) collective-permute-start(f32[512,512]{1,0:T(8,128)S(1)} %get-tuple-element.20), channel_id=1, source_target_pairs={{8,0},{12,4},{16,8},{20,12},{24,16},{28,20},{32,24},{36,28},{40,32... | collective-permute-start | bytes 3145736 | tf_op jit(solution)/shard_map/ppermute | solution.py:105
  64.0 63.3 %collective-permute-start.5 = (f32[256,512]{1,0:T(8,128)S(1)}, f32[256,512]{1,0:T(8,128)S(1)}, u32[]{:S(2)}, u32[]{:S(2)}) collective-permute-start(f32[256,512]{1,0:T(8,128)S(1)} %slice.67), channel_id=1, source_target_pairs={{12,0},{16,4},{20,8},{24,12},{28,16},{32,20},{36,24},{40,28},{44,3... | collective-permute-start | bytes 1572872 | tf_op jit(solution)/shard_map/ppermute | solution.py:105

commit v5 on v4

--- a/solution.py
+++ b/solution.py
@@ -54,7 +54,7 @@
             weights_low = weights.astype(jnp.bfloat16)
             dv = jnp.dot(weights_low, do, preferred_element_type=jnp.float32)
             dk = jnp.dot(score_grads, q, preferred_element_type=jnp.float32)
-            part_query = lax.dot_general(score_grads, k, TN, preferred_element_type=jnp.float32) * scale
+            part_query = lax.dot_general(score_grads, k, TN, preferred_element_type=jnp.float32)
             for j, c in enumerate(head_cols):
                 dq_ref[pl.ds(qrow, BLOCK), c] += part_query[j * BLOCK:(j + 1) * BLOCK]
             dkv_ref[pl.ds(krow, BLOCK), pl.ds(g * HEAD_DIM, HEAD_DIM)] += dk * scale
@@ -152,10 +152,10 @@
     segments = keyval_grads.reshape(REACH + 1, own_blocks * BLOCK, 2 * kv_features)
     own_grads = segments[REACH]
     for hop in range(1, REACH):
-        own_grads = own_grads + shifted(segments[REACH - hop], "ctx", -hop)
-    far_grads = shifted(segments[0][first_used:], "ctx", -REACH)
-    own_grads = own_grads.at[first_used:].add(far_grads)
-    grad_query = query_grads.reshape(tokens, features).astype(jnp.bfloat16)
+        own_grads = own_grads + shifted(segments[REACH - hop].astype(jnp.bfloat16), "ctx", -hop)
+    far_grads = shifted(segments[0][first_used:].astype(jnp.bfloat16), "ctx", -REACH)
+    own_grads = own_grads.at[first_used:].add(far_grads.astype(jnp.float32))
+    grad_query = (query_grads * HEAD_DIM ** (-0.5)).astype(jnp.bfloat16)
     grad_key = own_grads[:, :kv_features].astype(jnp.bfloat16)
     grad_value = own_grads[:, kv_features:].astype(jnp.bfloat16)
     return (grad_query, grad_key, grad_value)

time: 129 us -> 108 us (0.84)
  the two profiles are of different devices: /device:TPU:10 before, /device:TPU:144 now
where the time goes in v5:
time: 108 us
  starting transfers between devices  40.1 us (37%)
  waiting for transfers between devices  25.5 us (24%)
  Pallas kernels  16.9 us (16%)
  local copies, waits for them, and re-layouts  16.8 us (16%)
  other arithmetic  7.78 us (7%)
    ppermute x6, starting transfers between devices, shifted(): return lax.ppermute(shard, axis, pairs)  40.1 us
    ppermute x6, waiting for transfers between devices, shifted(): return lax.ppermute(shard, axis, pairs)  25.5 us
    pallas_call x1, Pallas kernels, run_pairs(): pl.pallas_call(pair_kernel, out_shape=(jax.ShapeDtypeStruct((tokens, feat...  16.9 us
    unnamed x28, local copies, waits for them, and re-layouts  9.89 us
    another operation x2, other arithmetic  2.68 us
  transfers between devices with their start and end apart: 6, of which 3 were waited for; matrix products, arithmetic and copies ran while one was open for 14% of the time, Pallas kernels for 0%

profile of v5, /device:TPU:144, one launch (start us, length us, event | category | flops | bytes accessed | tf_op | source)
XLA Modules:
  0.0 108.0 jit_solution(9229953288348842383)
XLA Ops:
  0.6 1.7 %constant_dynamic-update-slice_fusion.1 = bf16[512,512]{1,0:T(8,128)(2,1)} fusion(bf16[512,256]{1,0:T(8,128)(2,1)} %param.12), kind=kLoop, calls=%fused_computation.13 | loop fusion | bytes 524288
  2.3 1.7 %constant_dynamic-update-slice_fusion = bf16[512,512]{1,0:T(8,128)(2,1)} fusion(bf16[512,512]{1,0:T(8,128)(2,1)} %constant_dynamic-update-slice_fusion.1, bf16[512,256]{1,0:T(8,128)(2,1)} %param.13), kind=kLoop, calls=%fused_computation.12 | loop fusion | bytes 524288 | tf_op jit(solution)/shard_map/concatenate | solution.py:128
  4.0 1.9 %collective-permute-start.2 = (bf16[512,512]{1,0:T(8,128)(2,1)}, bf16[512,512]{1,0:T(8,128)(2,1)}, u32[]{:S(2)}, u32[]{:S(2)}) collective-permute-start(bf16[512,512]{1,0:T(8,128)(2,1)} %constant_dynamic-update-slice_fusion), channel_id=1, source_target_pairs={{0,4},{4,8},{8,12},{12,16},{16,20},{20,24},{24,28},{28,32},{32,36}... | collective-permute-start | bytes 1572872 | tf_op jit(solution)/shard_map/ppermute | solution.py:105
  5.9 3.2 %collective-permute-start.1 = (bf16[512,512]{1,0:T(8,128)(2,1)}, bf16[512,512]{1,0:T(8,128)(2,1)}, u32[]{:S(2)}, u32[]{:S(2)}) collective-permute-start(bf16[512,512]{1,0:T(8,128)(2,1)} %constant_dynamic-update-slice_fusion), channel_id=1, source_target_pairs={{0,8},{4,12},{8,16},{12,20},{16,24},{20,28},{24,32},{28,36},{32,40... | collective-permute-start | bytes 1572872 | tf_op jit(solution)/shard_map/ppermute | solution.py:105
  9.1 1.7 %slice.73 = bf16[256,512]{1,0:T(8,128)(2,1)} slice(bf16[512,512]{1,0:T(8,128)(2,1)} %constant_dynamic-update-slice_fusion), slice={[256:512], [0:512]} | slice | bytes 524288 | tf_op jit(solution)/shard_map/slice | solution.py:133
  10.8 3.6 %collective-permute-start = (bf16[256,512]{1,0:T(8,128)(2,1)}, bf16[256,512]{1,0:T(8,128)(2,1)}, u32[]{:S(2)}, u32[]{:S(2)}) collective-permute-start(bf16[256,512]{1,0:T(8,128)(2,1)} %slice.73), channel_id=1, source_target_pairs={{0,12},{4,16},{8,20},{12,24},{16,28},{20,32},{24,36},{28,40},{32,4... | collective-permute-start | bytes 786440 | tf_op jit(solution)/shard_map/ppermute | solution.py:105
  14.4 0.7 broadcast_dynamic-update-slice_fusion
  15.1 0.7 slice.64
  15.9 0.8 constant_dynamic-slice_fusion
  16.8 0.1 slice_reduce_fusion
  17.0 2.3 %copy.35 = bf16[64,8,16,128]{3,2,1,0:T(8,128)(2,1)S(1)} copy(bf16[64,8,16,128]{3,1,2,0:T(8,128)(2,1)} %bitcast.34) | data formatting | bytes 4194304
  19.4 0.6 copy.34
  20.0 0.1 convert_reduce_fusion
  20.1 1.2 %fusion = f32[16,512]{0,1:T(8,128)S(1)} fusion(bf16[512,16,128]{2,1,0:T(8,128)(2,1)S(1)} %bitcast.31, bf16[512,16,128]{2,1,0:T(8,128)(2,1)S(1)} %bitcast.32), kind=kLoop, calls=%fused_computation.1 | loop fusion | flops 4186112 | bytes 4227072
  21.8 0.1 reshape.104.pairs_ref
  21.9 0.4 copy.22.kdoc_ref
  22.5 9.1 %collective-permute-done = bf16[256,512]{1,0:T(8,128)(2,1)} collective-permute-done((bf16[256,512]{1,0:T(8,128)(2,1)}, bf16[256,512]{1,0:T(8,128)(2,1)}, u32[]{:S(2)}, u32[]{:S(2)}) %collective-permute-start) | collective-permute-done | bytes 262176 | tf_op jit(solution)/shard_map/ppermute | solution.py:105
  31.7 1.0 constant_dynamic-update-slice_fusion.5
  32.6 1.1 constant_dynamic-update-slice_fusion.4
  33.7 1.1 constant_dynamic-update-slice_fusion.3
  34.9 1.3 %copy-done.5 = bf16[2048,512]{1,0:T(8,128)(2,1)} copy-done((bf16[2048,512]{1,0:T(8,128)(2,1)}, bf16[2048,512]{1,0:T(8,128)(2,1)S(1)}, u32[]{:S(2)}) %copy-start.5) | copy-done | bytes 2097176
  36.2 16.9 %shard_map.112 = (f32[512,2048]{1,0:T(8,128)}, f32[2048,512]{1,0:T(8,128)}) custom-call(s32[120]{0:T(128)S(1)} %reshape.104.pairs_ref, bf16[512,2048]{1,0:T(8,128)(2,1)S(1)} %copy-done.1, bf16[512,2048]{1,0:T(8,128)(2,1)} %do_ref.1, f32[4,2048]{1,0:T(4,128)S(1)} %bitcast.29, f32[4,2048]{1,0:T(4,128)S(1)} %bitcast.28, s32[4,128]{1,0:T(4,128)S(1)} %bitcast.30, ...), custom_call_target="tpu_custom_call" | custom-call | tf_op jit(solution)/shard_map/pallas_call | solution.py:85
  53.1 2.6 %convert.9 = bf16[2048,512]{1,0:T(8,128)(2,1)S(1)} convert(f32[2048,512]{1,0:T(8,128)} %get-tuple-element.18) | non-fusion elementwise | flops 1048576 | bytes 6291456 | tf_op jit(solution)/shard_map/convert.4
  55.8 8.7 %collective-permute-start.5 = (bf16[256,512]{1,0:T(8,128)(2,1)S(1)}, bf16[256,512]{1,0:T(8,128)(2,1)S(1)}, u32[]{:S(2)}, u32[]{:S(2)}) collective-permute-start(bf16[256,512]{1,0:T(8,128)(2,1)S(1)} %slice.77), channel_id=1, source_target_pairs={{12,0},{16,4},{20,8},{24,12},{28,16},{32,20},{36,24},{40,28},{44,3... | collective-permute-start | bytes 786440 | tf_op jit(solution)/shard_map/ppermute | solution.py:105
  64.5 16.1 %collective-permute-start.3 = (bf16[512,512]{1,0:T(8,128)(2,1)S(1)}, bf16[512,512]{1,0:T(8,128)(2,1)S(1)}, u32[]{:S(2)}, u32[]{:S(2)}) collective-permute-start(bf16[512,512]{1,0:T(8,128)(2,1)S(1)} %get-tuple-element.19), channel_id=1, source_target_pairs={{4,0},{8,4},{12,8},{16,12},{20,16},{24,20},{28,24},{32,28},{36,32}... | collective-permute-start | bytes 1572872 | tf_op jit(solution)/shard_map/ppermute | solution.py:105
  80.6 6.7 %collective-permute-start.4 = (bf16[512,512]{1,0:T(8,128)(2,1)S(1)}, bf16[512,512]{1,0:T(8,128)(2,1)S(1)}, u32[]{:S(2)}, u32[]{:S(2)}) collective-permute-start(bf16[512,512]{1,0:T(8,128)(2,1)S(1)} %get-tuple-element.20), channel_id=1, source_target_pairs={{8,0},{12,4},{16,8},{20,12},{24,16},{28,20},{32,24},{36,28},{40,32... | collective-permute-start | bytes 1572872 | tf_op jit(solution)/shard_map/ppermute | solution.py:105
  87.3 1.8 %multiply_convert_fusion = bf16[512,2048]{1,0:T(8,128)(2,1)} fusion(f32[512,2048]{1,0:T(8,128)S(1)} %copy-done.3), kind=kLoop, calls=%fused_computation.2 | loop fusion | flops 2097152 | bytes 6291456 | tf_op jit(solution)/shard_map/convert_element_type | solution.py:158
  89.2 1.4 %collective-permute-done.3 = bf16[512,512]{1,0:T(8,128)(2,1)S(1)} collective-permute-done((bf16[512,512]{1,0:T(8,128)(2,1)S(1)}, bf16[512,512]{1,0:T(8,128)(2,1)S(1)}, u32[]{:S(2)}, u32[]{:S(2)}) %collective-permute-start.3) | collective-permute-done | bytes 524320 | tf_op jit(solution)/shard_map/ppermute | solution.py:105
  90.6 14.9 %collective-permute-done.4 = bf16[512,512]{1,0:T(8,128)(2,1)S(1)} collective-permute-done((bf16[512,512]{1,0:T(8,128)(2,1)S(1)}, bf16[512,512]{1,0:T(8,128)(2,1)S(1)}, u32[]{:S(2)}, u32[]{:S(2)}) %collective-permute-start.4) | collective-permute-done | bytes 524320 | tf_op jit(solution)/shard_map/ppermute | solution.py:105
  105.5 1.4 %convert_add_fusion = f32[512,512]{1,0:T(8,128)S(1)} fusion(bf16[512,512]{1,0:T(8,128)(2,1)S(1)} %collective-permute-done.4, bf16[512,512]{1,0:T(8,128)(2,1)S(1)} %collective-permute-done.3, f32[2048,512]{1,0:T(8,128)} %get-tuple-element.18), kind=kLoop, calls=%fused_computation.3 | loop fusion | flops 1048576 | bytes 3145728 | tf_op jit(solution)/shard_map/add | solution.py:155
  106.9 0.1 fusion.1
  107.1 0.8 fusion.4
  (39 shorter events, 1.2 us)
Async XLA Ops:
  0.6 16.4 %copy-start = (f32[16,512]{1,0:T(8,128)S(1)}, f32[16,512]{1,0:T(8,128)}, u32[]{:S(2)}) copy-start(f32[16,512]{1,0:T(8,128)} %param.16) | copy-start | bytes 98308
  4.0 29.7 %collective-permute-start.2 = (bf16[512,512]{1,0:T(8,128)(2,1)}, bf16[512,512]{1,0:T(8,128)(2,1)}, u32[]{:S(2)}, u32[]{:S(2)}) collective-permute-start(bf16[512,512]{1,0:T(8,128)(2,1)} %constant_dynamic-update-slice_fusion), channel_id=1, source_target_pairs={{0,4},{4,8},{8,12},{12,16},{16,20},{20,24},{24,28},{28,32},{32,36}... | collective-permute-start | bytes 1572872 | tf_op jit(solution)/shard_map/ppermute | solution.py:105
  5.9 26.7 %collective-permute-start.1 = (bf16[512,512]{1,0:T(8,128)(2,1)}, bf16[512,512]{1,0:T(8,128)(2,1)}, u32[]{:S(2)}, u32[]{:S(2)}) collective-permute-start(bf16[512,512]{1,0:T(8,128)(2,1)} %constant_dynamic-update-slice_fusion), channel_id=1, source_target_pairs={{0,8},{4,12},{8,16},{12,20},{16,24},{20,28},{24,32},{28,36},{32,40... | collective-permute-start | bytes 1572872 | tf_op jit(solution)/shard_map/ppermute | solution.py:105
  10.8 20.8 %collective-permute-start = (bf16[256,512]{1,0:T(8,128)(2,1)}, bf16[256,512]{1,0:T(8,128)(2,1)}, u32[]{:S(2)}, u32[]{:S(2)}) collective-permute-start(bf16[256,512]{1,0:T(8,128)(2,1)} %slice.73), channel_id=1, source_target_pairs={{0,12},{4,16},{8,20},{12,24},{16,28},{20,32},{24,36},{28,40},{32,4... | collective-permute-start | bytes 786440 | tf_op jit(solution)/shard_map/ppermute | solution.py:105
  17.0 2.4 %copy-start.2 = (bf16[512,2048]{1,0:T(8,128)(2,1)S(1)}, bf16[512,2048]{1,0:T(8,128)(2,1)}, u32[]{:S(2)}) copy-start(bf16[512,2048]{1,0:T(8,128)(2,1)} %do_ref.1) | copy-start | bytes 6291460
  20.1 1.5 %copy-start.8 = (s32[44,2]{0,1:T(2,128)S(1)}, s32[44,2]{0,1:T(2,128)}, u32[]{:S(2)}) copy-start(s32[44,2]{0,1:T(2,128)} %param.18) | copy-start | bytes 1060
  21.3 10.3 %copy-start.4 = (bf16[2048,512]{1,0:T(8,128)(2,1)S(1)}, bf16[2048,512]{1,0:T(8,128)(2,1)}, u32[]{:S(2)}) copy-start(bf16[2048,512]{1,0:T(8,128)(2,1)} %broadcast_dynamic-update-slice_fusion) | copy-start | bytes 6291460
  22.4 12.4 %copy-start.6 = (bf16[512,256]{1,0:T(8,128)(2,1)S(1)}, bf16[512,256]{1,0:T(8,128)(2,1)}, u32[]{:S(2)}) copy-start(bf16[512,256]{1,0:T(8,128)(2,1)} %param.12) | copy-start | bytes 786436
  22.4 12.4 %copy-start.7 = (bf16[512,256]{1,0:T(8,128)(2,1)S(1)}, bf16[512,256]{1,0:T(8,128)(2,1)}, u32[]{:S(2)}) copy-start(bf16[512,256]{1,0:T(8,128)(2,1)} %param.13) | copy-start | bytes 786436
  22.5 13.7 %copy-start.1 = (bf16[512,2048]{1,0:T(8,128)(2,1)S(1)}, bf16[512,2048]{1,0:T(8,128)(2,1)}, u32[]{:S(2)}) copy-start(bf16[512,2048]{1,0:T(8,128)(2,1)} %q_ref.1) | copy-start | bytes 6291460
  34.9 1.3 %copy-start.5 = (bf16[2048,512]{1,0:T(8,128)(2,1)}, bf16[2048,512]{1,0:T(8,128)(2,1)S(1)}, u32[]{:S(2)}) copy-start(bf16[2048,512]{1,0:T(8,128)(2,1)S(1)} %constant_dynamic-update-slice_fusion.6.kv_ref) | copy-start | bytes 6291460
  53.1 34.2 %copy-start.3 = (f32[512,2048]{1,0:T(8,128)S(1)}, f32[512,2048]{1,0:T(8,128)}, u32[]{:S(2)}) copy-start(f32[512,2048]{1,0:T(8,128)} %get-tuple-element.17) | copy-start | bytes 12582916
  55.8 51.1 %collective-permute-start.5 = (bf16[256,512]{1,0:T(8,128)(2,1)S(1)}, bf16[256,512]{1,0:T(8,128)(2,1)S(1)}, u32[]{:S(2)}, u32[]{:S(2)}) collective-permute-start(bf16[256,512]{1,0:T(8,128)(2,1)S(1)} %slice.77), channel_id=1, source_target_pairs={{12,0},{16,4},{20,8},{24,12},{28,16},{32,20},{36,24},{40,28},{44,3... | collective-permute-start | bytes 786440 | tf_op jit(solution)/shard_map/ppermute | solution.py:105
  64.5 26.1 %collective-permute-start.3 = (bf16[512,512]{1,0:T(8,128)(2,1)S(1)}, bf16[512,512]{1,0:T(8,128)(2,1)S(1)}, u32[]{:S(2)}, u32[]{:S(2)}) collective-permute-start(bf16[512,512]{1,0:T(8,128)(2,1)S(1)} %get-tuple-element.19), channel_id=1, source_target_pairs={{4,0},{8,4},{12,8},{16,12},{20,16},{24,20},{28,24},{32,28},{36,32}... | collective-permute-start | bytes 1572872 | tf_op jit(solution)/shard_map/ppermute | solution.py:105
  80.6 24.9 %collective-permute-start.4 = (bf16[512,512]{1,0:T(8,128)(2,1)S(1)}, bf16[512,512]{1,0:T(8,128)(2,1)S(1)}, u32[]{:S(2)}, u32[]{:S(2)}) collective-permute-start(bf16[512,512]{1,0:T(8,128)(2,1)S(1)} %get-tuple-element.20), channel_id=1, source_target_pairs={{8,0},{12,4},{16,8},{20,12},{24,16},{28,20},{32,24},{36,28},{40,32... | collective-permute-start | bytes 1572872 | tf_op jit(solution)/shard_map/ppermute | solution.py:105

commit v6 on v5

--- a/solution.py
+++ b/solution.py
@@ -13,12 +13,14 @@
 TN = (((0,), (0,)), ((), ()))
 
 
-def pair_kernel(pairs_ref, q_ref, do_ref, norm_ref, delta_ref, qdoc_ref, qpos_ref,
-                kdoc_ref, kpos_ref, kv_ref, dq_ref, dkv_ref):
+def pair_kernel(piece_starts, pairs_ref, q_ref, do_ref, norm_ref, delta_ref, qdoc_ref, qpos_ref,
+                kdoc_ref, kpos_ref, *refs):
+    piece_refs = refs[:len(piece_starts)]
+    dq_ref, dkv_ref = refs[len(piece_starts):]
     dq_ref[...] = jnp.zeros(dq_ref.shape, jnp.float32)
     dkv_ref[...] = jnp.zeros(dkv_ref.shape, jnp.float32)
     heads = norm_ref.shape[1] // BLOCK
-    kv_features = kv_ref.shape[1] // 2
+    kv_features = piece_refs[0].shape[1] // 2
     kv_heads = kv_features // HEAD_DIM
     group = heads // kv_heads
     scale = HEAD_DIM ** (-0.5)
@@ -26,10 +28,17 @@
     def body(i, carry):
         qb_raw = pairs_ref[2 * i]
         kb_raw = pairs_ref[2 * i + 1]
-        pl.when((qb_raw >= 0) & (kb_raw >= 0))(lambda: one_pair(jnp.maximum(qb_raw, 0), jnp.maximum(kb_raw, 0)))
+        live = (qb_raw >= 0) & (kb_raw >= 0)
+        qb = jnp.maximum(qb_raw, 0)
+        kb = jnp.maximum(kb_raw, 0)
+        for start, kv_ref in zip(piece_starts, piece_refs):
+            end = start + kv_ref.shape[0] // BLOCK
+            inside = live & (kb >= start) & (kb < end)
+            pl.when(inside)(functools.partial(one_pair, qb, kb, kv_ref, start))
         return carry
 
-    def one_pair(qb, kb):
+    def one_pair(qb, kb, kv_ref, start):
+        local_row = pl.multiple_of((kb - start) * BLOCK, BLOCK)
         qrow = pl.multiple_of(qb * BLOCK, BLOCK)
         krow = pl.multiple_of(kb * BLOCK, BLOCK)
         qdoc = qdoc_ref[pl.ds(qb, 1), :]
@@ -39,8 +48,8 @@
         allowed = (kdoc == qdoc) & (kpos <= qpos)
         wide_allowed = jnp.concatenate([allowed] * group, axis=1)
         for g in range(kv_heads):
-            k = kv_ref[pl.ds(krow, BLOCK), pl.ds(g * HEAD_DIM, HEAD_DIM)]
-            v = kv_ref[pl.ds(krow, BLOCK), pl.ds(kv_features + g * HEAD_DIM, HEAD_DIM)]
+            k = kv_ref[pl.ds(local_row, BLOCK), pl.ds(g * HEAD_DIM, HEAD_DIM)]
+            v = kv_ref[pl.ds(local_row, BLOCK), pl.ds(kv_features + g * HEAD_DIM, HEAD_DIM)]
             head_cols = [pl.ds((g * group + j) * HEAD_DIM, HEAD_DIM) for j in range(group)]
             q = jnp.concatenate([q_ref[pl.ds(qrow, BLOCK), c] for c in head_cols], axis=0)
             do = jnp.concatenate([do_ref[pl.ds(qrow, BLOCK), c] for c in head_cols], axis=0)
@@ -63,15 +72,15 @@
     lax.fori_loop(0, pairs_ref.shape[0] // 2, body, 0)
 
 
-def run_pairs(pairs, queries, outgrads, norms, deltas, query_pos, keyval, key_pos, doc_bounds):
+def run_pairs(pairs, queries, outgrads, norms, deltas, query_pos, pieces, key_pos, doc_bounds):
     q_doc = doc_index(query_pos, doc_bounds)
     k_doc = doc_index(key_pos, doc_bounds)
     tokens, features = queries.shape
-    window, both = keyval.shape
+    window = key_pos.shape[0]
+    both = pieces[0][1].shape[1]
     heads = norms.shape[0]
     blocks = tokens // BLOCK
     norms = norms.reshape(heads, blocks, BLOCK).transpose(1, 0, 2).reshape(blocks, heads * BLOCK)
-    deltas = deltas.reshape(heads, blocks, BLOCK).transpose(1, 0, 2).reshape(blocks, heads * BLOCK)
     vmem = pltpu.MemorySpace.VMEM
     smem = pltpu.MemorySpace.SMEM
     args = (
@@ -79,11 +88,11 @@
         queries, outgrads, norms, deltas,
         q_doc, query_pos,
         k_doc.reshape(window, 1), key_pos.reshape(window, 1),
-        keyval,
-    )
-    specs = [pl.BlockSpec(memory_space=smem)] + [pl.BlockSpec(memory_space=vmem)] * 9
+    ) + tuple(rows for _, rows in pieces)
+    specs = [pl.BlockSpec(memory_space=smem)] + [pl.BlockSpec(memory_space=vmem)] * (len(args) - 1)
+    kernel = functools.partial(pair_kernel, tuple(start for start, _ in pieces))
     return pl.pallas_call(
-        pair_kernel,
+        kernel,
         out_shape=(
             jax.ShapeDtypeStruct((tokens, features), jnp.float32),
             jax.ShapeDtypeStruct((window, both), jnp.float32),
@@ -119,23 +128,15 @@
     heads = log_norm.shape[0]
     own_blocks = tokens // BLOCK
     offsets = jnp.arange(BLOCK, dtype=jnp.int32)
-    delta = jnp.einsum(
-        "thd,thd->ht",
-        grad_out.reshape(tokens, heads, HEAD_DIM),
-        attn_out.reshape(tokens, heads, HEAD_DIM),
-        preferred_element_type=jnp.float32,
-    )
+    products = grad_out.astype(jnp.float32) * attn_out.astype(jnp.float32)
+    delta = jnp.sum(products.reshape(tokens, heads, HEAD_DIM), axis=2)
+    delta = delta.reshape(own_blocks, BLOCK, heads).transpose(0, 2, 1).reshape(own_blocks, heads * BLOCK)
     own_keyval = jnp.concatenate([key, value], axis=1)
     first_used = min(max(REACH * own_blocks - DOC_BLOCKS, 0), own_blocks) * BLOCK
-    pieces = []
-    for hop in range(REACH, 0, -1):
-        if hop == REACH:
-            tail = shifted(own_keyval[first_used:], "ctx", hop)
-            pieces.append(jnp.zeros((first_used, 2 * kv_features), own_keyval.dtype))
-            pieces.append(tail)
-        else:
-            pieces.append(shifted(own_keyval, "ctx", hop))
-    keyval_window = jnp.concatenate(pieces + [own_keyval], axis=0)
+    pieces = [(first_used // BLOCK, shifted(own_keyval[first_used:], "ctx", REACH))]
+    for hop in range(REACH - 1, 0, -1):
+        pieces.append(((REACH - hop) * own_blocks, shifted(own_keyval, "ctx", hop)))
+    pieces.append((REACH * own_blocks, own_keyval))
     first_block = position * own_blocks
     query_pos = (first_block + jnp.arange(own_blocks, dtype=jnp.int32))[:, None] * BLOCK + offsets
     window_first = first_block - REACH * own_blocks
@@ -147,7 +148,7 @@
     pairs = jnp.concatenate([local_pairs, ship_pairs], axis=0)
     query_grads, keyval_grads = run_pairs(
         pairs, query, grad_out, log_norm, delta, query_pos,
-        keyval_window, key_pos, doc_bounds,
+        pieces, key_pos, doc_bounds,
     )
     segments = keyval_grads.reshape(REACH + 1, own_blocks * BLOCK, 2 * kv_features)
     own_grads = segments[REACH]

time: 108 us -> 109 us (level)
  the two profiles are of different devices: /device:TPU:144 before, /device:TPU:132 now
where the time goes in v6:
time: 109 us; the launch traced here: 108 us
  Pallas kernels  42.1 us (39%)
  waiting for transfers between devices  19.7 us (18%)
  other arithmetic  15.8 us (14%)
  starting transfers between devices  15.3 us (14%)
  local copies, waits for them, and re-layouts  14.6 us (13%)
    pallas_call x1, Pallas kernels, run_pairs(): pl.pallas_call(kernel, out_shape=(jax.ShapeDtypeStruct((tokens, features)...  42.1 us
    ppermute x6, waiting for transfers between devices, shifted(): return lax.ppermute(shard, axis, pairs)  19.7 us
    ppermute x6, starting transfers between devices, shifted(): return lax.ppermute(shard, axis, pairs)  15.3 us
    unnamed x12, local copies, waits for them, and re-layouts  6.8 us
    unnamed x1, other arithmetic  4.98 us
    reduce_sum x1, other arithmetic, local(): delta = jnp.sum(products.reshape(tokens, heads, HEAD_DIM), axis=2)  4.2 us
    another operation x2, other arithmetic  2.68 us
  transfers between devices with their start and end apart: 6, of which 2 were waited for; matrix products, arithmetic and copies ran while one was open for 21% of the time, Pallas kernels for 0%

profile of v6, /device:TPU:132, one launch (start us, length us, event | category | flops | bytes accessed | tf_op | source)
XLA Modules:
  0.0 108.4 jit_solution(7079943312108685992)
XLA Ops:
  0.6 1.7 %constant_dynamic-update-slice_fusion.1 = bf16[512,512]{1,0:T(8,128)(2,1)} fusion(bf16[512,256]{1,0:T(8,128)(2,1)} %param.12), kind=kLoop, calls=%fused_computation.12 | loop fusion | bytes 524288
  2.3 1.7 %constant_dynamic-update-slice_fusion.refs_3_ = bf16[512,512]{1,0:T(8,128)(2,1)} fusion(bf16[512,512]{1,0:T(8,128)(2,1)} %constant_dynamic-update-slice_fusion.1, bf16[512,256]{1,0:T(8,128)(2,1)} %param.13), kind=kLoop, calls=%fused_computation.11 | loop fusion | bytes 524288 | tf_op jit(solution)/shard_map/concatenate | solution.py:134
  4.0 1.9 %collective-permute-start.2 = (bf16[512,512]{1,0:T(8,128)(2,1)}, bf16[512,512]{1,0:T(8,128)(2,1)}, u32[]{:S(2)}, u32[]{:S(2)}) collective-permute-start(bf16[512,512]{1,0:T(8,128)(2,1)} %constant_dynamic-update-slice_fusion.refs_3_), channel_id=1, source_target_pairs={{0,4},{4,8},{8,12},{12,16},{16,20},{20,24},{24,28},{28,32},{32,36}... | collective-permute-start | bytes 1572872 | tf_op jit(solution)/shard_map/ppermute | solution.py:114
  5.9 3.5 %collective-permute-start.1 = (bf16[512,512]{1,0:T(8,128)(2,1)}, bf16[512,512]{1,0:T(8,128)(2,1)}, u32[]{:S(2)}, u32[]{:S(2)}) collective-permute-start(bf16[512,512]{1,0:T(8,128)(2,1)} %constant_dynamic-update-slice_fusion.refs_3_), channel_id=1, source_target_pairs={{0,8},{4,12},{8,16},{12,20},{16,24},{20,28},{24,32},{28,36},{32,40... | collective-permute-start | bytes 1572872 | tf_op jit(solution)/shard_map/ppermute | solution.py:114
  9.4 1.7 %slice.73 = bf16[256,512]{1,0:T(8,128)(2,1)} slice(bf16[512,512]{1,0:T(8,128)(2,1)} %constant_dynamic-update-slice_fusion.refs_3_), slice={[256:512], [0:512]} | slice | bytes 524288 | tf_op jit(solution)/shard_map/slice | solution.py:136
  11.1 4.2 %collective-permute-start = (bf16[256,512]{1,0:T(8,128)(2,1)}, bf16[256,512]{1,0:T(8,128)(2,1)S(1)}, u32[]{:S(2)}, u32[]{:S(2)}) collective-permute-start(bf16[256,512]{1,0:T(8,128)(2,1)} %slice.73), channel_id=1, source_target_pairs={{0,12},{4,16},{8,20},{12,24},{16,28},{20,32},{24,36},{28,40},{32,4... | collective-permute-start | bytes 786440 | tf_op jit(solution)/shard_map/ppermute | solution.py:114
  15.3 0.7 slice.64
  16.1 0.8 constant_dynamic-slice_fusion
  16.9 0.1 copy.24
  17.0 0.1 slice_reduce_fusion
  17.2 0.1 convert_reduce_fusion.1
  17.3 5.0 %multiply_bitcast_fusion = f32[64,8,16,128]{3,1,2,0:T(8,128)} fusion(bf16[512,2048]{1,0:T(8,128)(2,1)} %param.14, bf16[512,2048]{1,0:T(8,128)(2,1)} %do_ref.1), kind=kLoop, calls=%fused_computation.1 | loop fusion | flops 3145728 | bytes 8388608
  22.3 0.1 stack.9
  22.3 0.1 stack.10
  22.4 0.1 convert_reduce_fusion
  22.6 0.1 copy.25
  22.7 0.1 reshape.101.pairs_ref
  22.9 0.4 copy.28.kdoc_ref
  23.3 5.1 %copy.32 = f32[64,8,16,128]{3,2,1,0:T(8,128)} copy(f32[64,8,16,128]{3,1,2,0:T(8,128)} %multiply_bitcast_fusion) | data formatting | bytes 8388608
  28.4 4.2 %reduce_sum.27 = f32[512,16]{1,0:T(8,128)} reduce(f32[512,16,128]{2,1,0:T(8,128)} %bitcast.26, f32[]{:T(128)} %constant.47.clone.1), dimensions={2}, to_apply=%region_0.0 | reduce | flops 1040384 | bytes 4227076 | tf_op jit(solution)/shard_map/reduce_sum | solution.py:132
  32.6 1.0 copy.29
  33.7 42.1 %shard_map.112 = (f32[512,2048]{1,0:T(8,128)}, f32[2048,512]{1,0:T(8,128)}) custom-call(s32[120]{0:T(128)S(1)} %reshape.101.pairs_ref, bf16[512,2048]{1,0:T(8,128)(2,1)S(1)} %copy-done.1, bf16[512,2048]{1,0:T(8,128)(2,1)} %do_ref.1, f32[4,2048]{1,0:T(4,128)S(1)} %bitcast.24, f32[4,2048]{1,0:T(4,128)S(1)} %bitcast.23, s32[4,128]{1,0:T(4,128)S(1)} %bitcast.25, ...), custom_call_target="tpu_custom_call" | custom-call | tf_op jit(solution)/shard_map/pallas_call | solution.py:94
  75.8 2.6 %convert.9 = bf16[2048,512]{1,0:T(8,128)(2,1)S(1)} convert(f32[2048,512]{1,0:T(8,128)} %get-tuple-element.18) | non-fusion elementwise | flops 1048576 | bytes 6291456 | tf_op jit(solution)/shard_map/convert.4
  78.5 1.9 %collective-permute-start.5 = (bf16[256,512]{1,0:T(8,128)(2,1)S(1)}, bf16[256,512]{1,0:T(8,128)(2,1)S(1)}, u32[]{:S(2)}, u32[]{:S(2)}) collective-permute-start(bf16[256,512]{1,0:T(8,128)(2,1)S(1)} %slice.77), channel_id=1, source_target_pairs={{12,0},{16,4},{20,8},{24,12},{28,16},{32,20},{36,24},{40,28},{44,3... | collective-permute-start | bytes 786440 | tf_op jit(solution)/shard_map/ppermute | solution.py:114
  80.5 1.9 %collective-permute-start.3 = (bf16[512,512]{1,0:T(8,128)(2,1)S(1)}, bf16[512,512]{1,0:T(8,128)(2,1)S(1)}, u32[]{:S(2)}, u32[]{:S(2)}) collective-permute-start(bf16[512,512]{1,0:T(8,128)(2,1)S(1)} %get-tuple-element.19), channel_id=1, source_target_pairs={{4,0},{8,4},{12,8},{16,12},{20,16},{24,20},{28,24},{32,28},{36,32}... | collective-permute-start | bytes 1572872 | tf_op jit(solution)/shard_map/ppermute | solution.py:114
  82.4 1.9 %collective-permute-start.4 = (bf16[512,512]{1,0:T(8,128)(2,1)S(1)}, bf16[512,512]{1,0:T(8,128)(2,1)S(1)}, u32[]{:S(2)}, u32[]{:S(2)}) collective-permute-start(bf16[512,512]{1,0:T(8,128)(2,1)S(1)} %get-tuple-element.20), channel_id=1, source_target_pairs={{8,0},{12,4},{16,8},{20,12},{24,16},{28,20},{32,24},{36,28},{40,32... | collective-permute-start | bytes 1572872 | tf_op jit(solution)/shard_map/ppermute | solution.py:114
  84.3 1.8 %multiply_convert_fusion = bf16[512,2048]{1,0:T(8,128)(2,1)} fusion(f32[512,2048]{1,0:T(8,128)S(1)} %copy-done.2), kind=kLoop, calls=%fused_computation | loop fusion | flops 2097152 | bytes 6291456 | tf_op jit(solution)/shard_map/convert_element_type | solution.py:159
  86.2 8.7 %collective-permute-done.3 = bf16[512,512]{1,0:T(8,128)(2,1)S(1)} collective-permute-done((bf16[512,512]{1,0:T(8,128)(2,1)S(1)}, bf16[512,512]{1,0:T(8,128)(2,1)S(1)}, u32[]{:S(2)}, u32[]{:S(2)}) %collective-permute-start.3) | collective-permute-done | bytes 524320 | tf_op jit(solution)/shard_map/ppermute | solution.py:114
  94.9 11.0 %collective-permute-done.4 = bf16[512,512]{1,0:T(8,128)(2,1)S(1)} collective-permute-done((bf16[512,512]{1,0:T(8,128)(2,1)S(1)}, bf16[512,512]{1,0:T(8,128)(2,1)S(1)}, u32[]{:S(2)}, u32[]{:S(2)}) %collective-permute-start.4) | collective-permute-done | bytes 524320 | tf_op jit(solution)/shard_map/ppermute | solution.py:114
  105.9 1.4 %convert_add_fusion = f32[512,512]{1,0:T(8,128)S(1)} fusion(bf16[512,512]{1,0:T(8,128)(2,1)S(1)} %collective-permute-done.4, bf16[512,512]{1,0:T(8,128)(2,1)S(1)} %collective-permute-done.3, f32[2048,512]{1,0:T(8,128)} %get-tuple-element.18), kind=kLoop, calls=%fused_computation.2 | loop fusion | flops 1048576 | bytes 3145728 | tf_op jit(solution)/shard_map/add | solution.py:156
  107.3 0.1 fusion
  107.5 0.8 fusion.3
  (23 shorter events, 0.5 us)
Async XLA Ops:
  0.6 16.5 %copy-start = (f32[16,512]{1,0:T(8,128)S(1)}, f32[16,512]{1,0:T(8,128)}, u32[]{:S(2)}) copy-start(f32[16,512]{1,0:T(8,128)} %param.16) | copy-start | bytes 98308
  4.0 29.7 %collective-permute-start.2 = (bf16[512,512]{1,0:T(8,128)(2,1)}, bf16[512,512]{1,0:T(8,128)(2,1)}, u32[]{:S(2)}, u32[]{:S(2)}) collective-permute-start(bf16[512,512]{1,0:T(8,128)(2,1)} %constant_dynamic-update-slice_fusion.refs_3_), channel_id=1, source_target_pairs={{0,4},{4,8},{8,12},{12,16},{16,20},{20,24},{24,28},{28,32},{32,36}... | collective-permute-start | bytes 1572872 | tf_op jit(solution)/shard_map/ppermute | solution.py:114
  5.9 27.8 %collective-permute-start.1 = (bf16[512,512]{1,0:T(8,128)(2,1)}, bf16[512,512]{1,0:T(8,128)(2,1)}, u32[]{:S(2)}, u32[]{:S(2)}) collective-permute-start(bf16[512,512]{1,0:T(8,128)(2,1)} %constant_dynamic-update-slice_fusion.refs_3_), channel_id=1, source_target_pairs={{0,8},{4,12},{8,16},{12,20},{16,24},{20,28},{24,32},{28,36},{32,40... | collective-permute-start | bytes 1572872 | tf_op jit(solution)/shard_map/ppermute | solution.py:114
  11.1 22.6 %collective-permute-start = (bf16[256,512]{1,0:T(8,128)(2,1)}, bf16[256,512]{1,0:T(8,128)(2,1)S(1)}, u32[]{:S(2)}, u32[]{:S(2)}) collective-permute-start(bf16[256,512]{1,0:T(8,128)(2,1)} %slice.73), channel_id=1, source_target_pairs={{0,12},{4,16},{8,20},{12,24},{16,28},{20,32},{24,36},{28,40},{32,4... | collective-permute-start | bytes 786440 | tf_op jit(solution)/shard_map/ppermute | solution.py:114
  17.3 5.3 %copy-start.3 = (s32[44,2]{0,1:T(2,128)S(1)}, s32[44,2]{0,1:T(2,128)}, u32[]{:S(2)}) copy-start(s32[44,2]{0,1:T(2,128)} %param.18) | copy-start | bytes 1060
  28.4 5.4 %copy-start.1 = (bf16[512,2048]{1,0:T(8,128)(2,1)S(1)}, bf16[512,2048]{1,0:T(8,128)(2,1)}, u32[]{:S(2)}) copy-start(bf16[512,2048]{1,0:T(8,128)(2,1)} %q_ref.1) | copy-start | bytes 6291460
  75.8 8.5 %copy-start.2 = (f32[512,2048]{1,0:T(8,128)S(1)}, f32[512,2048]{1,0:T(8,128)}, u32[]{:S(2)}) copy-start(f32[512,2048]{1,0:T(8,128)} %get-tuple-element.17) | copy-start | bytes 12582916
  78.5 28.8 %collective-permute-start.5 = (bf16[256,512]{1,0:T(8,128)(2,1)S(1)}, bf16[256,512]{1,0:T(8,128)(2,1)S(1)}, u32[]{:S(2)}, u32[]{:S(2)}) collective-permute-start(bf16[256,512]{1,0:T(8,128)(2,1)S(1)} %slice.77), channel_id=1, source_target_pairs={{12,0},{16,4},{20,8},{24,12},{28,16},{32,20},{36,24},{40,28},{44,3... | collective-permute-start | bytes 786440 | tf_op jit(solution)/shard_map/ppermute | solution.py:114
  80.5 14.5 %collective-permute-start.3 = (bf16[512,512]{1,0:T(8,128)(2,1)S(1)}, bf16[512,512]{1,0:T(8,128)(2,1)S(1)}, u32[]{:S(2)}, u32[]{:S(2)}) collective-permute-start(bf16[512,512]{1,0:T(8,128)(2,1)S(1)} %get-tuple-element.19), channel_id=1, source_target_pairs={{4,0},{8,4},{12,8},{16,12},{20,16},{24,20},{28,24},{32,28},{36,32}... | collective-permute-start | bytes 1572872 | tf_op jit(solution)/shard_map/ppermute | solution.py:114
  82.4 23.5 %collective-permute-start.4 = (bf16[512,512]{1,0:T(8,128)(2,1)S(1)}, bf16[512,512]{1,0:T(8,128)(2,1)S(1)}, u32[]{:S(2)}, u32[]{:S(2)}) collective-permute-start(bf16[512,512]{1,0:T(8,128)(2,1)S(1)} %get-tuple-element.20), channel_id=1, source_target_pairs={{8,0},{12,4},{16,8},{20,12},{24,16},{28,20},{32,24},{36,28},{40,32... | collective-permute-start | bytes 1572872 | tf_op jit(solution)/shard_map/ppermute | solution.py:114

commit v7 on v6

--- a/solution.py
+++ b/solution.py
@@ -13,10 +13,10 @@
 TN = (((0,), (0,)), ((), ()))
 
 
-def pair_kernel(piece_starts, pairs_ref, q_ref, do_ref, norm_ref, delta_ref, qdoc_ref, qpos_ref,
+def pair_kernel(piece_starts, pairs_ref, q_ref, do_ref, o_ref, norm_ref, qdoc_ref, qpos_ref,
                 kdoc_ref, kpos_ref, *refs):
     piece_refs = refs[:len(piece_starts)]
-    dq_ref, dkv_ref = refs[len(piece_starts):]
+    dq_ref, dkv_ref, delta_ref = refs[len(piece_starts):]
     dq_ref[...] = jnp.zeros(dq_ref.shape, jnp.float32)
     dkv_ref[...] = jnp.zeros(dkv_ref.shape, jnp.float32)
     heads = norm_ref.shape[1] // BLOCK
@@ -24,6 +24,16 @@
     kv_heads = kv_features // HEAD_DIM
     group = heads // kv_heads
     scale = HEAD_DIM ** (-0.5)
+
+    def one_delta(qb, carry):
+        rows = pl.ds(pl.multiple_of(qb * BLOCK, BLOCK), BLOCK)
+        for h in range(heads):
+            cols = pl.ds(h * HEAD_DIM, HEAD_DIM)
+            prod = do_ref[rows, cols].astype(jnp.float32) * o_ref[rows, cols].astype(jnp.float32)
+            delta_ref[qb, :, pl.ds(h * BLOCK, BLOCK)] = jnp.sum(prod.T, axis=0, keepdims=True)
+        return carry
+
+    lax.fori_loop(0, q_ref.shape[0] // BLOCK, one_delta, 0)
 
     def body(i, carry):
         qb_raw = pairs_ref[2 * i]
@@ -55,7 +65,7 @@
             do = jnp.concatenate([do_ref[pl.ds(qrow, BLOCK), c] for c in head_cols], axis=0)
             group_cols = pl.ds(g * group * BLOCK, group * BLOCK)
             norm = norm_ref[pl.ds(qb, 1), group_cols]
-            dl = delta_ref[pl.ds(qb, 1), group_cols]
+            dl = delta_ref[qb, :, group_cols]
             scores = lax.dot_general(k, q, NT, preferred_element_type=jnp.float32) * scale
             weights = jnp.where(wide_allowed, jnp.exp(scores - norm), 0.0)
             weight_grads = lax.dot_general(v, do, NT, preferred_element_type=jnp.float32)
@@ -72,7 +82,7 @@
     lax.fori_loop(0, pairs_ref.shape[0] // 2, body, 0)
 
 
-def run_pairs(pairs, queries, outgrads, norms, deltas, query_pos, pieces, key_pos, doc_bounds):
+def run_pairs(pairs, queries, outgrads, outputs, norms, query_pos, pieces, key_pos, doc_bounds):
     q_doc = doc_index(query_pos, doc_bounds)
     k_doc = doc_index(key_pos, doc_bounds)
     tokens, features = queries.shape
@@ -85,7 +95,7 @@
     smem = pltpu.MemorySpace.SMEM
     args = (
         pairs.reshape(-1).astype(jnp.int32),
-        queries, outgrads, norms, deltas,
+        queries, outgrads, outputs, norms,
         q_doc, query_pos,
         k_doc.reshape(window, 1), key_pos.reshape(window, 1),
     ) + tuple(rows for _, rows in pieces)
@@ -99,6 +109,7 @@
         ),
         in_specs=specs,
         out_specs=(pl.BlockSpec(memory_space=vmem), pl.BlockSpec(memory_space=vmem)),
+        scratch_shapes=[pltpu.VMEM((blocks, 1, heads * BLOCK), jnp.float32)],
         compiler_params=pltpu.CompilerParams(vmem_limit_bytes=48 * 1024 * 1024),
     )(*args)
 
@@ -128,9 +139,6 @@
     heads = log_norm.shape[0]
     own_blocks = tokens // BLOCK
     offsets = jnp.arange(BLOCK, dtype=jnp.int32)
-    products = grad_out.astype(jnp.float32) * attn_out.astype(jnp.float32)
-    delta = jnp.sum(products.reshape(tokens, heads, HEAD_DIM), axis=2)
-    delta = delta.reshape(own_blocks, BLOCK, heads).transpose(0, 2, 1).reshape(own_blocks, heads * BLOCK)
     own_keyval = jnp.concatenate([key, value], axis=1)
     first_used = min(max(REACH * own_blocks - DOC_BLOCKS, 0), own_blocks) * BLOCK
     pieces = [(first_used // BLOCK, shifted(own_keyval[first_used:], "ctx", REACH))]
@@ -147,7 +155,7 @@
     ship_pairs = jnp.stack([ship_queries, ship_keys], axis=2).reshape(-1, 2)
     pairs = jnp.concatenate([local_pairs, ship_pairs], axis=0)
     query_grads, keyval_grads = run_pairs(
-        pairs, query, grad_out, log_norm, delta, query_pos,
+        pairs, query, grad_out, attn_out, log_norm, query_pos,
         pieces, key_pos, doc_bounds,
     )
     segments = keyval_grads.reshape(REACH + 1, own_blocks * BLOCK, 2 * kv_features)

time: 109 us -> 106 us (0.972)
  the two profiles are of different devices: /device:TPU:132 before, /device:TPU:84 now
where the time goes in v7:
time: 106 us; the launch traced here: 105 us
  starting transfers between devices  39.9 us (38%)
  waiting for transfers between devices  28.8 us (27%)
  Pallas kernels  20.1 us (19%)
  local copies, waits for them, and re-layouts  8.61 us (8%)
  other arithmetic  7.28 us (7%)
    ppermute x6, starting transfers between devices, shifted(): return lax.ppermute(shard, axis, pairs)  39.9 us
    ppermute x6, waiting for transfers between devices, shifted(): return lax.ppermute(shard, axis, pairs)  28.8 us
    pallas_call x1, Pallas kernels, run_pairs(): pl.pallas_call(kernel, out_shape=(jax.ShapeDtypeStruct((tokens, features)...  20.1 us
    another operation x2, other arithmetic  2.68 us
  transfers between devices with their start and end apart: 6, of which 2 were waited for; matrix products, arithmetic and copies ran while one was open for 8% of the time, Pallas kernels for 0%

profile of v7, /device:TPU:84, one launch (start us, length us, event | category | flops | bytes accessed | tf_op | source)
XLA Modules:
  0.0 105.5 jit_solution(3105226278788946688)
XLA Ops:
  0.7 1.8 %constant_dynamic-update-slice_fusion.1 = bf16[512,512]{1,0:T(8,128)(2,1)} fusion(bf16[512,256]{1,0:T(8,128)(2,1)} %param.12), kind=kLoop, calls=%fused_computation.11 | loop fusion | bytes 524288
  2.5 1.7 %constant_dynamic-update-slice_fusion.refs_3_ = bf16[512,512]{1,0:T(8,128)(2,1)} fusion(bf16[512,512]{1,0:T(8,128)(2,1)} %constant_dynamic-update-slice_fusion.1, bf16[512,256]{1,0:T(8,128)(2,1)} %param.13), kind=kLoop, calls=%fused_computation.10 | loop fusion | bytes 524288 | tf_op jit(solution)/shard_map/concatenate | solution.py:142
  4.1 1.9 %collective-permute-start.2 = (bf16[512,512]{1,0:T(8,128)(2,1)}, bf16[512,512]{1,0:T(8,128)(2,1)}, u32[]{:S(2)}, u32[]{:S(2)}) collective-permute-start(bf16[512,512]{1,0:T(8,128)(2,1)} %constant_dynamic-update-slice_fusion.refs_3_), channel_id=1, source_target_pairs={{0,4},{4,8},{8,12},{12,16},{16,20},{20,24},{24,28},{28,32},{32,36}... | collective-permute-start | bytes 1572872 | tf_op jit(solution)/shard_map/ppermute | solution.py:125
  6.1 3.2 %collective-permute-start.1 = (bf16[512,512]{1,0:T(8,128)(2,1)}, bf16[512,512]{1,0:T(8,128)(2,1)}, u32[]{:S(2)}, u32[]{:S(2)}) collective-permute-start(bf16[512,512]{1,0:T(8,128)(2,1)} %constant_dynamic-update-slice_fusion.refs_3_), channel_id=1, source_target_pairs={{0,8},{4,12},{8,16},{12,20},{16,24},{20,28},{24,32},{28,36},{32,40... | collective-permute-start | bytes 1572872 | tf_op jit(solution)/shard_map/ppermute | solution.py:125
  9.3 1.7 %slice.73 = bf16[256,512]{1,0:T(8,128)(2,1)} slice(bf16[512,512]{1,0:T(8,128)(2,1)} %constant_dynamic-update-slice_fusion.refs_3_), slice={[256:512], [0:512]} | slice | bytes 524288 | tf_op jit(solution)/shard_map/slice | solution.py:144
  10.9 4.5 %collective-permute-start = (bf16[256,512]{1,0:T(8,128)(2,1)}, bf16[256,512]{1,0:T(8,128)(2,1)S(1)}, u32[]{:S(2)}, u32[]{:S(2)}) collective-permute-start(bf16[256,512]{1,0:T(8,128)(2,1)} %slice.73), channel_id=1, source_target_pairs={{0,12},{4,16},{8,20},{12,24},{16,28},{20,32},{24,36},{28,40},{32,4... | collective-permute-start | bytes 786440 | tf_op jit(solution)/shard_map/ppermute | solution.py:125
  15.4 0.7 slice.64
  16.2 0.1 iota_add_fusion.2
  16.2 0.8 constant_dynamic-slice_fusion
  17.0 0.1 copy.19
  17.1 0.1 slice_reduce_fusion
  17.2 0.1 compare_select_fusion
  17.3 0.1 convert_reduce_fusion.1
  17.4 0.1 stack.9
  17.5 0.1 stack.10
  17.6 0.1 convert_reduce_fusion
  17.7 0.8 add_add_fusion
  18.5 0.1 copy.20
  18.6 0.1 reshape.92.pairs_ref
  18.7 0.4 copy.22.kdoc_ref
  19.1 0.1 iota_add_fusion.kpos_ref
  19.2 12.5 %collective-permute-done.refs_0_ = bf16[256,512]{1,0:T(8,128)(2,1)S(1)} collective-permute-done((bf16[256,512]{1,0:T(8,128)(2,1)}, bf16[256,512]{1,0:T(8,128)(2,1)S(1)}, u32[]{:S(2)}, u32[]{:S(2)}) %collective-permute-start) | collective-permute-done | bytes 262176 | tf_op jit(solution)/shard_map/ppermute | solution.py:125
  31.7 20.1 %shard_map.112 = (f32[512,2048]{1,0:T(8,128)}, f32[2048,512]{1,0:T(8,128)}) custom-call(s32[120]{0:T(128)S(1)} %reshape.92.pairs_ref, bf16[512,2048]{1,0:T(8,128)(2,1)S(1)} %copy-done.1, bf16[512,2048]{1,0:T(8,128)(2,1)} %do_ref.1, bf16[512,2048]{1,0:T(8,128)(2,1)} %o_ref.1, f32[4,2048]{1,0:T(4,128)S(1)} %bitcast.16, s32[4,128]{1,0:T(4,128)S(1)} %bitcast.17, ...), custom_call_target="tpu_custom_call" | custom-call | tf_op jit(solution)/shard_map/pallas_call | solution.py:104
  51.8 2.6 %convert.9 = bf16[2048,512]{1,0:T(8,128)(2,1)S(1)} convert(f32[2048,512]{1,0:T(8,128)} %get-tuple-element.18) | non-fusion elementwise | flops 1048576 | bytes 6291456 | tf_op jit(solution)/shard_map/convert.4
  54.5 7.9 %collective-permute-start.5 = (bf16[256,512]{1,0:T(8,128)(2,1)S(1)}, bf16[256,512]{1,0:T(8,128)(2,1)S(1)}, u32[]{:S(2)}, u32[]{:S(2)}) collective-permute-start(bf16[256,512]{1,0:T(8,128)(2,1)S(1)} %slice.77), channel_id=1, source_target_pairs={{12,0},{16,4},{20,8},{24,12},{28,16},{32,20},{36,24},{40,28},{44,3... | collective-permute-start | bytes 786440 | tf_op jit(solution)/shard_map/ppermute | solution.py:125
  62.4 7.8 %collective-permute-start.3 = (bf16[512,512]{1,0:T(8,128)(2,1)S(1)}, bf16[512,512]{1,0:T(8,128)(2,1)S(1)}, u32[]{:S(2)}, u32[]{:S(2)}) collective-permute-start(bf16[512,512]{1,0:T(8,128)(2,1)S(1)} %get-tuple-element.19), channel_id=1, source_target_pairs={{4,0},{8,4},{12,8},{16,12},{20,16},{24,20},{28,24},{32,28},{36,32}... | collective-permute-start | bytes 1572872 | tf_op jit(solution)/shard_map/ppermute | solution.py:125
  70.2 14.6 %collective-permute-start.4 = (bf16[512,512]{1,0:T(8,128)(2,1)S(1)}, bf16[512,512]{1,0:T(8,128)(2,1)S(1)}, u32[]{:S(2)}, u32[]{:S(2)}) collective-permute-start(bf16[512,512]{1,0:T(8,128)(2,1)S(1)} %get-tuple-element.20), channel_id=1, source_target_pairs={{8,0},{12,4},{16,8},{20,12},{24,16},{28,20},{32,24},{36,28},{40,32... | collective-permute-start | bytes 1572872 | tf_op jit(solution)/shard_map/ppermute | solution.py:125
  84.8 1.8 %multiply_convert_fusion = bf16[512,2048]{1,0:T(8,128)(2,1)} fusion(f32[512,2048]{1,0:T(8,128)S(1)} %copy-done.2), kind=kLoop, calls=%fused_computation | loop fusion | flops 2097152 | bytes 6291456 | tf_op jit(solution)/shard_map/convert_element_type | solution.py:167
  86.7 16.3 %collective-permute-done.4 = bf16[512,512]{1,0:T(8,128)(2,1)S(1)} collective-permute-done((bf16[512,512]{1,0:T(8,128)(2,1)S(1)}, bf16[512,512]{1,0:T(8,128)(2,1)S(1)}, u32[]{:S(2)}, u32[]{:S(2)}) %collective-permute-start.4) | collective-permute-done | bytes 524320 | tf_op jit(solution)/shard_map/ppermute | solution.py:125
  103.0 1.4 %convert_add_fusion = f32[512,512]{1,0:T(8,128)S(1)} fusion(bf16[512,512]{1,0:T(8,128)(2,1)S(1)} %collective-permute-done.4, bf16[512,512]{1,0:T(8,128)(2,1)S(1)} %collective-permute-done.3, f32[2048,512]{1,0:T(8,128)} %get-tuple-element.18), kind=kLoop, calls=%fused_computation.1 | loop fusion | flops 1048576 | bytes 3145728 | tf_op jit(solution)/shard_map/add | solution.py:164
  104.4 0.1 fusion
  104.6 0.8 fusion.3
  (17 shorter events, 0.2 us)
Async XLA Ops:
  0.6 16.7 %copy-start = (f32[16,512]{1,0:T(8,128)S(1)}, f32[16,512]{1,0:T(8,128)}, u32[]{:S(2)}) copy-start(f32[16,512]{1,0:T(8,128)} %param.16) | copy-start | bytes 98308
  0.6 31.0 %copy-start.1 = (bf16[512,2048]{1,0:T(8,128)(2,1)S(1)}, bf16[512,2048]{1,0:T(8,128)(2,1)}, u32[]{:S(2)}) copy-start(bf16[512,2048]{1,0:T(8,128)(2,1)} %q_ref.1) | copy-start | bytes 6291460
  4.1 27.5 %collective-permute-start.2 = (bf16[512,512]{1,0:T(8,128)(2,1)}, bf16[512,512]{1,0:T(8,128)(2,1)}, u32[]{:S(2)}, u32[]{:S(2)}) collective-permute-start(bf16[512,512]{1,0:T(8,128)(2,1)} %constant_dynamic-update-slice_fusion.refs_3_), channel_id=1, source_target_pairs={{0,4},{4,8},{8,12},{12,16},{16,20},{20,24},{24,28},{28,32},{32,36}... | collective-permute-start | bytes 1572872 | tf_op jit(solution)/shard_map/ppermute | solution.py:125
  6.1 25.6 %collective-permute-start.1 = (bf16[512,512]{1,0:T(8,128)(2,1)}, bf16[512,512]{1,0:T(8,128)(2,1)}, u32[]{:S(2)}, u32[]{:S(2)}) collective-permute-start(bf16[512,512]{1,0:T(8,128)(2,1)} %constant_dynamic-update-slice_fusion.refs_3_), channel_id=1, source_target_pairs={{0,8},{4,12},{8,16},{12,20},{16,24},{20,28},{24,32},{28,36},{32,40... | collective-permute-start | bytes 1572872 | tf_op jit(solution)/shard_map/ppermute | solution.py:125
  10.9 20.7 %collective-permute-start = (bf16[256,512]{1,0:T(8,128)(2,1)}, bf16[256,512]{1,0:T(8,128)(2,1)S(1)}, u32[]{:S(2)}, u32[]{:S(2)}) collective-permute-start(bf16[256,512]{1,0:T(8,128)(2,1)} %slice.73), channel_id=1, source_target_pairs={{0,12},{4,16},{8,20},{12,24},{16,28},{20,32},{24,36},{28,40},{32,4... | collective-permute-start | bytes 786440 | tf_op jit(solution)/shard_map/ppermute | solution.py:125
  51.8 33.0 %copy-start.2 = (f32[512,2048]{1,0:T(8,128)S(1)}, f32[512,2048]{1,0:T(8,128)}, u32[]{:S(2)}) copy-start(f32[512,2048]{1,0:T(8,128)} %get-tuple-element.17) | copy-start | bytes 12582916
  54.5 49.9 %collective-permute-start.5 = (bf16[256,512]{1,0:T(8,128)(2,1)S(1)}, bf16[256,512]{1,0:T(8,128)(2,1)S(1)}, u32[]{:S(2)}, u32[]{:S(2)}) collective-permute-start(bf16[256,512]{1,0:T(8,128)(2,1)S(1)} %slice.77), channel_id=1, source_target_pairs={{12,0},{16,4},{20,8},{24,12},{28,16},{32,20},{36,24},{40,28},{44,3... | collective-permute-start | bytes 786440 | tf_op jit(solution)/shard_map/ppermute | solution.py:125
  62.4 24.3 %collective-permute-start.3 = (bf16[512,512]{1,0:T(8,128)(2,1)S(1)}, bf16[512,512]{1,0:T(8,128)(2,1)S(1)}, u32[]{:S(2)}, u32[]{:S(2)}) collective-permute-start(bf16[512,512]{1,0:T(8,128)(2,1)S(1)} %get-tuple-element.19), channel_id=1, source_target_pairs={{4,0},{8,4},{12,8},{16,12},{20,16},{24,20},{28,24},{32,28},{36,32}... | collective-permute-start | bytes 1572872 | tf_op jit(solution)/shard_map/ppermute | solution.py:125
  70.2 32.8 %collective-permute-start.4 = (bf16[512,512]{1,0:T(8,128)(2,1)S(1)}, bf16[512,512]{1,0:T(8,128)(2,1)S(1)}, u32[]{:S(2)}, u32[]{:S(2)}) collective-permute-start(bf16[512,512]{1,0:T(8,128)(2,1)S(1)} %get-tuple-element.20), channel_id=1, source_target_pairs={{8,0},{12,4},{16,8},{20,12},{24,16},{28,20},{32,24},{36,28},{40,32... | collective-permute-start | bytes 1572872 | tf_op jit(solution)/shard_map/ppermute | solution.py:125

commit v8 on v7

--- a/solution.py
+++ b/solution.py
@@ -13,7 +13,7 @@
 TN = (((0,), (0,)), ((), ()))
 
 
-def pair_kernel(piece_starts, pairs_ref, q_ref, do_ref, o_ref, norm_ref, qdoc_ref, qpos_ref,
+def pair_kernel(piece_starts, pairs_ref, whole_ref, q_ref, do_ref, o_ref, norm_ref, qdoc_ref, qpos_ref,
                 kdoc_ref, kpos_ref, *refs):
     piece_refs = refs[:len(piece_starts)]
     dq_ref, dkv_ref, delta_ref = refs[len(piece_starts):]
@@ -41,22 +41,26 @@
         live = (qb_raw >= 0) & (kb_raw >= 0)
         qb = jnp.maximum(qb_raw, 0)
         kb = jnp.maximum(kb_raw, 0)
+        whole = whole_ref[i] > 0
         for start, kv_ref in zip(piece_starts, piece_refs):
             end = start + kv_ref.shape[0] // BLOCK
             inside = live & (kb >= start) & (kb < end)
-            pl.when(inside)(functools.partial(one_pair, qb, kb, kv_ref, start))
+            pl.when(inside & whole)(functools.partial(one_pair, qb, kb, kv_ref, start, False))
+            pl.when(inside & jnp.logical_not(whole))(
+                functools.partial(one_pair, qb, kb, kv_ref, start, True))
         return carry
 
-    def one_pair(qb, kb, kv_ref, start):
+    def one_pair(qb, kb, kv_ref, start, masked):
         local_row = pl.multiple_of((kb - start) * BLOCK, BLOCK)
         qrow = pl.multiple_of(qb * BLOCK, BLOCK)
         krow = pl.multiple_of(kb * BLOCK, BLOCK)
-        qdoc = qdoc_ref[pl.ds(qb, 1), :]
-        qpos = qpos_ref[pl.ds(qb, 1), :]
-        kdoc = kdoc_ref[pl.ds(krow, BLOCK), :]
-        kpos = kpos_ref[pl.ds(krow, BLOCK), :]
-        allowed = (kdoc == qdoc) & (kpos <= qpos)
-        wide_allowed = jnp.concatenate([allowed] * group, axis=1)
+        if masked:
+            qdoc = qdoc_ref[pl.ds(qb, 1), :]
+            qpos = qpos_ref[pl.ds(qb, 1), :]
+            kdoc = kdoc_ref[pl.ds(krow, BLOCK), :]
+            kpos = kpos_ref[pl.ds(krow, BLOCK), :]
+            allowed = (kdoc == qdoc) & (kpos <= qpos)
+            wide_allowed = jnp.concatenate([allowed] * group, axis=1)
         for g in range(kv_heads):
             k = kv_ref[pl.ds(local_row, BLOCK), pl.ds(g * HEAD_DIM, HEAD_DIM)]
             v = kv_ref[pl.ds(local_row, BLOCK), pl.ds(kv_features + g * HEAD_DIM, HEAD_DIM)]
@@ -67,7 +71,9 @@
             norm = norm_ref[pl.ds(qb, 1), group_cols]
             dl = delta_ref[qb, :, group_cols]
             scores = lax.dot_general(k, q, NT, preferred_element_type=jnp.float32) * scale
-            weights = jnp.where(wide_allowed, jnp.exp(scores - norm), 0.0)
+            weights = jnp.exp(scores - norm)
+            if masked:
+                weights = jnp.where(wide_allowed, weights, 0.0)
             weight_grads = lax.dot_general(v, do, NT, preferred_element_type=jnp.float32)
             score_grads = (weights * (weight_grads - dl)).astype(jnp.bfloat16)
             weights_low = weights.astype(jnp.bfloat16)
@@ -93,13 +99,19 @@
     norms = norms.reshape(heads, blocks, BLOCK).transpose(1, 0, 2).reshape(blocks, heads * BLOCK)
     vmem = pltpu.MemorySpace.VMEM
     smem = pltpu.MemorySpace.SMEM
+    query_block = jnp.maximum(pairs[:, 0], 0)
+    key_first = jnp.maximum(pairs[:, 1], 0) * BLOCK
+    whole = (k_doc[key_first] == q_doc[query_block, BLOCK - 1]) & (
+        key_pos[key_first + BLOCK - 1] <= query_pos[query_block, 0]
+    )
     args = (
         pairs.reshape(-1).astype(jnp.int32),
+        whole.astype(jnp.int32),
         queries, outgrads, outputs, norms,
         q_doc, query_pos,
         k_doc.reshape(window, 1), key_pos.reshape(window, 1),
     ) + tuple(rows for _, rows in pieces)
-    specs = [pl.BlockSpec(memory_space=smem)] + [pl.BlockSpec(memory_space=vmem)] * (len(args) - 1)
+    specs = [pl.BlockSpec(memory_space=smem)] * 2 + [pl.BlockSpec(memory_space=vmem)] * (len(args) - 2)
     kernel = functools.partial(pair_kernel, tuple(start for start, _ in pieces))
     return pl.pallas_call(
         kernel,

time: 106 us -> 107 us (level)
  the two profiles are of different devices: /device:TPU:84 before, /device:TPU:102 now
where the time goes in v8:
time: 107 us; the launch traced here: 106 us
  Pallas kernels  37.5 us (35%)
  starting transfers between devices  24.5 us (23%)
  waiting for transfers between devices  24.2 us (23%)
  local copies, waits for them, and re-layouts  12.1 us (11%)
  other arithmetic  7.31 us (7%)
    pallas_call x1, Pallas kernels, run_pairs(): pl.pallas_call(kernel, out_shape=(jax.ShapeDtypeStruct((tokens, features)...  37.5 us
    ppermute x6, starting transfers between devices, shifted(): return lax.ppermute(shard, axis, pairs)  24.5 us
    ppermute x6, waiting for transfers between devices, shifted(): return lax.ppermute(shard, axis, pairs)  24.2 us
    another operation x2, other arithmetic  2.68 us
  transfers between devices with their start and end apart: 6, of which 3 were waited for; matrix products, arithmetic and copies ran while one was open for 12% of the time, Pallas kernels for 0%

profile of v8, /device:TPU:102, one launch (start us, length us, event | category | flops | bytes accessed | tf_op | source)
XLA Modules:
  0.0 106.5 jit_solution(4464713935664930068)
XLA Ops:
  0.6 1.7 %constant_dynamic-update-slice_fusion.1 = bf16[512,512]{1,0:T(8,128)(2,1)} fusion(bf16[512,256]{1,0:T(8,128)(2,1)} %param.12), kind=kLoop, calls=%fused_computation.17 | loop fusion | bytes 524288
  2.3 1.7 %constant_dynamic-update-slice_fusion.refs_3_ = bf16[512,512]{1,0:T(8,128)(2,1)} fusion(bf16[512,512]{1,0:T(8,128)(2,1)} %constant_dynamic-update-slice_fusion.1, bf16[512,256]{1,0:T(8,128)(2,1)} %param.13), kind=kLoop, calls=%fused_computation.16 | loop fusion | bytes 524288 | tf_op jit(solution)/shard_map/concatenate | solution.py:154
  4.0 1.9 %collective-permute-start.2 = (bf16[512,512]{1,0:T(8,128)(2,1)}, bf16[512,512]{1,0:T(8,128)(2,1)}, u32[]{:S(2)}, u32[]{:S(2)}) collective-permute-start(bf16[512,512]{1,0:T(8,128)(2,1)} %constant_dynamic-update-slice_fusion.refs_3_), channel_id=1, source_target_pairs={{0,4},{4,8},{8,12},{12,16},{16,20},{20,24},{24,28},{28,32},{32,36}... | collective-permute-start | bytes 1572872 | tf_op jit(solution)/shard_map/ppermute | solution.py:137
  5.9 3.5 %collective-permute-start.1 = (bf16[512,512]{1,0:T(8,128)(2,1)}, bf16[512,512]{1,0:T(8,128)(2,1)}, u32[]{:S(2)}, u32[]{:S(2)}) collective-permute-start(bf16[512,512]{1,0:T(8,128)(2,1)} %constant_dynamic-update-slice_fusion.refs_3_), channel_id=1, source_target_pairs={{0,8},{4,12},{8,16},{12,20},{16,24},{20,28},{24,32},{28,36},{32,40... | collective-permute-start | bytes 1572872 | tf_op jit(solution)/shard_map/ppermute | solution.py:137
  9.4 1.7 %slice.89 = bf16[256,512]{1,0:T(8,128)(2,1)} slice(bf16[512,512]{1,0:T(8,128)(2,1)} %constant_dynamic-update-slice_fusion.refs_3_), slice={[256:512], [0:512]} | slice | bytes 524288 | tf_op jit(solution)/shard_map/slice | solution.py:156
  11.1 4.2 %collective-permute-start = (bf16[256,512]{1,0:T(8,128)(2,1)}, bf16[256,512]{1,0:T(8,128)(2,1)S(1)}, u32[]{:S(2)}, u32[]{:S(2)}) collective-permute-start(bf16[256,512]{1,0:T(8,128)(2,1)} %slice.89), channel_id=1, source_target_pairs={{0,12},{4,16},{8,20},{12,24},{16,28},{20,32},{24,36},{28,40},{32,4... | collective-permute-start | bytes 786440 | tf_op jit(solution)/shard_map/ppermute | solution.py:137
  15.3 0.7 slice.70
  16.1 0.1 convert_reduce_fusion.1
  16.2 0.1 convert_reduce_fusion
  16.3 0.8 constant_dynamic-slice_fusion
  17.1 0.1 copy.19
  17.2 0.1 slice_reduce_fusion
  17.5 0.8 add_add_fusion
  18.4 0.8 gather_fusion.2
  19.1 1.1 gather_fusion.1
  20.2 1.1 gather_fusion.3
  21.3 0.8 gather_fusion
  22.1 0.1 copy.20
  22.2 0.1 reshape.92.pairs_ref
  22.3 0.4 copy.22.kdoc_ref
  22.8 4.8 %collective-permute-done.refs_0_ = bf16[256,512]{1,0:T(8,128)(2,1)S(1)} collective-permute-done((bf16[256,512]{1,0:T(8,128)(2,1)}, bf16[256,512]{1,0:T(8,128)(2,1)S(1)}, u32[]{:S(2)}, u32[]{:S(2)}) %collective-permute-start) | collective-permute-done | bytes 262176 | tf_op jit(solution)/shard_map/ppermute | solution.py:137
  27.6 0.2 collective-permute-done.1.refs_1_
  27.8 37.5 %shard_map.112 = (f32[512,2048]{1,0:T(8,128)}, f32[2048,512]{1,0:T(8,128)}) custom-call(s32[120]{0:T(128)S(1)} %reshape.92.pairs_ref, s32[60]{0:T(128)S(1)} %and_convert_fusion.whole_ref, bf16[512,2048]{1,0:T(8,128)(2,1)S(1)} %copy-done.1, bf16[512,2048]{1,0:T(8,128)(2,1)} %do_ref.1, bf16[512,2048]{1,0:T(8,128)(2,1)} %o_ref.1, f32[4,2048]{1,0:T(4,128)S(1)} %bitcast.26, ...), custom_call_target="tpu_custom_call" | custom-call | tf_op jit(solution)/shard_map/pallas_call | solution.py:116
  65.4 2.6 %convert.9 = bf16[2048,512]{1,0:T(8,128)(2,1)S(1)} convert(f32[2048,512]{1,0:T(8,128)} %get-tuple-element.18) | non-fusion elementwise | flops 1048576 | bytes 6291456 | tf_op jit(solution)/shard_map/convert.4
  68.1 1.9 %collective-permute-start.5 = (bf16[256,512]{1,0:T(8,128)(2,1)S(1)}, bf16[256,512]{1,0:T(8,128)(2,1)S(1)}, u32[]{:S(2)}, u32[]{:S(2)}) collective-permute-start(bf16[256,512]{1,0:T(8,128)(2,1)S(1)} %slice.93), channel_id=1, source_target_pairs={{12,0},{16,4},{20,8},{24,12},{28,16},{32,20},{36,24},{40,28},{44,3... | collective-permute-start | bytes 786440 | tf_op jit(solution)/shard_map/ppermute | solution.py:137
  70.0 1.9 %collective-permute-start.3 = (bf16[512,512]{1,0:T(8,128)(2,1)S(1)}, bf16[512,512]{1,0:T(8,128)(2,1)S(1)}, u32[]{:S(2)}, u32[]{:S(2)}) collective-permute-start(bf16[512,512]{1,0:T(8,128)(2,1)S(1)} %get-tuple-element.19), channel_id=1, source_target_pairs={{4,0},{8,4},{12,8},{16,12},{20,16},{24,20},{28,24},{32,28},{36,32}... | collective-permute-start | bytes 1572872 | tf_op jit(solution)/shard_map/ppermute | solution.py:137
  71.9 11.0 %collective-permute-start.4 = (bf16[512,512]{1,0:T(8,128)(2,1)S(1)}, bf16[512,512]{1,0:T(8,128)(2,1)S(1)}, u32[]{:S(2)}, u32[]{:S(2)}) collective-permute-start(bf16[512,512]{1,0:T(8,128)(2,1)S(1)} %get-tuple-element.20), channel_id=1, source_target_pairs={{8,0},{12,4},{16,8},{20,12},{24,16},{28,20},{32,24},{36,28},{40,32... | collective-permute-start | bytes 1572872 | tf_op jit(solution)/shard_map/ppermute | solution.py:137
  83.0 1.8 %multiply_convert_fusion = bf16[512,2048]{1,0:T(8,128)(2,1)} fusion(f32[512,2048]{1,0:T(8,128)S(1)} %copy-done.2), kind=kLoop, calls=%fused_computation.4 | loop fusion | flops 2097152 | bytes 6291456 | tf_op jit(solution)/shard_map/convert_element_type | solution.py:179
  84.9 19.1 %collective-permute-done.4 = bf16[512,512]{1,0:T(8,128)(2,1)S(1)} collective-permute-done((bf16[512,512]{1,0:T(8,128)(2,1)S(1)}, bf16[512,512]{1,0:T(8,128)(2,1)S(1)}, u32[]{:S(2)}, u32[]{:S(2)}) %collective-permute-start.4) | collective-permute-done | bytes 524320 | tf_op jit(solution)/shard_map/ppermute | solution.py:137
  104.0 1.4 %convert_add_fusion = f32[512,512]{1,0:T(8,128)S(1)} fusion(bf16[512,512]{1,0:T(8,128)(2,1)S(1)} %collective-permute-done.4, bf16[512,512]{1,0:T(8,128)(2,1)S(1)} %collective-permute-done.3, f32[2048,512]{1,0:T(8,128)} %get-tuple-element.18), kind=kLoop, calls=%fused_computation.5 | loop fusion | flops 1048576 | bytes 3145728 | tf_op jit(solution)/shard_map/add | solution.py:176
  105.4 0.1 fusion
  105.6 0.8 fusion.6
  (24 shorter events, 0.6 us)
Async XLA Ops:
  0.6 17.7 %copy-start = (f32[16,512]{1,0:T(8,128)S(1)}, f32[16,512]{1,0:T(8,128)}, u32[]{:S(2)}) copy-start(f32[16,512]{1,0:T(8,128)} %param.16) | copy-start | bytes 98308
  4.0 23.6 %collective-permute-start.2 = (bf16[512,512]{1,0:T(8,128)(2,1)}, bf16[512,512]{1,0:T(8,128)(2,1)}, u32[]{:S(2)}, u32[]{:S(2)}) collective-permute-start(bf16[512,512]{1,0:T(8,128)(2,1)} %constant_dynamic-update-slice_fusion.refs_3_), channel_id=1, source_target_pairs={{0,4},{4,8},{8,12},{12,16},{16,20},{20,24},{24,28},{28,32},{32,36}... | collective-permute-start | bytes 1572872 | tf_op jit(solution)/shard_map/ppermute | solution.py:137
  5.9 21.9 %collective-permute-start.1 = (bf16[512,512]{1,0:T(8,128)(2,1)}, bf16[512,512]{1,0:T(8,128)(2,1)}, u32[]{:S(2)}, u32[]{:S(2)}) collective-permute-start(bf16[512,512]{1,0:T(8,128)(2,1)} %constant_dynamic-update-slice_fusion.refs_3_), channel_id=1, source_target_pairs={{0,8},{4,12},{8,16},{12,20},{16,24},{20,28},{24,32},{28,36},{32,40... | collective-permute-start | bytes 1572872 | tf_op jit(solution)/shard_map/ppermute | solution.py:137
  11.1 16.5 %collective-permute-start = (bf16[256,512]{1,0:T(8,128)(2,1)}, bf16[256,512]{1,0:T(8,128)(2,1)S(1)}, u32[]{:S(2)}, u32[]{:S(2)}) collective-permute-start(bf16[256,512]{1,0:T(8,128)(2,1)} %slice.89), channel_id=1, source_target_pairs={{0,12},{4,16},{8,20},{12,24},{16,28},{20,32},{24,36},{28,40},{32,4... | collective-permute-start | bytes 786440 | tf_op jit(solution)/shard_map/ppermute | solution.py:137
  18.4 9.5 %copy-start.1 = (bf16[512,2048]{1,0:T(8,128)(2,1)S(1)}, bf16[512,2048]{1,0:T(8,128)(2,1)}, u32[]{:S(2)}) copy-start(bf16[512,2048]{1,0:T(8,128)(2,1)} %q_ref.1) | copy-start | bytes 6291460
  65.4 17.6 %copy-start.2 = (f32[512,2048]{1,0:T(8,128)S(1)}, f32[512,2048]{1,0:T(8,128)}, u32[]{:S(2)}) copy-start(f32[512,2048]{1,0:T(8,128)} %get-tuple-element.17) | copy-start | bytes 12582916
  68.1 37.3 %collective-permute-start.5 = (bf16[256,512]{1,0:T(8,128)(2,1)S(1)}, bf16[256,512]{1,0:T(8,128)(2,1)S(1)}, u32[]{:S(2)}, u32[]{:S(2)}) collective-permute-start(bf16[256,512]{1,0:T(8,128)(2,1)S(1)} %slice.93), channel_id=1, source_target_pairs={{12,0},{16,4},{20,8},{24,12},{28,16},{32,20},{36,24},{40,28},{44,3... | collective-permute-start | bytes 786440 | tf_op jit(solution)/shard_map/ppermute | solution.py:137
  70.0 14.8 %collective-permute-start.3 = (bf16[512,512]{1,0:T(8,128)(2,1)S(1)}, bf16[512,512]{1,0:T(8,128)(2,1)S(1)}, u32[]{:S(2)}, u32[]{:S(2)}) collective-permute-start(bf16[512,512]{1,0:T(8,128)(2,1)S(1)} %get-tuple-element.19), channel_id=1, source_target_pairs={{4,0},{8,4},{12,8},{16,12},{20,16},{24,20},{28,24},{32,28},{36,32}... | collective-permute-start | bytes 1572872 | tf_op jit(solution)/shard_map/ppermute | solution.py:137
  71.9 32.0 %collective-permute-start.4 = (bf16[512,512]{1,0:T(8,128)(2,1)S(1)}, bf16[512,512]{1,0:T(8,128)(2,1)S(1)}, u32[]{:S(2)}, u32[]{:S(2)}) collective-permute-start(bf16[512,512]{1,0:T(8,128)(2,1)S(1)} %get-tuple-element.20), channel_id=1, source_target_pairs={{8,0},{12,4},{16,8},{20,12},{24,16},{28,20},{32,24},{36,28},{40,32... | collective-permute-start | bytes 1572872 | tf_op jit(solution)/shard_map/ppermute | solution.py:137

commit v9 on v7

--- a/solution.py
+++ b/solution.py
@@ -16,7 +16,7 @@
 def pair_kernel(piece_starts, pairs_ref, q_ref, do_ref, o_ref, norm_ref, qdoc_ref, qpos_ref,
                 kdoc_ref, kpos_ref, *refs):
     piece_refs = refs[:len(piece_starts)]
-    dq_ref, dkv_ref, delta_ref = refs[len(piece_starts):]
+    dq_out, far_out, own_out, delta_ref, dq_ref, dkv_ref = refs[len(piece_starts):]
     dq_ref[...] = jnp.zeros(dq_ref.shape, jnp.float32)
     dkv_ref[...] = jnp.zeros(dkv_ref.shape, jnp.float32)
     heads = norm_ref.shape[1] // BLOCK
@@ -81,6 +81,16 @@
 
     lax.fori_loop(0, pairs_ref.shape[0] // 2, body, 0)
 
+    def finish_query(qb, carry):
+        rows = pl.ds(pl.multiple_of(qb * BLOCK, BLOCK), BLOCK)
+        dq_out[rows, :] = (dq_ref[rows, :] * scale).astype(dq_out.dtype)
+        return carry
+
+    lax.fori_loop(0, dq_ref.shape[0] // BLOCK, finish_query, 0)
+    far_rows = far_out.shape[0]
+    far_out[...] = dkv_ref[pl.ds(0, far_rows), :].astype(far_out.dtype)
+    own_out[...] = dkv_ref[pl.ds(far_rows, own_out.shape[0]), :]
+
 
 def run_pairs(pairs, queries, outgrads, outputs, norms, query_pos, pieces, key_pos, doc_bounds):
     q_doc = doc_index(query_pos, doc_bounds)
@@ -88,6 +98,7 @@
     tokens, features = queries.shape
     window = key_pos.shape[0]
     both = pieces[0][1].shape[1]
+    own_rows = pieces[-1][1].shape[0]
     heads = norms.shape[0]
     blocks = tokens // BLOCK
     norms = norms.reshape(heads, blocks, BLOCK).transpose(1, 0, 2).reshape(blocks, heads * BLOCK)
@@ -104,12 +115,17 @@
     return pl.pallas_call(
         kernel,
         out_shape=(
-            jax.ShapeDtypeStruct((tokens, features), jnp.float32),
-            jax.ShapeDtypeStruct((window, both), jnp.float32),
+            jax.ShapeDtypeStruct((tokens, features), jnp.bfloat16),
+            jax.ShapeDtypeStruct((window - own_rows, both), jnp.bfloat16),
+            jax.ShapeDtypeStruct((own_rows, both), jnp.float32),
         ),
         in_specs=specs,
-        out_specs=(pl.BlockSpec(memory_space=vmem), pl.BlockSpec(memory_space=vmem)),
-        scratch_shapes=[pltpu.VMEM((blocks, 1, heads * BLOCK), jnp.float32)],
+        out_specs=tuple(pl.BlockSpec(memory_space=vmem) for _ in range(3)),
+        scratch_shapes=[
+            pltpu.VMEM((blocks, 1, heads * BLOCK), jnp.float32),
+            pltpu.VMEM((tokens, features), jnp.float32),
+            pltpu.VMEM((window, both), jnp.float32),
+        ],
         compiler_params=pltpu.CompilerParams(vmem_limit_bytes=48 * 1024 * 1024),
     )(*args)
 
@@ -154,17 +170,15 @@
     ship_queries = jnp.where(ship_keys >= 0, own_ship[:, :1], -1)
     ship_pairs = jnp.stack([ship_queries, ship_keys], axis=2).reshape(-1, 2)
     pairs = jnp.concatenate([local_pairs, ship_pairs], axis=0)
-    query_grads, keyval_grads = run_pairs(
+    grad_query, far_low, own_grads = run_pairs(
         pairs, query, grad_out, attn_out, log_norm, query_pos,
         pieces, key_pos, doc_bounds,
     )
-    segments = keyval_grads.reshape(REACH + 1, own_blocks * BLOCK, 2 * kv_features)
-    own_grads = segments[REACH]
+    segments = far_low.reshape(REACH, own_blocks * BLOCK, 2 * kv_features)
     for hop in range(1, REACH):
-        own_grads = own_grads + shifted(segments[REACH - hop].astype(jnp.bfloat16), "ctx", -hop)
-    far_grads = shifted(segments[0][first_used:].astype(jnp.bfloat16), "ctx", -REACH)
+        own_grads = own_grads + shifted(segments[REACH - hop], "ctx", -hop)
+    far_grads = shifted(segments[0][first_used:], "ctx", -REACH)
     own_grads = own_grads.at[first_used:].add(far_grads.astype(jnp.float32))
-    grad_query = (query_grads * HEAD_DIM ** (-0.5)).astype(jnp.bfloat16)
     grad_key = own_grads[:, :kv_features].astype(jnp.bfloat16)
     grad_value = own_grads[:, kv_features:].astype(jnp.bfloat16)
     return (grad_query, grad_key, grad_value)

time: 106 us -> 106 us (level)
  the two profiles are of different devices: /device:TPU:84 before, /device:TPU:117 now
where the time goes in v9:
time: 106 us; the launch traced here: 104 us
  waiting for transfers between devices  37.9 us (36%)
  starting transfers between devices  33.3 us (31%)
  Pallas kernels  23.2 us (22%)
  local copies, waits for them, and re-layouts  7.54 us (7%)
  other arithmetic  1.6 us (2%)
    ppermute x6, waiting for transfers between devices, shifted(): return lax.ppermute(shard, axis, pairs)  37.9 us
    ppermute x6, starting transfers between devices, shifted(): return lax.ppermute(shard, axis, pairs)  33.3 us
    pallas_call x1, Pallas kernels, run_pairs(): pl.pallas_call(kernel, out_shape=(jax.ShapeDtypeStruct((tokens, features)...  23.2 us
  transfers between devices with their start and end apart: 6, of which 4 were waited for; matrix products, arithmetic and copies ran while one was open for 5% of the time, Pallas kernels for 0%

profile of v9, /device:TPU:117, one launch (start us, length us, event | category | flops | bytes accessed | tf_op | source)
XLA Modules:
  0.0 104.3 jit_solution(14242684763345806041)
XLA Ops:
  0.6 1.0 constant_dynamic-update-slice_fusion.1
  1.6 1.0 constant_dynamic-update-slice_fusion.refs_3_
  2.6 3.5 %collective-permute-start.2 = (bf16[512,512]{1,0:T(8,128)(2,1)S(1)}, bf16[512,512]{1,0:T(8,128)(2,1)S(1)}, u32[]{:S(2)}, u32[]{:S(2)}) collective-permute-start(bf16[512,512]{1,0:T(8,128)(2,1)S(1)} %constant_dynamic-update-slice_fusion.refs_3_), channel_id=1, source_target_pairs={{0,4},{4,8},{8,12},{12,16},{16,20},{20,24},{24,28},{28,32},{32,36}... | collective-permute-start | bytes 1572872 | tf_op jit(solution)/shard_map/ppermute | solution.py:141
  6.1 4.4 %collective-permute-start.1 = (bf16[512,512]{1,0:T(8,128)(2,1)S(1)}, bf16[512,512]{1,0:T(8,128)(2,1)S(1)}, u32[]{:S(2)}, u32[]{:S(2)}) collective-permute-start(bf16[512,512]{1,0:T(8,128)(2,1)S(1)} %constant_dynamic-update-slice_fusion.refs_3_), channel_id=1, source_target_pairs={{0,8},{4,12},{8,16},{12,20},{16,24},{20,28},{24,32},{28,36},{32,40... | collective-permute-start | bytes 1572872 | tf_op jit(solution)/shard_map/ppermute | solution.py:141
  10.5 2.6 %collective-permute-start = (bf16[256,512]{1,0:T(8,128)(2,1)S(1)}, bf16[256,512]{1,0:T(8,128)(2,1)S(1)}, u32[]{:S(2)}, u32[]{:S(2)}) collective-permute-start(bf16[256,512]{1,0:T(8,128)(2,1)S(1)} %slice.65), channel_id=1, source_target_pairs={{0,12},{4,16},{8,20},{12,24},{16,28},{20,32},{24,36},{28,40},{32,4... | collective-permute-start | bytes 786440 | tf_op jit(solution)/shard_map/ppermute | solution.py:141
  13.2 0.7 slice.57
  14.0 0.8 constant_dynamic-slice_fusion
  14.7 0.1 copy.19
  14.8 0.1 slice_reduce_fusion
  14.9 0.1 compare_select_fusion
  15.0 0.1 convert_reduce_fusion.1
  15.1 0.1 stack.9
  15.2 0.1 stack.10
  15.3 0.1 convert_reduce_fusion
  15.4 0.8 add_add_fusion
  16.2 0.1 copy.20
  16.3 0.1 reshape.90.pairs_ref
  16.5 0.4 copy.22.kdoc_ref
  16.8 0.1 iota_add_fusion.kpos_ref
  16.9 9.9 %collective-permute-done.refs_0_ = bf16[256,512]{1,0:T(8,128)(2,1)S(1)} collective-permute-done((bf16[256,512]{1,0:T(8,128)(2,1)S(1)}, bf16[256,512]{1,0:T(8,128)(2,1)S(1)}, u32[]{:S(2)}, u32[]{:S(2)}) %collective-permute-start) | collective-permute-done | bytes 262176 | tf_op jit(solution)/shard_map/ppermute | solution.py:141
  26.8 3.3 %collective-permute-done.1.refs_1_ = bf16[512,512]{1,0:T(8,128)(2,1)S(1)} collective-permute-done((bf16[512,512]{1,0:T(8,128)(2,1)S(1)}, bf16[512,512]{1,0:T(8,128)(2,1)S(1)}, u32[]{:S(2)}, u32[]{:S(2)}) %collective-permute-start.1) | collective-permute-done | bytes 524320 | tf_op jit(solution)/shard_map/ppermute | solution.py:141
  30.2 23.2 %shard_map.112 = (bf16[512,2048]{1,0:T(8,128)(2,1)}, bf16[1536,512]{1,0:T(8,128)(2,1)}, f32[512,512]{1,0:T(8,128)S(1)}) custom-call(s32[120]{0:T(128)S(1)} %reshape.90.pairs_ref, bf16[512,2048]{1,0:T(8,128)(2,1)} %q_ref.1, bf16[512,2048]{1,0:T(8,128)(2,1)} %do_ref.1, bf16[512,2048]{1,0:T(8,128)(2,1)} %o_ref.1, f32[4,2048]{1,0:T(4,128)S(1)} %bitcast.16, ...), custom_call_target="tpu_custom_call" | custom-call | tf_op jit(solution)/shard_map/pallas_call | solution.py:115
  53.3 1.3 %fusion.2 = (bf16[512,512]{1,0:T(8,128)(2,1)S(1)}, bf16[512,512]{1,0:T(8,128)(2,1)S(1)}) fusion(bf16[1536,512]{1,0:T(8,128)(2,1)} %get-tuple-element.20), kind=kLoop, calls=%fused_computation.18 | loop fusion | bytes 2097152 | tf_op jit(solution)/shard_map/slice | solution.py:179
  54.6 1.9 %collective-permute-start.3 = (bf16[512,512]{1,0:T(8,128)(2,1)S(1)}, bf16[512,512]{1,0:T(8,128)(2,1)S(1)}, u32[]{:S(2)}, u32[]{:S(2)}) collective-permute-start(bf16[512,512]{1,0:T(8,128)(2,1)S(1)} %get-tuple-element.21), channel_id=1, source_target_pairs={{4,0},{8,4},{12,8},{16,12},{20,16},{24,20},{28,24},{32,28},{36,32}... | collective-permute-start | bytes 1572872 | tf_op jit(solution)/shard_map/ppermute | solution.py:141
  56.5 15.6 %collective-permute-start.4 = (bf16[512,512]{1,0:T(8,128)(2,1)S(1)}, bf16[512,512]{1,0:T(8,128)(2,1)S(1)}, u32[]{:S(2)}, u32[]{:S(2)}) collective-permute-start(bf16[512,512]{1,0:T(8,128)(2,1)S(1)} %get-tuple-element.22), channel_id=1, source_target_pairs={{8,0},{12,4},{16,8},{20,12},{24,16},{28,20},{32,24},{36,28},{40,32... | collective-permute-start | bytes 1572872 | tf_op jit(solution)/shard_map/ppermute | solution.py:141
  72.2 1.0 slice.62
  73.1 5.3 %collective-permute-start.5 = (bf16[256,512]{1,0:T(8,128)(2,1)S(1)}, bf16[256,512]{1,0:T(8,128)(2,1)S(1)}, u32[]{:S(2)}, u32[]{:S(2)}) collective-permute-start(bf16[256,512]{1,0:T(8,128)(2,1)S(1)} %slice.62), channel_id=1, source_target_pairs={{12,0},{16,4},{20,8},{24,12},{28,16},{32,20},{36,24},{40,28},{44,3... | collective-permute-start | bytes 786440 | tf_op jit(solution)/shard_map/ppermute | solution.py:141
  78.5 7.8 %collective-permute-done.4 = bf16[512,512]{1,0:T(8,128)(2,1)S(1)} collective-permute-done((bf16[512,512]{1,0:T(8,128)(2,1)S(1)}, bf16[512,512]{1,0:T(8,128)(2,1)S(1)}, u32[]{:S(2)}, u32[]{:S(2)}) %collective-permute-start.4) | collective-permute-done | bytes 524320 | tf_op jit(solution)/shard_map/ppermute | solution.py:141
  86.2 0.2 convert_add_fusion
  86.4 16.8 %collective-permute-done.5 = bf16[256,512]{1,0:T(8,128)(2,1)S(1)} collective-permute-done((bf16[256,512]{1,0:T(8,128)(2,1)S(1)}, bf16[256,512]{1,0:T(8,128)(2,1)S(1)}, u32[]{:S(2)}, u32[]{:S(2)}) %collective-permute-start.5) | collective-permute-done | bytes 262176 | tf_op jit(solution)/shard_map/ppermute | solution.py:141
  103.3 0.1 fusion
  103.5 0.8 fusion.3
  (11 shorter events, 0.2 us)
Async XLA Ops:
  0.6 14.4 %copy-start = (f32[16,512]{1,0:T(8,128)S(1)}, f32[16,512]{1,0:T(8,128)}, u32[]{:S(2)}) copy-start(f32[16,512]{1,0:T(8,128)} %param.16) | copy-start | bytes 98308
  2.6 24.2 %collective-permute-start.2 = (bf16[512,512]{1,0:T(8,128)(2,1)S(1)}, bf16[512,512]{1,0:T(8,128)(2,1)S(1)}, u32[]{:S(2)}, u32[]{:S(2)}) collective-permute-start(bf16[512,512]{1,0:T(8,128)(2,1)S(1)} %constant_dynamic-update-slice_fusion.refs_3_), channel_id=1, source_target_pairs={{0,4},{4,8},{8,12},{12,16},{16,20},{20,24},{24,28},{28,32},{32,36}... | collective-permute-start | bytes 1572872 | tf_op jit(solution)/shard_map/ppermute | solution.py:141
  6.1 24.1 %collective-permute-start.1 = (bf16[512,512]{1,0:T(8,128)(2,1)S(1)}, bf16[512,512]{1,0:T(8,128)(2,1)S(1)}, u32[]{:S(2)}, u32[]{:S(2)}) collective-permute-start(bf16[512,512]{1,0:T(8,128)(2,1)S(1)} %constant_dynamic-update-slice_fusion.refs_3_), channel_id=1, source_target_pairs={{0,8},{4,12},{8,16},{12,20},{16,24},{20,28},{24,32},{28,36},{32,40... | collective-permute-start | bytes 1572872 | tf_op jit(solution)/shard_map/ppermute | solution.py:141
  10.5 16.3 %collective-permute-start = (bf16[256,512]{1,0:T(8,128)(2,1)S(1)}, bf16[256,512]{1,0:T(8,128)(2,1)S(1)}, u32[]{:S(2)}, u32[]{:S(2)}) collective-permute-start(bf16[256,512]{1,0:T(8,128)(2,1)S(1)} %slice.65), channel_id=1, source_target_pairs={{0,12},{4,16},{8,20},{12,24},{16,28},{20,32},{24,36},{28,40},{32,4... | collective-permute-start | bytes 786440 | tf_op jit(solution)/shard_map/ppermute | solution.py:141
  54.6 23.8 %collective-permute-start.3 = (bf16[512,512]{1,0:T(8,128)(2,1)S(1)}, bf16[512,512]{1,0:T(8,128)(2,1)S(1)}, u32[]{:S(2)}, u32[]{:S(2)}) collective-permute-start(bf16[512,512]{1,0:T(8,128)(2,1)S(1)} %get-tuple-element.21), channel_id=1, source_target_pairs={{4,0},{8,4},{12,8},{16,12},{20,16},{24,20},{28,24},{32,28},{36,32}... | collective-permute-start | bytes 1572872 | tf_op jit(solution)/shard_map/ppermute | solution.py:141
  56.5 29.7 %collective-permute-start.4 = (bf16[512,512]{1,0:T(8,128)(2,1)S(1)}, bf16[512,512]{1,0:T(8,128)(2,1)S(1)}, u32[]{:S(2)}, u32[]{:S(2)}) collective-permute-start(bf16[512,512]{1,0:T(8,128)(2,1)S(1)} %get-tuple-element.22), channel_id=1, source_target_pairs={{8,0},{12,4},{16,8},{20,12},{24,16},{28,20},{32,24},{36,28},{40,32... | collective-permute-start | bytes 1572872 | tf_op jit(solution)/shard_map/ppermute | solution.py:141
  73.1 30.1 %collective-permute-start.5 = (bf16[256,512]{1,0:T(8,128)(2,1)S(1)}, bf16[256,512]{1,0:T(8,128)(2,1)S(1)}, u32[]{:S(2)}, u32[]{:S(2)}) collective-permute-start(bf16[256,512]{1,0:T(8,128)(2,1)S(1)} %slice.62), channel_id=1, source_target_pairs={{12,0},{16,4},{20,8},{24,12},{28,16},{32,20},{36,24},{40,28},{44,3... | collective-permute-start | bytes 786440 | tf_op jit(solution)/shard_map/ppermute | solution.py:141

commit v10 on v9

--- a/solution.py
+++ b/solution.py
@@ -148,11 +148,10 @@
     return counts.reshape(positions.shape)
 
 
-def local(query, key, value, attn_out, grad_out, log_norm, doc_bounds, local_pairs, ship_table):
+def local_body(query, key, value, attn_out, grad_out, log_norm, doc_bounds, local_pairs, ship_table):
     position = lax.axis_index("ctx")
-    tokens, features = query.shape
+    tokens, _ = query.shape
     kv_features = key.shape[1]
-    heads = log_norm.shape[0]
     own_blocks = tokens // BLOCK
     offsets = jnp.arange(BLOCK, dtype=jnp.int32)
     own_keyval = jnp.concatenate([key, value], axis=1)
@@ -175,9 +174,9 @@
         pieces, key_pos, doc_bounds,
     )
     segments = far_low.reshape(REACH, own_blocks * BLOCK, 2 * kv_features)
+    far_grads = shifted(segments[0][first_used:], "ctx", -REACH)
     for hop in range(1, REACH):
         own_grads = own_grads + shifted(segments[REACH - hop], "ctx", -hop)
-    far_grads = shifted(segments[0][first_used:], "ctx", -REACH)
     own_grads = own_grads.at[first_used:].add(far_grads.astype(jnp.float32))
     grad_key = own_grads[:, :kv_features].astype(jnp.bfloat16)
     grad_value = own_grads[:, kv_features:].astype(jnp.bfloat16)
@@ -197,4 +196,4 @@
         P(),
     )
     out_specs = (P("ctx", "head"), P("ctx", "head"), P("ctx", "head"))
-    return jax.shard_map(local, mesh=mesh, in_specs=in_specs, out_specs=out_specs, check_vma=False)
+    return jax.shard_map(local_body, mesh=mesh, in_specs=in_specs, out_specs=out_specs, check_vma=False)

time: 106 us -> 105 us (level)
  waiting for transfers between devices: 37.9 us -> 44.5 us
  starting transfers between devices: 33.3 us -> 26.7 us
    ppermute x6, waiting for transfers between devices: 37.9 us -> 44.5 us  [shifted(): return lax.ppermute(shard, axis, pairs)]
    ppermute x6, starting transfers between devices: 33.3 us -> 26.7 us  [shifted(): return lax.ppermute(shard, axis, pairs)]
where the time goes in v10:
time: 105 us; the launch traced here: 104 us
  waiting for transfers between devices  44.5 us (42%)
  starting transfers between devices  26.7 us (25%)
  Pallas kernels  23.2 us (22%)
  local copies, waits for them, and re-layouts  7.54 us (7%)
  other arithmetic  1.6 us (2%)
    ppermute x6, waiting for transfers between devices, shifted(): return lax.ppermute(shard, axis, pairs)  44.5 us
    ppermute x6, starting transfers between devices, shifted(): return lax.ppermute(shard, axis, pairs)  26.7 us
    pallas_call x1, Pallas kernels, run_pairs(): pl.pallas_call(kernel, out_shape=(jax.ShapeDtypeStruct((tokens, features)...  23.2 us
  transfers between devices with their start and end apart: 6, of which 4 were waited for; matrix products, arithmetic and copies ran while one was open for 5% of the time, Pallas kernels for 0%

profile of v10, /device:TPU:117, one launch (start us, length us, event | category | flops | bytes accessed | tf_op | source)
XLA Modules:
  0.0 104.3 jit_solution(14242684763345806041)
XLA Ops:
  0.6 1.0 constant_dynamic-update-slice_fusion.1
  1.6 1.0 constant_dynamic-update-slice_fusion.refs_3_
  2.6 3.5 %collective-permute-start.2 = (bf16[512,512]{1,0:T(8,128)(2,1)S(1)}, bf16[512,512]{1,0:T(8,128)(2,1)S(1)}, u32[]{:S(2)}, u32[]{:S(2)}) collective-permute-start(bf16[512,512]{1,0:T(8,128)(2,1)S(1)} %constant_dynamic-update-slice_fusion.refs_3_), channel_id=1, source_target_pairs={{0,4},{4,8},{8,12},{12,16},{16,20},{20,24},{24,28},{28,32},{32,36}... | collective-permute-start | bytes 1572872 | tf_op jit(solution)/shard_map/ppermute | solution.py:141
  6.1 4.4 %collective-permute-start.1 = (bf16[512,512]{1,0:T(8,128)(2,1)S(1)}, bf16[512,512]{1,0:T(8,128)(2,1)S(1)}, u32[]{:S(2)}, u32[]{:S(2)}) collective-permute-start(bf16[512,512]{1,0:T(8,128)(2,1)S(1)} %constant_dynamic-update-slice_fusion.refs_3_), channel_id=1, source_target_pairs={{0,8},{4,12},{8,16},{12,20},{16,24},{20,28},{24,32},{28,36},{32,40... | collective-permute-start | bytes 1572872 | tf_op jit(solution)/shard_map/ppermute | solution.py:141
  10.5 2.6 %collective-permute-start = (bf16[256,512]{1,0:T(8,128)(2,1)S(1)}, bf16[256,512]{1,0:T(8,128)(2,1)S(1)}, u32[]{:S(2)}, u32[]{:S(2)}) collective-permute-start(bf16[256,512]{1,0:T(8,128)(2,1)S(1)} %slice.65), channel_id=1, source_target_pairs={{0,12},{4,16},{8,20},{12,24},{16,28},{20,32},{24,36},{28,40},{32,4... | collective-permute-start | bytes 786440 | tf_op jit(solution)/shard_map/ppermute | solution.py:141
  13.2 0.7 slice.57
  14.0 0.8 constant_dynamic-slice_fusion
  14.7 0.1 copy.19
  14.8 0.1 slice_reduce_fusion
  14.9 0.1 compare_select_fusion
  15.0 0.1 convert_reduce_fusion.1
  15.1 0.1 stack.9
  15.2 0.1 stack.10
  15.3 0.1 convert_reduce_fusion
  15.4 0.8 add_add_fusion
  16.2 0.1 copy.20
  16.3 0.1 reshape.90.pairs_ref
  16.5 0.4 copy.22.kdoc_ref
  16.8 0.1 iota_add_fusion.kpos_ref
  16.9 9.9 %collective-permute-done.refs_0_ = bf16[256,512]{1,0:T(8,128)(2,1)S(1)} collective-permute-done((bf16[256,512]{1,0:T(8,128)(2,1)S(1)}, bf16[256,512]{1,0:T(8,128)(2,1)S(1)}, u32[]{:S(2)}, u32[]{:S(2)}) %collective-permute-start) | collective-permute-done | bytes 262176 | tf_op jit(solution)/shard_map/ppermute | solution.py:141
  26.8 3.3 %collective-permute-done.1.refs_1_ = bf16[512,512]{1,0:T(8,128)(2,1)S(1)} collective-permute-done((bf16[512,512]{1,0:T(8,128)(2,1)S(1)}, bf16[512,512]{1,0:T(8,128)(2,1)S(1)}, u32[]{:S(2)}, u32[]{:S(2)}) %collective-permute-start.1) | collective-permute-done | bytes 524320 | tf_op jit(solution)/shard_map/ppermute | solution.py:141
  30.2 23.2 %shard_map.112 = (bf16[512,2048]{1,0:T(8,128)(2,1)}, bf16[1536,512]{1,0:T(8,128)(2,1)}, f32[512,512]{1,0:T(8,128)S(1)}) custom-call(s32[120]{0:T(128)S(1)} %reshape.90.pairs_ref, bf16[512,2048]{1,0:T(8,128)(2,1)} %q_ref.1, bf16[512,2048]{1,0:T(8,128)(2,1)} %do_ref.1, bf16[512,2048]{1,0:T(8,128)(2,1)} %o_ref.1, f32[4,2048]{1,0:T(4,128)S(1)} %bitcast.16, ...), custom_call_target="tpu_custom_call" | custom-call | tf_op jit(solution)/shard_map/pallas_call | solution.py:115
  53.3 1.3 %fusion.2 = (bf16[512,512]{1,0:T(8,128)(2,1)S(1)}, bf16[512,512]{1,0:T(8,128)(2,1)S(1)}) fusion(bf16[1536,512]{1,0:T(8,128)(2,1)} %get-tuple-element.20), kind=kLoop, calls=%fused_computation.18 | loop fusion | bytes 2097152 | tf_op jit(solution)/shard_map/slice | solution.py:179
  54.6 1.9 %collective-permute-start.3 = (bf16[512,512]{1,0:T(8,128)(2,1)S(1)}, bf16[512,512]{1,0:T(8,128)(2,1)S(1)}, u32[]{:S(2)}, u32[]{:S(2)}) collective-permute-start(bf16[512,512]{1,0:T(8,128)(2,1)S(1)} %get-tuple-element.21), channel_id=1, source_target_pairs={{4,0},{8,4},{12,8},{16,12},{20,16},{24,20},{28,24},{32,28},{36,32}... | collective-permute-start | bytes 1572872 | tf_op jit(solution)/shard_map/ppermute | solution.py:141
  56.5 10.7 %collective-permute-start.4 = (bf16[512,512]{1,0:T(8,128)(2,1)S(1)}, bf16[512,512]{1,0:T(8,128)(2,1)S(1)}, u32[]{:S(2)}, u32[]{:S(2)}) collective-permute-start(bf16[512,512]{1,0:T(8,128)(2,1)S(1)} %get-tuple-element.22), channel_id=1, source_target_pairs={{8,0},{12,4},{16,8},{20,12},{24,16},{28,20},{32,24},{36,28},{40,32... | collective-permute-start | bytes 1572872 | tf_op jit(solution)/shard_map/ppermute | solution.py:141
  67.2 1.0 slice.62
  68.2 3.6 %collective-permute-start.5 = (bf16[256,512]{1,0:T(8,128)(2,1)S(1)}, bf16[256,512]{1,0:T(8,128)(2,1)S(1)}, u32[]{:S(2)}, u32[]{:S(2)}) collective-permute-start(bf16[256,512]{1,0:T(8,128)(2,1)S(1)} %slice.62), channel_id=1, source_target_pairs={{12,0},{16,4},{20,8},{24,12},{28,16},{32,20},{36,24},{40,28},{44,3... | collective-permute-start | bytes 786440 | tf_op jit(solution)/shard_map/ppermute | solution.py:141
  71.8 6.8 %collective-permute-done.4 = bf16[512,512]{1,0:T(8,128)(2,1)S(1)} collective-permute-done((bf16[512,512]{1,0:T(8,128)(2,1)S(1)}, bf16[512,512]{1,0:T(8,128)(2,1)S(1)}, u32[]{:S(2)}, u32[]{:S(2)}) %collective-permute-start.4) | collective-permute-done | bytes 524320 | tf_op jit(solution)/shard_map/ppermute | solution.py:141
  78.6 0.2 convert_add_fusion
  78.9 24.4 %collective-permute-done.5 = bf16[256,512]{1,0:T(8,128)(2,1)S(1)} collective-permute-done((bf16[256,512]{1,0:T(8,128)(2,1)S(1)}, bf16[256,512]{1,0:T(8,128)(2,1)S(1)}, u32[]{:S(2)}, u32[]{:S(2)}) %collective-permute-start.5) | collective-permute-done | bytes 262176 | tf_op jit(solution)/shard_map/ppermute | solution.py:141
  103.3 0.1 fusion
  103.5 0.8 fusion.3
  (11 shorter events, 0.2 us)
Async XLA Ops:
  0.6 14.4 %copy-start = (f32[16,512]{1,0:T(8,128)S(1)}, f32[16,512]{1,0:T(8,128)}, u32[]{:S(2)}) copy-start(f32[16,512]{1,0:T(8,128)} %param.16) | copy-start | bytes 98308
  2.6 24.2 %collective-permute-start.2 = (bf16[512,512]{1,0:T(8,128)(2,1)S(1)}, bf16[512,512]{1,0:T(8,128)(2,1)S(1)}, u32[]{:S(2)}, u32[]{:S(2)}) collective-permute-start(bf16[512,512]{1,0:T(8,128)(2,1)S(1)} %constant_dynamic-update-slice_fusion.refs_3_), channel_id=1, source_target_pairs={{0,4},{4,8},{8,12},{12,16},{16,20},{20,24},{24,28},{28,32},{32,36}... | collective-permute-start | bytes 1572872 | tf_op jit(solution)/shard_map/ppermute | solution.py:141
  6.1 24.1 %collective-permute-start.1 = (bf16[512,512]{1,0:T(8,128)(2,1)S(1)}, bf16[512,512]{1,0:T(8,128)(2,1)S(1)}, u32[]{:S(2)}, u32[]{:S(2)}) collective-permute-start(bf16[512,512]{1,0:T(8,128)(2,1)S(1)} %constant_dynamic-update-slice_fusion.refs_3_), channel_id=1, source_target_pairs={{0,8},{4,12},{8,16},{12,20},{16,24},{20,28},{24,32},{28,36},{32,40... | collective-permute-start | bytes 1572872 | tf_op jit(solution)/shard_map/ppermute | solution.py:141
  10.5 16.3 %collective-permute-start = (bf16[256,512]{1,0:T(8,128)(2,1)S(1)}, bf16[256,512]{1,0:T(8,128)(2,1)S(1)}, u32[]{:S(2)}, u32[]{:S(2)}) collective-permute-start(bf16[256,512]{1,0:T(8,128)(2,1)S(1)} %slice.65), channel_id=1, source_target_pairs={{0,12},{4,16},{8,20},{12,24},{16,28},{20,32},{24,36},{28,40},{32,4... | collective-permute-start | bytes 786440 | tf_op jit(solution)/shard_map/ppermute | solution.py:141
  54.6 17.2 %collective-permute-start.3 = (bf16[512,512]{1,0:T(8,128)(2,1)S(1)}, bf16[512,512]{1,0:T(8,128)(2,1)S(1)}, u32[]{:S(2)}, u32[]{:S(2)}) collective-permute-start(bf16[512,512]{1,0:T(8,128)(2,1)S(1)} %get-tuple-element.21), channel_id=1, source_target_pairs={{4,0},{8,4},{12,8},{16,12},{20,16},{24,20},{28,24},{32,28},{36,32}... | collective-permute-start | bytes 1572872 | tf_op jit(solution)/shard_map/ppermute | solution.py:141
  56.5 22.1 %collective-permute-start.4 = (bf16[512,512]{1,0:T(8,128)(2,1)S(1)}, bf16[512,512]{1,0:T(8,128)(2,1)S(1)}, u32[]{:S(2)}, u32[]{:S(2)}) collective-permute-start(bf16[512,512]{1,0:T(8,128)(2,1)S(1)} %get-tuple-element.22), channel_id=1, source_target_pairs={{8,0},{12,4},{16,8},{20,12},{24,16},{28,20},{32,24},{36,28},{40,32... | collective-permute-start | bytes 1572872 | tf_op jit(solution)/shard_map/ppermute | solution.py:141
  68.2 35.1 %collective-permute-start.5 = (bf16[256,512]{1,0:T(8,128)(2,1)S(1)}, bf16[256,512]{1,0:T(8,128)(2,1)S(1)}, u32[]{:S(2)}, u32[]{:S(2)}) collective-permute-start(bf16[256,512]{1,0:T(8,128)(2,1)S(1)} %slice.62), channel_id=1, source_target_pairs={{12,0},{16,4},{20,8},{24,12},{28,16},{32,20},{36,24},{40,28},{44,3... | collective-permute-start | bytes 786440 | tf_op jit(solution)/shard_map/ppermute | solution.py:141

commit v11 on v9

--- a/solution.py
+++ b/solution.py
@@ -16,7 +16,7 @@
 def pair_kernel(piece_starts, pairs_ref, q_ref, do_ref, o_ref, norm_ref, qdoc_ref, qpos_ref,
                 kdoc_ref, kpos_ref, *refs):
     piece_refs = refs[:len(piece_starts)]
-    dq_out, far_out, own_out, delta_ref, dq_ref, dkv_ref = refs[len(piece_starts):]
+    dq_out, tail_out, far_out, own_out, delta_ref, dq_ref, dkv_ref = refs[len(piece_starts):]
     dq_ref[...] = jnp.zeros(dq_ref.shape, jnp.float32)
     dkv_ref[...] = jnp.zeros(dkv_ref.shape, jnp.float32)
     heads = norm_ref.shape[1] // BLOCK
@@ -87,9 +87,12 @@
         return carry
 
     lax.fori_loop(0, dq_ref.shape[0] // BLOCK, finish_query, 0)
+    near_start = piece_starts[1] * BLOCK
+    tail_start = piece_starts[0] * BLOCK
+    tail_out[...] = dkv_ref[pl.ds(tail_start, near_start - tail_start), :].astype(tail_out.dtype)
     far_rows = far_out.shape[0]
-    far_out[...] = dkv_ref[pl.ds(0, far_rows), :].astype(far_out.dtype)
-    own_out[...] = dkv_ref[pl.ds(far_rows, own_out.shape[0]), :]
+    far_out[...] = dkv_ref[pl.ds(near_start, far_rows), :].astype(far_out.dtype)
+    own_out[...] = dkv_ref[pl.ds(near_start + far_rows, own_out.shape[0]), :]
 
 
 def run_pairs(pairs, queries, outgrads, outputs, norms, query_pos, pieces, key_pos, doc_bounds):
@@ -116,11 +119,12 @@
         kernel,
         out_shape=(
             jax.ShapeDtypeStruct((tokens, features), jnp.bfloat16),
-            jax.ShapeDtypeStruct((window - own_rows, both), jnp.bfloat16),
+            jax.ShapeDtypeStruct(((pieces[1][0] - pieces[0][0]) * BLOCK, both), jnp.bfloat16),
+            jax.ShapeDtypeStruct((window - own_rows - pieces[1][0] * BLOCK, both), jnp.bfloat16),
             jax.ShapeDtypeStruct((own_rows, both), jnp.float32),
         ),
         in_specs=specs,
-        out_specs=tuple(pl.BlockSpec(memory_space=vmem) for _ in range(3)),
+        out_specs=tuple(pl.BlockSpec(memory_space=vmem) for _ in range(4)),
         scratch_shapes=[
             pltpu.VMEM((blocks, 1, heads * BLOCK), jnp.float32),
             pltpu.VMEM((tokens, features), jnp.float32),
@@ -170,14 +174,14 @@
     ship_queries = jnp.where(ship_keys >= 0, own_ship[:, :1], -1)
     ship_pairs = jnp.stack([ship_queries, ship_keys], axis=2).reshape(-1, 2)
     pairs = jnp.concatenate([local_pairs, ship_pairs], axis=0)
-    grad_query, far_low, own_grads = run_pairs(
+    grad_query, tail_low, far_low, own_grads = run_pairs(
         pairs, query, grad_out, attn_out, log_norm, query_pos,
         pieces, key_pos, doc_bounds,
     )
-    segments = far_low.reshape(REACH, own_blocks * BLOCK, 2 * kv_features)
+    segments = far_low.reshape(REACH - 1, own_blocks * BLOCK, 2 * kv_features)
     for hop in range(1, REACH):
-        own_grads = own_grads + shifted(segments[REACH - hop], "ctx", -hop)
-    far_grads = shifted(segments[0][first_used:], "ctx", -REACH)
+        own_grads = own_grads + shifted(segments[REACH - 1 - hop], "ctx", -hop)
+    far_grads = shifted(tail_low, "ctx", -REACH)
     own_grads = own_grads.at[first_used:].add(far_grads.astype(jnp.float32))
     grad_key = own_grads[:, :kv_features].astype(jnp.bfloat16)
     grad_value = own_grads[:, kv_features:].astype(jnp.bfloat16)

time: 106 us -> 103 us (0.972)
  the two profiles are of different devices: /device:TPU:117 before, /device:TPU:115 now
where the time goes in v11:
time: 103 us
  waiting for transfers between devices  44.5 us (43%)
  Pallas kernels  26.9 us (26%)
  starting transfers between devices  22.7 us (22%)
  local copies, waits for them, and re-layouts  5.37 us (5%)
  other arithmetic  2.57 us (2%)
    ppermute x6, waiting for transfers between devices, shifted(): return lax.ppermute(shard, axis, pairs)  44.5 us
    pallas_call x1, Pallas kernels, run_pairs(): pl.pallas_call(kernel, out_shape=(jax.ShapeDtypeStruct((tokens, features)...  26.9 us
    ppermute x6, starting transfers between devices, shifted(): return lax.ppermute(shard, axis, pairs)  22.7 us
  transfers between devices with their start and end apart: 6, of which 4 were waited for; matrix products, arithmetic and copies ran while one was open for 5% of the time, Pallas kernels for 0%

profile of v11, /device:TPU:115, one launch (start us, length us, event | category | flops | bytes accessed | tf_op | source)
XLA Modules:
  0.0 102.8 jit_solution(9789994514075684907)
XLA Ops:
  0.6 1.0 constant_dynamic-update-slice_fusion.1
  1.6 1.0 constant_dynamic-update-slice_fusion.refs_3_
  2.6 3.5 %collective-permute-start.2 = (bf16[512,512]{1,0:T(8,128)(2,1)S(1)}, bf16[512,512]{1,0:T(8,128)(2,1)S(1)}, u32[]{:S(2)}, u32[]{:S(2)}) collective-permute-start(bf16[512,512]{1,0:T(8,128)(2,1)S(1)} %constant_dynamic-update-slice_fusion.refs_3_), channel_id=1, source_target_pairs={{0,4},{4,8},{8,12},{12,16},{16,20},{20,24},{24,28},{28,32},{32,36}... | collective-permute-start | bytes 1572872 | tf_op jit(solution)/shard_map/ppermute | solution.py:145
  6.1 4.4 %collective-permute-start.1 = (bf16[512,512]{1,0:T(8,128)(2,1)S(1)}, bf16[512,512]{1,0:T(8,128)(2,1)S(1)}, u32[]{:S(2)}, u32[]{:S(2)}) collective-permute-start(bf16[512,512]{1,0:T(8,128)(2,1)S(1)} %constant_dynamic-update-slice_fusion.refs_3_), channel_id=1, source_target_pairs={{0,8},{4,12},{8,16},{12,20},{16,24},{20,28},{24,32},{28,36},{32,40... | collective-permute-start | bytes 1572872 | tf_op jit(solution)/shard_map/ppermute | solution.py:145
  10.5 2.6 %collective-permute-start = (bf16[256,512]{1,0:T(8,128)(2,1)S(1)}, bf16[256,512]{1,0:T(8,128)(2,1)S(1)}, u32[]{:S(2)}, u32[]{:S(2)}) collective-permute-start(bf16[256,512]{1,0:T(8,128)(2,1)S(1)} %slice.57), channel_id=1, source_target_pairs={{0,12},{4,16},{8,20},{12,24},{16,28},{20,32},{24,36},{28,40},{32,4... | collective-permute-start | bytes 786440 | tf_op jit(solution)/shard_map/ppermute | solution.py:145
  13.2 0.7 slice.50
  13.9 0.1 iota_add_fusion.2
  14.0 0.8 constant_dynamic-slice_fusion
  14.7 0.1 copy.19
  14.8 0.1 slice_reduce_fusion
  14.9 0.1 compare_select_fusion
  15.0 0.1 convert_reduce_fusion.1
  15.1 0.1 stack.9
  15.2 0.1 stack.10
  15.3 0.1 convert_reduce_fusion
  15.4 0.8 add_add_fusion
  16.2 0.1 copy.20
  16.3 0.1 reshape.87.pairs_ref
  16.5 0.4 copy.22.kdoc_ref
  16.8 1.0 %iota_add_fusion.kpos_ref = s32[2048,1]{1,0:T(8,128)} fusion(s32[]{:T(128)S(6)} %mul.16), kind=kLoop, calls=%fused_computation.1 | loop fusion | flops 2048 | bytes 8196 | tf_op jit(solution)/shard_map/add | solution.py:171
  17.9 8.9 %collective-permute-done.refs_0_ = bf16[256,512]{1,0:T(8,128)(2,1)S(1)} collective-permute-done((bf16[256,512]{1,0:T(8,128)(2,1)S(1)}, bf16[256,512]{1,0:T(8,128)(2,1)S(1)}, u32[]{:S(2)}, u32[]{:S(2)}) %collective-permute-start) | collective-permute-done | bytes 262176 | tf_op jit(solution)/shard_map/ppermute | solution.py:145
  26.8 3.3 %collective-permute-done.1.refs_1_ = bf16[512,512]{1,0:T(8,128)(2,1)S(1)} collective-permute-done((bf16[512,512]{1,0:T(8,128)(2,1)S(1)}, bf16[512,512]{1,0:T(8,128)(2,1)S(1)}, u32[]{:S(2)}, u32[]{:S(2)}) %collective-permute-start.1) | collective-permute-done | bytes 524320 | tf_op jit(solution)/shard_map/ppermute | solution.py:145
  30.2 26.9 %shard_map.112 = (bf16[512,2048]{1,0:T(8,128)(2,1)}, bf16[256,512]{1,0:T(8,128)(2,1)S(1)}, bf16[1024,512]{1,0:T(8,128)(2,1)S(1)}, f32[512,512]{1,0:T(8,128)S(1)}) custom-call(s32[120]{0:T(128)S(1)} %reshape.87.pairs_ref, bf16[512,2048]{1,0:T(8,128)(2,1)} %q_ref.1, bf16[512,2048]{1,0:T(8,128)(2,1)} %do_ref.1, bf16[512,2048]{1,0:T(8,128)(2,1)} %o_ref.1, ...), custom_call_target="tpu_custom_call" | custom-call | tf_op jit(solution)/shard_map/pallas_call | solution.py:118
  57.1 0.1 fusion.2
  57.1 1.9 %collective-permute-start.3 = (bf16[512,512]{1,0:T(8,128)(2,1)S(1)}, bf16[512,512]{1,0:T(8,128)(2,1)S(1)}, u32[]{:S(2)}, u32[]{:S(2)}) collective-permute-start(bf16[512,512]{1,0:T(8,128)(2,1)S(1)} %get-tuple-element.23), channel_id=1, source_target_pairs={{4,0},{8,4},{12,8},{16,12},{20,16},{24,20},{28,24},{32,28},{36,32}... | collective-permute-start | bytes 1572872 | tf_op jit(solution)/shard_map/ppermute | solution.py:145
  59.1 7.0 %collective-permute-start.4 = (bf16[512,512]{1,0:T(8,128)(2,1)S(1)}, bf16[512,512]{1,0:T(8,128)(2,1)S(1)}, u32[]{:S(2)}, u32[]{:S(2)}) collective-permute-start(bf16[512,512]{1,0:T(8,128)(2,1)S(1)} %get-tuple-element.24), channel_id=1, source_target_pairs={{8,0},{12,4},{16,8},{20,12},{24,16},{28,20},{32,24},{36,28},{40,32... | collective-permute-start | bytes 1572872 | tf_op jit(solution)/shard_map/ppermute | solution.py:145
  66.0 3.3 %collective-permute-start.5 = (bf16[256,512]{1,0:T(8,128)(2,1)S(1)}, bf16[256,512]{1,0:T(8,128)(2,1)S(1)}, u32[]{:S(2)}, u32[]{:S(2)}) collective-permute-start(bf16[256,512]{1,0:T(8,128)(2,1)S(1)} %get-tuple-element.22), channel_id=1, source_target_pairs={{12,0},{16,4},{20,8},{24,12},{28,16},{32,20},{36,24},{40,28},{44,3... | collective-permute-start | bytes 786440 | tf_op jit(solution)/shard_map/ppermute | solution.py:145
  69.4 8.4 %collective-permute-done.4 = bf16[512,512]{1,0:T(8,128)(2,1)S(1)} collective-permute-done((bf16[512,512]{1,0:T(8,128)(2,1)S(1)}, bf16[512,512]{1,0:T(8,128)(2,1)S(1)}, u32[]{:S(2)}, u32[]{:S(2)}) %collective-permute-start.4) | collective-permute-done | bytes 524320 | tf_op jit(solution)/shard_map/ppermute | solution.py:145
  77.8 0.2 convert_add_fusion
  78.0 23.8 %collective-permute-done.5 = bf16[256,512]{1,0:T(8,128)(2,1)S(1)} collective-permute-done((bf16[256,512]{1,0:T(8,128)(2,1)S(1)}, bf16[256,512]{1,0:T(8,128)(2,1)S(1)}, u32[]{:S(2)}, u32[]{:S(2)}) %collective-permute-start.5) | collective-permute-done | bytes 262176 | tf_op jit(solution)/shard_map/ppermute | solution.py:145
  101.8 0.1 fusion
  102.0 0.8 fusion.3
  (10 shorter events, 0.1 us)
Async XLA Ops:
  0.6 14.4 %copy-start = (f32[16,512]{1,0:T(8,128)S(1)}, f32[16,512]{1,0:T(8,128)}, u32[]{:S(2)}) copy-start(f32[16,512]{1,0:T(8,128)} %param.16) | copy-start | bytes 98308
  2.6 24.2 %collective-permute-start.2 = (bf16[512,512]{1,0:T(8,128)(2,1)S(1)}, bf16[512,512]{1,0:T(8,128)(2,1)S(1)}, u32[]{:S(2)}, u32[]{:S(2)}) collective-permute-start(bf16[512,512]{1,0:T(8,128)(2,1)S(1)} %constant_dynamic-update-slice_fusion.refs_3_), channel_id=1, source_target_pairs={{0,4},{4,8},{8,12},{12,16},{16,20},{20,24},{24,28},{28,32},{32,36}... | collective-permute-start | bytes 1572872 | tf_op jit(solution)/shard_map/ppermute | solution.py:145
  6.1 24.1 %collective-permute-start.1 = (bf16[512,512]{1,0:T(8,128)(2,1)S(1)}, bf16[512,512]{1,0:T(8,128)(2,1)S(1)}, u32[]{:S(2)}, u32[]{:S(2)}) collective-permute-start(bf16[512,512]{1,0:T(8,128)(2,1)S(1)} %constant_dynamic-update-slice_fusion.refs_3_), channel_id=1, source_target_pairs={{0,8},{4,12},{8,16},{12,20},{16,24},{20,28},{24,32},{28,36},{32,40... | collective-permute-start | bytes 1572872 | tf_op jit(solution)/shard_map/ppermute | solution.py:145
  10.5 16.3 %collective-permute-start = (bf16[256,512]{1,0:T(8,128)(2,1)S(1)}, bf16[256,512]{1,0:T(8,128)(2,1)S(1)}, u32[]{:S(2)}, u32[]{:S(2)}) collective-permute-start(bf16[256,512]{1,0:T(8,128)(2,1)S(1)} %slice.57), channel_id=1, source_target_pairs={{0,12},{4,16},{8,20},{12,24},{16,28},{20,32},{24,36},{28,40},{32,4... | collective-permute-start | bytes 786440 | tf_op jit(solution)/shard_map/ppermute | solution.py:145
  57.1 12.2 %collective-permute-start.3 = (bf16[512,512]{1,0:T(8,128)(2,1)S(1)}, bf16[512,512]{1,0:T(8,128)(2,1)S(1)}, u32[]{:S(2)}, u32[]{:S(2)}) collective-permute-start(bf16[512,512]{1,0:T(8,128)(2,1)S(1)} %get-tuple-element.23), channel_id=1, source_target_pairs={{4,0},{8,4},{12,8},{16,12},{20,16},{24,20},{28,24},{32,28},{36,32}... | collective-permute-start | bytes 1572872 | tf_op jit(solution)/shard_map/ppermute | solution.py:145
  59.1 18.7 %collective-permute-start.4 = (bf16[512,512]{1,0:T(8,128)(2,1)S(1)}, bf16[512,512]{1,0:T(8,128)(2,1)S(1)}, u32[]{:S(2)}, u32[]{:S(2)}) collective-permute-start(bf16[512,512]{1,0:T(8,128)(2,1)S(1)} %get-tuple-element.24), channel_id=1, source_target_pairs={{8,0},{12,4},{16,8},{20,12},{24,16},{28,20},{32,24},{36,28},{40,32... | collective-permute-start | bytes 1572872 | tf_op jit(solution)/shard_map/ppermute | solution.py:145
  66.0 35.7 %collective-permute-start.5 = (bf16[256,512]{1,0:T(8,128)(2,1)S(1)}, bf16[256,512]{1,0:T(8,128)(2,1)S(1)}, u32[]{:S(2)}, u32[]{:S(2)}) collective-permute-start(bf16[256,512]{1,0:T(8,128)(2,1)S(1)} %get-tuple-element.22), channel_id=1, source_target_pairs={{12,0},{16,4},{20,8},{24,12},{28,16},{32,20},{36,24},{40,28},{44,3... | collective-permute-start | bytes 786440 | tf_op jit(solution)/shard_map/ppermute | solution.py:145
